TPU v7x, 32 devices: a whole 2x2x4 slice. The times are simulated.
32 devices in a mesh: dp: 8 (over y, x, core), tensor: 4 (over z).
Axes of the slice: x: 2, y: 2, z: 4, core: 2. Of those that a mesh axis runs over, the one named last changes fastest.
Arguments:
- tokens: bfloat16 [8192, 2048], P(('dp', 'tensor')), may hold values from -6 to 6
- segments: int32 [8192], P('dp'), may hold values from 0 to 1023, as said below
- positions: int32 [8192], P('dp'), may hold values from 0 to 1023, as said below
- norm_attn: float32 [2048], replicated, may hold values from 0.25 to 1.75
- w_query: bfloat16 [2048, 2048], P('dp', 'tensor'), may hold values from -0.125 to 0.125
- w_key: bfloat16 [2048, 512], P('dp', 'tensor'), may hold values from -0.125 to 0.125
- w_value: bfloat16 [2048, 512], P('dp', 'tensor'), may hold values from -0.125 to 0.125
- w_out: bfloat16 [2048, 2048], P('tensor', 'dp'), may hold values from -0.375 to 0.375
- norm_mlp: float32 [2048], replicated, may hold values from 0.25 to 1.75
- w_gate: bfloat16 [2048, 8192], P('dp', 'tensor'), may hold values from -0.125 to 0.125
- w_up: bfloat16 [2048, 8192], P('dp', 'tensor'), may hold values from -0.125 to 0.125
- w_down: bfloat16 [8192, 2048], P('tensor', 'dp'), may hold values from -0.09375 to 0.09375
- cotangent: bfloat16 [8192, 2048], P(('dp', 'tensor')), may hold values from -6 to 6
Outputs:
- layer_out: bfloat16 [8192, 2048], P(('dp', 'tensor'))
- input_grad: float32 [8192, 2048], P(('dp', 'tensor'))
- grad_norm_attn: float32 [2048], replicated
- grad_query: float32 [2048, 2048], P('dp', 'tensor')
- grad_key: float32 [2048, 512], P('dp', 'tensor')
- grad_value: float32 [2048, 512], P('dp', 'tensor')
- grad_output: float32 [2048, 2048], P('tensor', 'dp')
- grad_norm_mlp: float32 [2048], replicated
- grad_gate: float32 [2048, 8192], P('dp', 'tensor')
- grad_up: float32 [2048, 8192], P('dp', 'tensor')
- grad_down: float32 [8192, 2048], P('tensor', 'dp')
Inputs may be any that keep to these rules, and one draw needn't show every extreme that they name: `segments`: within each sequence of 1024 tokens, a token's label is the place in that sequence of its document's first token, so labels never fall along a sequence; the first sequence of all is a single document, and the last token of the last sequence starts a document of its own. `positions`: each token's position counts from 0 at its document's first token.
All inputs are finite; a program needn't handle non-finite values.
Results may differ from a plain program's by a relative error of at most 0.022.
Values may be sent and summed in bfloat16 or wider, within the bound.
No kernel may reach another device: no remote copies, remote signals or barrier semaphores. Data moves between devices by JAX's collectives and lax.ppermute only.
A program may use at most 192 MiB of HBM per device.

v0:
```python
from functools import partial
import math

import jax
import jax.numpy as jnp
from jax import lax
from jax.sharding import PartitionSpec as P

QH = 32
KVH = 8
HD = 64
LEN = 1024


def rms_scale(values, norm_gain):
    inverse = lax.rsqrt(jnp.mean(values * values, axis=-1, keepdims=True) + 1e-05)
    return values * inverse * norm_gain


def rotary_tables(positions):
    freq_index = jnp.arange(HD // 2, dtype=jnp.int32).astype(jnp.float32)
    inverse = jnp.exp(freq_index * (-2.0 * math.log(500000.0) / HD))
    angles = positions.astype(jnp.float32)[:, None] * inverse[None, :]
    return (jnp.cos(angles), jnp.sin(angles))


def rotate(values, cosine_table, sine_table):
    half_width = values.shape[-1] // 2
    lower_half = values[..., :half_width]
    upper_half = values[..., half_width:]
    cosine_rows = cosine_table[:, None, :]
    sine_rows = sine_table[:, None, :]
    return jnp.concatenate(
        [
            lower_half * cosine_rows - upper_half * sine_rows,
            upper_half * cosine_rows + lower_half * sine_rows,
        ],
        axis=-1,
    )


def silu_product(gate_values, up_values):
    return jax.nn.silu(gate_values) * up_values


def local(
    tokens,
    segments,
    positions,
    norm_attn,
    w_query,
    w_key,
    w_value,
    w_out,
    norm_mlp,
    w_gate,
    w_up,
    w_down,
    cotangent,
):
    kv_local = w_key.shape[1] // HD
    per_group = QH // KVH
    block_rows = min(512, LEN)
    score_scale = 1.0 / math.sqrt(HD)
    inputs = tokens.astype(jnp.float32)
    normed_local = rms_scale(inputs, norm_attn).astype(jnp.bfloat16)
    normed_in = lax.all_gather(normed_local, "tensor", axis=0, tiled=True)
    query_all, key_all, value_all, out_all = (
        lax.all_gather(w_query, "dp", axis=0, tiled=True),
        lax.all_gather(w_key, "dp", axis=0, tiled=True),
        lax.all_gather(w_value, "dp", axis=0, tiled=True),
        lax.all_gather(w_out, "dp", axis=1, tiled=True),
    )
    group_rows = normed_in.shape[0]
    block_count = group_rows // block_rows
    cosine_table, sine_table = rotary_tables(positions)
    rotate_here = partial(rotate, cosine_table=cosine_table, sine_table=sine_table)
    query_raw = jnp.dot(normed_in, query_all, preferred_element_type=jnp.float32).reshape(
        group_rows, kv_local * per_group, HD
    )
    key_raw = jnp.dot(normed_in, key_all, preferred_element_type=jnp.float32).reshape(
        group_rows, kv_local, HD
    )
    all_queries = (
        rotate_here(query_raw).astype(jnp.bfloat16).reshape(group_rows, kv_local, per_group, HD)
    )
    all_keys = rotate_here(key_raw).astype(jnp.bfloat16)
    all_values = (
        jnp.dot(normed_in, value_all, preferred_element_type=jnp.float32)
        .astype(jnp.bfloat16)
        .reshape(group_rows, kv_local, HD)
    )
    place_index = jnp.arange(LEN, dtype=jnp.int32)

    def block_scores(block_index):
        row_start = block_index * block_rows
        seq_start = row_start // LEN * LEN
        query_rows = lax.dynamic_slice_in_dim(all_queries, row_start, block_rows, 0)
        query_segs = lax.dynamic_slice_in_dim(segments, row_start, block_rows, 0)
        query_place = row_start - seq_start + jnp.arange(block_rows, dtype=jnp.int32)
        allowed = (place_index[None, :] <= query_place[:, None]) & (
            segments[None, :] == query_segs[:, None]
        )
        scores = (
            jnp.einsum("qhgd,khd->hgqk", query_rows, all_keys, preferred_element_type=jnp.float32)
            * score_scale
        )
        return (jnp.where(allowed, scores, -1e30), query_rows, all_keys, all_values, seq_start)

    def forward_block(block_index):
        scores, query_rows, near_keys, near_values, seq_start = block_scores(block_index)
        row_peak = jnp.max(scores, axis=-1, keepdims=True)
        row_total = jnp.sum(jnp.exp(scores - row_peak), axis=-1, keepdims=True)
        log_total = row_peak + jnp.log(row_total)
        attn_probs = jnp.exp(scores - log_total).astype(jnp.bfloat16)
        context_block = jnp.einsum(
            "hgqk,khd->qhgd", attn_probs, near_values, preferred_element_type=jnp.float32
        )
        return (context_block.reshape(block_rows, -1).astype(jnp.bfloat16), log_total)

    context, log_totals = lax.map(forward_block, jnp.arange(block_count, dtype=jnp.int32))
    context = context.reshape(group_rows, -1)
    attn_branch = lax.psum_scatter(
        jnp.dot(context, out_all, preferred_element_type=jnp.float32).astype(jnp.bfloat16),
        "tensor",
        scatter_dimension=0,
        tiled=True,
    ).astype(jnp.float32)
    middle = inputs + attn_branch
    normed_mid_local = rms_scale(middle, norm_mlp).astype(jnp.bfloat16)
    normed_mid = lax.all_gather(normed_mid_local, "tensor", axis=0, tiled=True)
    gate_all, up_all, down_all = (
        lax.all_gather(w_gate, "dp", axis=0, tiled=True),
        lax.all_gather(w_up, "dp", axis=0, tiled=True),
        lax.all_gather(w_down, "dp", axis=1, tiled=True),
    )
    gate_values = jnp.dot(normed_mid, gate_all, preferred_element_type=jnp.float32)
    up_values = jnp.dot(normed_mid, up_all, preferred_element_type=jnp.float32)
    hidden = silu_product(gate_values, up_values).astype(jnp.bfloat16)
    mlp_branch = lax.psum_scatter(
        jnp.dot(hidden, down_all, preferred_element_type=jnp.float32).astype(jnp.bfloat16),
        "tensor",
        scatter_dimension=0,
        tiled=True,
    ).astype(jnp.float32)
    layer_out = (middle + mlp_branch).astype(jnp.bfloat16)
    cot_all = lax.all_gather(cotangent, "tensor", axis=0, tiled=True)
    d_hidden = jnp.einsum("rd,fd->rf", cot_all, down_all, preferred_element_type=jnp.float32)
    silu_back = jax.vjp(silu_product, gate_values, up_values)[1]
    d_gate32, d_up32 = silu_back(d_hidden)
    d_gate = d_gate32.astype(jnp.bfloat16)
    d_up = d_up32.astype(jnp.bfloat16)
    gate_part = jnp.einsum("rd,rf->df", normed_mid, d_gate, preferred_element_type=jnp.float32)
    up_part = jnp.einsum("rd,rf->df", normed_mid, d_up, preferred_element_type=jnp.float32)
    down_part = jnp.einsum("rf,rd->fd", hidden, cot_all, preferred_element_type=jnp.float32)
    d_normed_mid = lax.psum_scatter(
        (
            jnp.einsum("rf,df->rd", d_gate, gate_all, preferred_element_type=jnp.float32)
            + jnp.einsum("rf,df->rd", d_up, up_all, preferred_element_type=jnp.float32)
        ).astype(jnp.bfloat16),
        "tensor",
        scatter_dimension=0,
        tiled=True,
    ).astype(jnp.float32)
    mid_back = jax.vjp(rms_scale, middle, norm_mlp)[1]
    d_middle_norm, mlp_gain_part = mid_back(d_normed_mid)
    d_middle = cotangent.astype(jnp.float32) + d_middle_norm
    d_branch = lax.all_gather(d_middle.astype(jnp.bfloat16), "tensor", axis=0, tiled=True)
    out_part = jnp.einsum("rc,rd->cd", context, d_branch, preferred_element_type=jnp.float32)
    d_context = jnp.einsum(
        "rd,cd->rc", d_branch, out_all, preferred_element_type=jnp.float32
    ).astype(jnp.bfloat16)
    d_context = d_context.reshape(group_rows, kv_local, per_group, HD)

    def backward_block(grad_carry, block_index):
        key_grads, value_grads = grad_carry
        scores, query_rows, near_keys, near_values, seq_start = block_scores(block_index)
        probs_full = jnp.exp(scores - log_totals[block_index])
        attn_probs = probs_full.astype(jnp.bfloat16)
        d_rows = lax.dynamic_slice_in_dim(d_context, block_index * block_rows, block_rows, 0)
        d_probs = jnp.einsum(
            "qhgd,khd->hgqk", d_rows, near_values, preferred_element_type=jnp.float32
        )
        d_scores = (
            probs_full * (d_probs - jnp.sum(probs_full * d_probs, axis=-1, keepdims=True))
        ).astype(jnp.bfloat16)
        d_queries = (
            jnp.einsum("hgqk,khd->qhgd", d_scores, near_keys, preferred_element_type=jnp.float32)
            * score_scale
        )
        d_keys = (
            jnp.einsum("hgqk,qhgd->khd", d_scores, query_rows, preferred_element_type=jnp.float32)
            * score_scale
        )
        d_values = jnp.einsum(
            "hgqk,qhgd->khd", attn_probs, d_rows, preferred_element_type=jnp.float32
        )
        old_keys = key_grads
        key_grads = old_keys + d_keys
        old_values = value_grads
        value_grads = old_values + d_values
        return ((key_grads, value_grads), d_queries)

    empty_grads = jnp.zeros((group_rows, kv_local, HD), jnp.float32)
    kv_grads, query_grads = lax.scan(
        backward_block, (empty_grads, empty_grads), jnp.arange(block_count, dtype=jnp.int32)
    )
    query_grads = query_grads.reshape(group_rows, kv_local * per_group, HD)
    query_back = jax.vjp(rotate_here, query_raw)[1]
    key_back = jax.vjp(rotate_here, key_raw)[1]
    d_query_raw = query_back(query_grads)[0].astype(jnp.bfloat16).reshape(group_rows, -1)
    d_key_raw = key_back(kv_grads[0])[0].astype(jnp.bfloat16).reshape(group_rows, -1)
    d_value_raw = kv_grads[1].astype(jnp.bfloat16).reshape(group_rows, -1)
    query_part = jnp.einsum("rd,rc->dc", normed_in, d_query_raw, preferred_element_type=jnp.float32)
    key_part = jnp.einsum("rd,rc->dc", normed_in, d_key_raw, preferred_element_type=jnp.float32)
    value_part = jnp.einsum("rd,rc->dc", normed_in, d_value_raw, preferred_element_type=jnp.float32)
    query_rows = d_query_raw
    d_normed_in = lax.psum_scatter(
        (
            jnp.einsum("rc,dc->rd", query_rows, query_all, preferred_element_type=jnp.float32)
            + jnp.einsum("rc,dc->rd", d_key_raw, key_all, preferred_element_type=jnp.float32)
            + jnp.einsum("rc,dc->rd", d_value_raw, value_all, preferred_element_type=jnp.float32)
        ).astype(jnp.bfloat16),
        "tensor",
        scatter_dimension=0,
        tiled=True,
    ).astype(jnp.float32)
    in_back = jax.vjp(rms_scale, inputs, norm_attn)[1]
    d_input_norm, attn_gain_part = in_back(d_normed_in)
    input_grad = d_middle + d_input_norm
    grad_norm_attn, grad_norm_mlp = lax.psum((attn_gain_part, mlp_gain_part), ("dp", "tensor"))
    grad_query, grad_key, grad_value, grad_output, grad_gate, grad_up, grad_down = (
        lax.psum_scatter(
            query_part.astype(jnp.bfloat16), "dp", scatter_dimension=0, tiled=True
        ).astype(jnp.float32),
        lax.psum_scatter(
            key_part.astype(jnp.bfloat16), "dp", scatter_dimension=0, tiled=True
        ).astype(jnp.float32),
        lax.psum_scatter(
            value_part.astype(jnp.bfloat16), "dp", scatter_dimension=0, tiled=True
        ).astype(jnp.float32),
        lax.psum_scatter(
            out_part.astype(jnp.bfloat16), "dp", scatter_dimension=1, tiled=True
        ).astype(jnp.float32),
        lax.psum_scatter(
            gate_part.astype(jnp.bfloat16), "dp", scatter_dimension=0, tiled=True
        ).astype(jnp.float32),
        lax.psum_scatter(
            up_part.astype(jnp.bfloat16), "dp", scatter_dimension=0, tiled=True
        ).astype(jnp.float32),
        lax.psum_scatter(
            down_part.astype(jnp.bfloat16), "dp", scatter_dimension=1, tiled=True
        ).astype(jnp.float32),
    )
    return (
        layer_out,
        input_grad,
        grad_norm_attn,
        grad_query,
        grad_key,
        grad_value,
        grad_output,
        grad_norm_mlp,
        grad_gate,
        grad_up,
        grad_down,
    )


def solution(mesh):
    in_specs = (
        P(("dp", "tensor"), None),
        P("dp"),
        P("dp"),
        P(),
        P("dp", "tensor"),
        P("dp", "tensor"),
        P("dp", "tensor"),
        P("tensor", "dp"),
        P(),
        P("dp", "tensor"),
        P("dp", "tensor"),
        P("tensor", "dp"),
        P(("dp", "tensor"), None),
    )
    out_specs = (
        P(("dp", "tensor"), None),
        P(("dp", "tensor"), None),
        P(),
        P("dp", "tensor"),
        P("dp", "tensor"),
        P("dp", "tensor"),
        P("tensor", "dp"),
        P(),
        P("dp", "tensor"),
        P("dp", "tensor"),
        P("tensor", "dp"),
    )
    return jax.shard_map(local, mesh=mesh, in_specs=in_specs, out_specs=out_specs, check_vma=False)
```

profile of v0, /device:TPU:0, one launch (start us, length us, event | category | flops | bytes accessed | tf_op | source)
XLA Modules:
  0.0 1351.4 jit_solution(8502099795112230766)
XLA Ops:
  14.0 11.3 all_gather.35
  25.4 9.8 all_gather.36
  35.7 60.3 %all-gather.10.cloned.1.call-done = bf16[1024,2048]{1,0:T(8,128)(2,1)} async-done(((bf16[256,2048]{1,0:T(8,128)(2,1)}), bf16[1024,2048]{1,0:T(8,128)(2,1)}) %all-gather.10.cloned.1.call-update) | async-done | bytes 4194320 | tf_op jit(solution)/shard_map/all_gather | solution.py:67
  99.8 24.4 %all-gather.12.cloned.1.call-done = bf16[2048,512]{1,0:T(8,128)(2,1)} async-done(((bf16[256,512]{1,0:T(8,128)(2,1)}), bf16[2048,512]{1,0:T(8,128)(2,1)}) %all-gather.12.cloned.1.call-update) | async-done | bytes 2097168 | tf_op jit(solution)/shard_map/all_gather | solution.py:69
  124.2 5.2 fusion.75
  133.2 30.5 %while.32 = (s32[]{:T(128)}, bf16[2,512,512]{2,1,0:T(8,128)(2,1)}, f32[2,2,4,512,1]{3,2,1,4,0:T(4,128)}, s32[2]{0:T(128)S(1)}, s32[1024]{0:T(1024)S(1)}, /*index...) while((s32[]{:T(128)}, bf16[2,512,512]{2,1,0:T(8,128)(2,1)}, ...), condition=%wide.region_4.5_spmd.clone, body=%wide.region_1.4_spmd.clone.sunk | while | flops 1121710592 | bytes 56244616 | solution.py:121
  143.2 4.4 fusion.150
  163.7 6.9 convolution_convert_fusion.4
  171.3 76.3 %reduce-scatter.12.cloned.1.call-done = bf16[256,2048]{1,0:T(8,128)(2,1)} async-done(((bf16[1024,2048]{1,0:T(8,128)(2,1)}), bf16[256,2048]{1,0:T(8,128)(2,1)}) %reduce-scatter.12.cloned.1.call-update) | async-done | bytes 1048592 | tf_op jit(solution)/shard_map/reduce_scatter | solution.py:123
  254.2 50.0 %all-gather.20.cloned.1.call-done = bf16[2048,2048]{1,0:T(8,128)(2,1)} async-done(((bf16[256,2048]{1,0:T(8,128)(2,1)}), bf16[2048,2048]{1,0:T(8,128)(2,1)}) %all-gather.20.cloned.1.call-update) | async-done | bytes 8388624 | tf_op jit(solution)/shard_map/all_gather | solution.py:134
  304.1 82.8 %all-gather.16.cloned.1.call-done = bf16[1024,2048]{1,0:T(8,128)(2,1)} async-done(((bf16[256,2048]{1,0:T(8,128)(2,1)}), bf16[1024,2048]{1,0:T(8,128)(2,1)}) %all-gather.16.cloned.1.call-update) | async-done | bytes 4194320 | tf_op jit(solution)/shard_map/all_gather | solution.py:131
  386.9 14.9 %fusion.78 = f32[1024,2048]{1,0:T(8,128)} fusion(bf16[1024,2048]{1,0:T(8,128)(2,1)} %all-gather.16.cloned.1.call-done, bf16[2048,2048]{1,0:T(8,128)(2,1)} %all-gather.20.cloned.1.call-done), kind=kOutput, calls=%fused_computation.135 | convolution fusion | flops 8589934592 | bytes 20971520 | tf_op jit(solution)/shard_map/dot_general | solution.py:138
  401.8 39.8 %all-gather.18.cloned.1.call-done = bf16[2048,2048]{1,0:T(8,128)(2,1)} async-done(((bf16[256,2048]{1,0:T(8,128)(2,1)}), bf16[2048,2048]{1,0:T(8,128)(2,1)}) %all-gather.18.cloned.1.call-update) | async-done | bytes 8388624 | tf_op jit(solution)/shard_map/all_gather | solution.py:133
  441.6 14.4 %fusion.77 = f32[1024,2048]{1,0:T(8,128)} fusion(bf16[1024,2048]{1,0:T(8,128)(2,1)} %all-gather.16.cloned.1.call-done, bf16[2048,2048]{1,0:T(8,128)(2,1)} %all-gather.18.cloned.1.call-done), kind=kOutput, calls=%fused_computation.134 | convolution fusion | flops 8589934592 | bytes 20971520 | tf_op jit(solution)/shard_map/dot_general | solution.py:137
  455.9 67.9 %all-gather.24.cloned.1.call-done = bf16[1024,2048]{1,0:T(8,128)(2,1)} async-done(((bf16[256,2048]{1,0:T(8,128)(2,1)}), bf16[1024,2048]{1,0:T(8,128)(2,1)}) %all-gather.24.cloned.1.call-update) | async-done | bytes 4194320 | tf_op jit(solution)/shard_map/all_gather | solution.py:147
  523.9 56.3 %all-gather.22.cloned.1.call-done = bf16[2048,2048]{1,0:T(8,128)(2,1)} async-done(((bf16[2048,256]{1,0:T(8,128)(2,1)}), bf16[2048,2048]{1,0:T(8,128)(2,1)}) %all-gather.22.cloned.1.call-update) | async-done | bytes 8388624 | tf_op jit(solution)/shard_map/all_gather | solution.py:135
  580.2 21.8 %multiply_convert_fusion = (bf16[1024,2048]{1,0:T(8,128)(2,1)}, bf16[1024,2048]{1,0:T(8,128)(2,1)}, bf16[1024,2048]{1,0:T(8,128)(2,1)}) fusion(f32[1024,2048]{1,0:T(8,128)} %fusion.77, f32[1024,2048]{1,0:T(8,128)} %fusion.78, bf16[1024,2048]{1,0:T(8,128)(2,1)} %all-gather.24.cloned.1.call-done, bf16[2048,2048]{1,0:T(8,128)(2,1)} %all-gather.22.cloned.1.call-done), kind=kOutput, calls=%fused_computation.69 | convolution fusion | flops 8623489024 | bytes 41943040 | tf_op jit(solution)/shard_map/rd,fd->rf/dot_general | solution.py:148
  602.0 12.9 fusion.79
  614.9 12.9 add_convert_fusion.1
  627.9 76.9 %reduce-scatter.16.cloned.1.call-done = bf16[256,2048]{1,0:T(8,128)(2,1)} async-done(((bf16[1024,2048]{1,0:T(8,128)(2,1)}), bf16[256,2048]{1,0:T(8,128)(2,1)}) %reduce-scatter.16.cloned.1.call-update) | async-done | bytes 1048592 | tf_op jit(solution)/shard_map/reduce_scatter | solution.py:156
  710.8 14.4 %convolution_convert_fusion.1 = bf16[2048,2048]{1,0:T(8,128)(2,1)} fusion(bf16[1024,2048]{1,0:T(8,128)(2,1)} %all-gather.16.cloned.1.call-done, bf16[1024,2048]{1,0:T(8,128)(2,1)} %get-tuple-element.389), kind=kOutput, calls=%fused_computation.74 | convolution fusion | flops 8594128896 | bytes 16777216 | tf_op jit(solution)/shard_map/rd,rf->df/dot_general | solution.py:154
  725.3 14.1 %convolution_convert_fusion.2 = bf16[2048,2048]{1,0:T(8,128)(2,1)} fusion(bf16[1024,2048]{1,0:T(8,128)(2,1)} %all-gather.16.cloned.1.call-done, bf16[1024,2048]{1,0:T(8,128)(2,1)} %get-tuple-element.390), kind=kOutput, calls=%fused_computation.75 | convolution fusion | flops 8594128896 | bytes 16777216 | tf_op jit(solution)/shard_map/rd,rf->df/dot_general | solution.py:153
  739.5 14.1 %convolution_convert_fusion = bf16[2048,2048]{1,0:T(8,128)(2,1)} fusion(bf16[1024,2048]{1,0:T(8,128)(2,1)} %get-tuple-element.391, bf16[1024,2048]{1,0:T(8,128)(2,1)} %all-gather.24.cloned.1.call-done), kind=kOutput, calls=%fused_computation.73 | convolution fusion | flops 8594128896 | bytes 16777216 | tf_op jit(solution)/shard_map/rf,rd->fd/dot_general | solution.py:155
  753.7 38.5 %all-gather.26.cloned.1.call-done = bf16[1024,2048]{1,0:T(8,128)(2,1)} async-done(((bf16[256,2048]{1,0:T(8,128)(2,1)}), bf16[1024,2048]{1,0:T(8,128)(2,1)}) %all-gather.26.cloned.1.call-update) | async-done | bytes 4194320 | tf_op jit(solution)/shard_map/all_gather | solution.py:168
  792.2 5.5 convolution_convert_fusion.9
  797.7 133.2 %while.33 = (s32[]{:T(128)}, f32[1024,2,64]{0,2,1:T(8,128)}, f32[1024,2,64]{0,2,1:T(8,128)}, f32[2,512,2,4,64]{1,0,4,3,2:T(2,128)}, s32[2]{0:T(128)S(1)}, /*inde...) while((s32[]{:T(128)}, f32[1024,2,64]{0,2,1:T(8,128)}, ...), condition=%wide.region_12.13_spmd.clone, body=%wide.region_10.12_spmd.clone.sunk | while | flops 2749755904 | bytes 184482448 | solution.py:205
  806.1 5.3 fusion.164
  811.4 11.0 fusion.161
  822.3 8.5 fusion.162
  836.6 6.1 fusion.165
  843.8 19.7 %dynamic_update_slice.31 = f32[2,512,2,4,64]{1,0,4,3,2:T(2,128)} dynamic-update-slice(f32[2,512,2,4,64]{1,0,4,3,2:T(2,128)} %get-tuple-element.599, f32[1,512,2,4,64]{1,0,4,3,2:T(1,128)S(1)} %copy.49, s32[]{:T(128)S(6)} %copy.66, s32[]{:T(128)} %constant.161.clone.1..sunk.1, s32[]{:T(128)} %constant.161.clone.1..sunk.1, s32[]{:T(128)} %constant.161.clone.1..sunk.1, s32[]{:T(128)} %constant.161.clone.1..sunk.1) | dynamic-update-slice | bytes 2097156 | tf_op jit(solution)/shard_map/while/body/jit(dynamic_update_index_in_dim)/dynamic_update_slice | solution.py:205
  871.5 6.3 fusion.164
  877.8 11.1 fusion.161
  889.0 9.0 fusion.162
  903.7 6.2 fusion.165
  911.0 19.7 %dynamic_update_slice.31 = f32[2,512,2,4,64]{1,0,4,3,2:T(2,128)} dynamic-update-slice(f32[2,512,2,4,64]{1,0,4,3,2:T(2,128)} %get-tuple-element.599, f32[1,512,2,4,64]{1,0,4,3,2:T(1,128)S(1)} %copy.49, s32[]{:T(128)S(6)} %copy.66, s32[]{:T(128)} %constant.161.clone.1..sunk.1, s32[]{:T(128)} %constant.161.clone.1..sunk.1, s32[]{:T(128)} %constant.161.clone.1..sunk.1, s32[]{:T(128)} %constant.161.clone.1..sunk.1) | dynamic-update-slice | bytes 2097156 | tf_op jit(solution)/shard_map/while/body/jit(dynamic_update_index_in_dim)/dynamic_update_slice | solution.py:205
  936.6 4.5 convolution_convert_fusion.8
  941.2 5.9 convolution_convert_fusion.5
  965.3 13.9 %convolution_convert_fusion.3 = bf16[1024,2048]{1,0:T(8,128)(2,1)} fusion(bf16[1024,2048]{1,0:T(8,128)(2,1)} %get-tuple-element.391, bf16[2048,2048]{1,0:T(8,128)(2,1)} %all-gather.22.cloned.1.call-done), kind=kOutput, calls=%fused_computation.81 | convolution fusion | flops 8592031744 | bytes 16777216 | tf_op jit(solution)/shard_map/dot_general | solution.py:141
  984.9 30.2 %reduce-scatter.32.cloned.1.call-done = bf16[2048,256]{1,0:T(8,128)(2,1)} async-done(((bf16[2048,2048]{1,0:T(8,128)(2,1)}), bf16[2048,256]{1,0:T(8,128)(2,1)}) %reduce-scatter.32.cloned.1.call-update) | async-done | bytes 1048592 | tf_op jit(solution)/shard_map/reduce_scatter | solution.py:251
  1017.9 35.0 %reduce-scatter.24.cloned.1.call-done = bf16[256,128]{1,0:T(8,128)(2,1)} async-done(((bf16[2048,128]{1,0:T(8,128)(2,1)}), bf16[256,128]{1,0:T(8,128)(2,1)}) %reduce-scatter.24.cloned.1.call-update) | async-done | bytes 65552 | tf_op jit(solution)/shard_map/reduce_scatter | solution.py:239
  1054.3 36.1 %reduce-scatter.22.cloned.1.call-done = bf16[256,128]{1,0:T(8,128)(2,1)} async-done(((bf16[2048,128]{1,0:T(8,128)(2,1)}), bf16[256,128]{1,0:T(8,128)(2,1)}) %reduce-scatter.22.cloned.1.call-update) | async-done | bytes 65552 | tf_op jit(solution)/shard_map/reduce_scatter | solution.py:236
  1092.0 42.8 %reduce-scatter.26.cloned.1.call-done = bf16[512,256]{1,0:T(8,128)(2,1)} async-done(((bf16[512,2048]{1,0:T(8,128)(2,1)}), bf16[512,256]{1,0:T(8,128)(2,1)}) %reduce-scatter.26.cloned.1.call-update) | async-done | bytes 262160 | tf_op jit(solution)/shard_map/reduce_scatter | solution.py:242
  1136.5 43.1 %reduce-scatter.20.cloned.1.call-done = bf16[256,512]{1,0:T(8,128)(2,1)} async-done(((bf16[2048,512]{1,0:T(8,128)(2,1)}), bf16[256,512]{1,0:T(8,128)(2,1)}) %reduce-scatter.20.cloned.1.call-update) | async-done | bytes 262160 | tf_op jit(solution)/shard_map/reduce_scatter | solution.py:233
  1181.4 77.3 %reduce-scatter.18.cloned.1.call-done = bf16[256,2048]{1,0:T(8,128)(2,1)} async-done(((bf16[1024,2048]{1,0:T(8,128)(2,1)}), bf16[256,2048]{1,0:T(8,128)(2,1)}) %reduce-scatter.18.cloned.1.call-update) | async-done | bytes 1048592 | tf_op jit(solution)/shard_map/reduce_scatter | solution.py:218
  1261.0 45.8 %all-reduce.4 = (f32[2048]{0:T(1024)}, f32[2048]{0:T(1024)}) all-reduce(f32[2048]{0:T(1024)S(1)} %get-tuple-element.341, f32[2048]{0:T(1024)S(1)} %copy-done.35), channel_id=1, replica_groups=mesh['dp'=8,'tensor'=4] {'dp','tensor'}, use_global_device_ids=true, to_apply=%region_16.17 | all-reduce | flops 4096 | bytes 32768 | tf_op jit(solution)/shard_map/psum | solution.py:231
  1306.8 32.4 %reduce-scatter.14.cloned.1.call-done = bf16[256,2048]{1,0:T(8,128)(2,1)} async-done(((bf16[1024,2048]{1,0:T(8,128)(2,1)}), bf16[256,2048]{1,0:T(8,128)(2,1)}) %reduce-scatter.14.cloned.1.call-update) | async-done | bytes 1048592 | tf_op jit(solution)/shard_map/reduce_scatter | solution.py:140
  1339.3 5.1 fusion.69
  (233 shorter events, 118.1 us)
Async XLA Ops:
  7.2 18.2 %copy-start.34 = (bf16[256,128]{1,0:T(8,128)(2,1)S(1)}, bf16[256,128]{1,0:T(8,128)(2,1)}, u32[]{:S(2)}) copy-start(bf16[256,128]{1,0:T(8,128)(2,1)} %param.23) | copy-start | bytes 196612
  7.2 88.8 %all-gather.10.cloned.1.call-start = ((), (), s32[]{:S(2)}) async-start(), calls=%async_computation.11 | async-start | bytes 5242880 | tf_op jit(solution)/shard_map/all_gather | solution.py:67
  12.4 111.8 %all-gather.12.cloned.1.call-start = ((), (), s32[]{:S(2)}) async-start(), calls=%async_computation.12 | async-start | bytes 2359296 | tf_op jit(solution)/shard_map/all_gather | solution.py:69
  13.2 150.5 %all-gather.14.cloned.1.call-start = ((), (), s32[]{:S(2)}) async-start(), calls=%async_computation.13 | async-start | bytes 2359296 | tf_op jit(solution)/shard_map/all_gather | solution.py:72
  13.9 233.7 %reduce-scatter.12.cloned.1.call-start = ((), (), s32[]{:S(2)}) async-start(), calls=%async_computation.14 | async-start | bytes 5242880 | tf_op jit(solution)/shard_map/reduce_scatter | solution.py:123
  25.4 104.1 %copy-start.21 = (bf16[2048,128]{1,0:T(8,128)(2,1)}, bf16[2048,128]{1,0:T(8,128)(2,1)S(1)}, u32[]{:S(2)}) copy-start(bf16[2048,128]{1,0:T(8,128)(2,1)S(1)} %all_gather.35) | copy-start | bytes 1572868
  35.2 94.8 %copy-start.19 = (bf16[2048,128]{1,0:T(8,128)(2,1)}, bf16[2048,128]{1,0:T(8,128)(2,1)S(1)}, u32[]{:S(2)}) copy-start(bf16[2048,128]{1,0:T(8,128)(2,1)S(1)} %all_gather.36) | copy-start | bytes 1572868
  35.7 93.8 %copy-start.24 = (f32[1024,32]{0,1:T(8,128)}, f32[1024,32]{0,1:T(8,128)S(1)}, u32[]{:S(2)}) copy-start(f32[1024,32]{0,1:T(8,128)S(1)} %get-tuple-element.402) | copy-start | bytes 393220
  35.7 93.8 %copy-start.26 = (f32[1024,32]{0,1:T(8,128)}, f32[1024,32]{0,1:T(8,128)S(1)}, u32[]{:S(2)}) copy-start(f32[1024,32]{0,1:T(8,128)S(1)} %get-tuple-element.403) | copy-start | bytes 393220
  170.6 77.0 %copy-start.5 = (bf16[256,2048]{1,0:T(8,128)(2,1)S(1)}, bf16[256,2048]{1,0:T(8,128)(2,1)}, u32[]{:S(2)}) copy-start(bf16[256,2048]{1,0:T(8,128)(2,1)} %param.17) | copy-start | bytes 3145732
  170.6 78.6 %copy-start.30 = (f32[2048]{0:T(1024)S(1)}, f32[2048]{0:T(1024)}, u32[]{:S(2)}) copy-start(f32[2048]{0:T(1024)} %param.25) | copy-start | bytes 24580
  170.7 133.5 %all-gather.20.cloned.1.call-start = ((), (), s32[]{:S(2)}) async-start(), calls=%async_computation.17 | async-start | bytes 9437184 | tf_op jit(solution)/shard_map/all_gather | solution.py:134
  171.2 215.6 %all-gather.16.cloned.1.call-start = ((), (), s32[]{:S(2)}) async-start(), calls=%async_computation.15 | async-start | bytes 5242880 | tf_op jit(solution)/shard_map/all_gather | solution.py:131
  249.2 458.3 %copy-start.36 = (f32[256]{0:T(256)}, f32[256]{0:T(256)S(1)}, u32[]{:S(2)}) copy-start(f32[256]{0:T(256)S(1)} %fusion.73) | copy-start | bytes 3076
  251.9 189.7 %all-gather.18.cloned.1.call-start = ((), (), s32[]{:S(2)}) async-start(), calls=%async_computation.16 | async-start | bytes 9437184 | tf_op jit(solution)/shard_map/all_gather | solution.py:133
  252.6 271.3 %all-gather.24.cloned.1.call-start = ((), (), s32[]{:S(2)}) async-start(), calls=%async_computation.20 | async-start | bytes 5242880 | tf_op jit(solution)/shard_map/all_gather | solution.py:147
  253.4 326.8 %all-gather.22.cloned.1.call-start = ((), (), s32[]{:S(2)}) async-start(), calls=%async_computation.18 | async-start | bytes 9437184 | tf_op jit(solution)/shard_map/all_gather | solution.py:135
  254.1 450.7 %reduce-scatter.16.cloned.1.call-start = ((), (), s32[]{:S(2)}) async-start(), calls=%async_computation.21 | async-start | bytes 5242880 | tf_op jit(solution)/shard_map/reduce_scatter | solution.py:156
  602.0 12.9 copy-start.48
  627.8 77.0 %copy-start.10 = (bf16[256,2048]{1,0:T(8,128)(2,1)S(1)}, bf16[256,2048]{1,0:T(8,128)(2,1)}, u32[]{:S(2)}) copy-start(bf16[256,2048]{1,0:T(8,128)(2,1)} %reduce-scatter.12.cloned.1.call-done) | copy-start | bytes 3145732
  627.8 79.8 %copy-start.16 = (bf16[256,2048]{1,0:T(8,128)(2,1)S(1)}, bf16[256,2048]{1,0:T(8,128)(2,1)}, u32[]{:S(2)}) copy-start(bf16[256,2048]{1,0:T(8,128)(2,1)} %param.29) | copy-start | bytes 3145732
  627.8 164.4 %all-gather.26.cloned.1.call-start = ((), (), s32[]{:S(2)}) async-start(), calls=%async_computation.22 | async-start | bytes 5242880 | tf_op jit(solution)/shard_map/all_gather | solution.py:168
  707.6 17.7 %copy-start.40 = (f32[256]{0:T(256)}, f32[256]{0:T(256)S(1)}, u32[]{:S(2)}) copy-start(f32[256]{0:T(256)S(1)} %multiply_multiply_fusion.1) | copy-start | bytes 3076
  710.8 268.4 %reduce-scatter.30.cloned.1.call-start = ((), (), s32[]{:S(2)}) async-start(), calls=%async_computation.29 | async-start | bytes 9437184 | tf_op jit(solution)/shard_map/reduce_scatter | solution.py:248
  725.3 256.7 %reduce-scatter.28.cloned.1.call-start = ((), (), s32[]{:S(2)}) async-start(), calls=%async_computation.28 | async-start | bytes 9437184 | tf_op jit(solution)/shard_map/reduce_scatter | solution.py:245
  739.5 275.7 %reduce-scatter.32.cloned.1.call-start = ((), (), s32[]{:S(2)}) async-start(), calls=%async_computation.30 | async-start | bytes 9437184 | tf_op jit(solution)/shard_map/reduce_scatter | solution.py:251
  753.6 38.6 %copy-start.46 = (bf16[512,2048]{1,0:T(8,128)(2,1)S(1)}, bf16[512,2048]{1,0:T(8,128)(2,1)}, u32[]{:S(2)}) copy-start(bf16[512,2048]{1,0:T(8,128)(2,1)} %all-gather.14.cloned.1.call-done) | copy-start | bytes 6291460
  753.6 44.1 %copy-start.4 = (bf16[1024,2,64]{0,2,1:T(8,128)(2,1)S(1)}, bf16[1024,2,64]{0,2,1:T(8,128)(2,1)}, u32[]{:S(2)}) copy-start(bf16[1024,2,64]{0,2,1:T(8,128)(2,1)} %copy-done.3) | copy-start | bytes 786436
  753.6 44.1 %copy-start.15 = (bf16[1024,2,64]{0,2,1:T(8,128)(2,1)S(1)}, bf16[1024,2,64]{0,2,1:T(8,128)(2,1)}, u32[]{:S(2)}) copy-start(bf16[1024,2,64]{0,2,1:T(8,128)(2,1)} %copy-done.14) | copy-start | bytes 786436
  753.7 44.0 %copy-start.29 = (s32[1024]{0:T(1024)S(1)}, s32[1024]{0:T(1024)}, u32[]{:S(2)}) copy-start(s32[1024]{0:T(1024)} %param.18) | copy-start | bytes 12292
  753.7 299.1 %reduce-scatter.24.cloned.1.call-start = ((), (), s32[]{:S(2)}) async-start(), calls=%async_computation.26 | async-start | bytes 589824 | tf_op jit(solution)/shard_map/reduce_scatter | solution.py:239
  889.0 12.3 copy-start.2
  889.0 12.3 copy-start.7
  936.4 154.0 %reduce-scatter.22.cloned.1.call-start = ((), (), s32[]{:S(2)}) async-start(), calls=%async_computation.25 | async-start | bytes 589824 | tf_op jit(solution)/shard_map/reduce_scatter | solution.py:236
  941.2 193.6 %reduce-scatter.26.cloned.1.call-start = ((), (), s32[]{:S(2)}) async-start(), calls=%async_computation.27 | async-start | bytes 2359296 | tf_op jit(solution)/shard_map/reduce_scatter | solution.py:242
  947.1 232.5 %reduce-scatter.20.cloned.1.call-start = ((), (), s32[]{:S(2)}) async-start(), calls=%async_computation.24 | async-start | bytes 2359296 | tf_op jit(solution)/shard_map/reduce_scatter | solution.py:233
  956.9 301.8 %reduce-scatter.18.cloned.1.call-start = ((), (), s32[]{:S(2)}) async-start(), calls=%async_computation.23 | async-start | bytes 5242880 | tf_op jit(solution)/shard_map/reduce_scatter | solution.py:218
  965.2 374.0 %reduce-scatter.14.cloned.1.call-start = ((), (), s32[]{:S(2)}) async-start(), calls=%async_computation.19 | async-start | bytes 5242880 | tf_op jit(solution)/shard_map/reduce_scatter | solution.py:140
  982.0 276.7 %copy-start.6 = (bf16[256,2048]{1,0:T(8,128)(2,1)S(1)}, bf16[256,2048]{1,0:T(8,128)(2,1)}, u32[]{:S(2)}) copy-start(bf16[256,2048]{1,0:T(8,128)(2,1)} %param.17) | copy-start | bytes 3145732
  982.0 276.7 %copy-start.32 = (f32[2048]{0:T(1024)S(1)}, f32[2048]{0:T(1024)}, u32[]{:S(2)}) copy-start(f32[2048]{0:T(1024)} %param.20) | copy-start | bytes 24580
  982.0 276.7 %copy-start.39 = (f32[256]{0:T(256)S(1)}, f32[256]{0:T(256)}, u32[]{:S(2)}) copy-start(f32[256]{0:T(256)} %copy-done.38) | copy-start | bytes 3076
  984.9 276.1 %copy-start.35 = (f32[2048]{0:T(1024)S(1)}, f32[2048]{0:T(1024)}, u32[]{:S(2)}) copy-start(f32[2048]{0:T(1024)} %get-tuple-element.339) | copy-start | bytes 24580
  984.9 321.9 %copy-start.43 = (f32[256]{0:T(256)S(1)}, f32[256]{0:T(256)}, u32[]{:S(2)}) copy-start(f32[256]{0:T(256)} %copy-done.42) | copy-start | bytes 3076
  984.9 354.3 %copy-start.11 = (bf16[256,2048]{1,0:T(8,128)(2,1)S(1)}, bf16[256,2048]{1,0:T(8,128)(2,1)}, u32[]{:S(2)}) copy-start(bf16[256,2048]{1,0:T(8,128)(2,1)} %reduce-scatter.12.cloned.1.call-done) | copy-start | bytes 3145732
  984.9 354.3 %copy-start.17 = (bf16[256,2048]{1,0:T(8,128)(2,1)S(1)}, bf16[256,2048]{1,0:T(8,128)(2,1)}, u32[]{:S(2)}) copy-start(bf16[256,2048]{1,0:T(8,128)(2,1)} %param.29) | copy-start | bytes 3145732
  984.9 354.3 %copy-start.31 = (f32[2048]{0:T(1024)S(1)}, f32[2048]{0:T(1024)}, u32[]{:S(2)}) copy-start(f32[2048]{0:T(1024)} %param.25) | copy-start | bytes 24580
  984.9 354.3 %copy-start.37 = (f32[256]{0:T(256)S(1)}, f32[256]{0:T(256)}, u32[]{:S(2)}) copy-start(f32[256]{0:T(256)} %copy-done.36) | copy-start | bytes 3076
  984.9 354.3 %copy-start.41 = (f32[256]{0:T(256)S(1)}, f32[256]{0:T(256)}, u32[]{:S(2)}) copy-start(f32[256]{0:T(256)} %copy-done.40) | copy-start | bytes 3076
  (27 other events, 121.2 us)
Sparse Core Ops, SparseCore 0:
  12.6 83.4 all-gather.9
  97.9 26.2 all-gather.11
  126.1 28.1 all-gather.13
  170.8 76.7 reduce-scatter.11
  249.3 54.7 all-gather.19
  306.1 80.7 all-gather.15
  388.8 52.7 all-gather.17
  443.1 80.7 all-gather.23
  525.8 54.3 all-gather.21
  627.9 76.7 reduce-scatter.15
  710.9 81.2 all-gather.25
  795.5 69.9 reduce-scatter.29
  869.0 71.4 reduce-scatter.27
  943.8 71.2 reduce-scatter.31
  1018.7 34.1 reduce-scatter.23
  1056.3 34.0 reduce-scatter.21
  1093.6 41.1 reduce-scatter.25
  1138.5 41.0 reduce-scatter.19
  1181.9 76.7 reduce-scatter.17
  1260.9 78.3 reduce-scatter.13
where the time goes:
time: 1360 us; the launch traced here: 1350 us
  waiting for transfers between devices  874 us (64%)
  matrix products  253 us (19%)
  other arithmetic  68.7 us (5%)
  blocking collectives  67 us (5%)
  local copies, waits for them, and re-layouts  65 us (5%)
  between operations  15.1 us (1%)
    all_gather x1, waiting for transfers between devices, local(): normed_mid = lax.all_gather(normed_mid_local, 'tensor', axis=0, tiled=True)  82.8 us
    reduce_scatter x1, waiting for transfers between devices, local(): lax.psum_scatter((jnp.einsum('rc,dc->rd', query_rows, query_all, preferre...  77.3 us
    reduce_scatter x1, waiting for transfers between devices, local(): lax.psum_scatter((jnp.einsum('rf,df->rd', d_gate, gate_all, preferred_ele...  76.9 us
    reduce_scatter x1, waiting for transfers between devices, local(): lax.psum_scatter(jnp.dot(context, out_all, preferred_element_type=jnp.flo...  76.3 us
    all_gather x1, waiting for transfers between devices, local(): cot_all = lax.all_gather(cotangent, 'tensor', axis=0, tiled=True)  67.9 us
    all_gather x1, waiting for transfers between devices, local(): normed_in = lax.all_gather(normed_local, 'tensor', axis=0, tiled=True)  60.3 us
    all_gather x1, waiting for transfers between devices, local(): lax.all_gather(w_down, 'dp', axis=1, tiled=True)  56.3 us
    all_gather x1, waiting for transfers between devices, local(): lax.all_gather(w_up, 'dp', axis=0, tiled=True)  50 us
  transfers between devices with their start and end apart: 20, of which 17 were waited for; matrix products, arithmetic and copies ran while one was open for 22% of the time, Pallas kernels for 0%

commit v1 on v0

v1 whole, which is shorter than its diff:
```python
from functools import partial
import math

import jax
import jax.numpy as jnp
from jax import lax
from jax.experimental import pallas as pl
from jax.experimental.pallas import tpu as pltpu
from jax.sharding import PartitionSpec as P


QH = 32
KVH = 8
HD = 64
LEN = 1024
WIDTH = 2048
GROUP = QH // KVH
LANES = 128
TILE = 256
NEG = -1e30
DP, TENSOR = "dp", "tensor"
EPS = 1e-05
VMEM_LIMIT = 58 << 20


f32 = jnp.float32
bf16 = jnp.bfloat16


def dot(a, b, contract):
    return lax.dot_general(a, b, (contract, ((), ())), preferred_element_type=f32)


def ways_of(n):
    return 2 if WIDTH // n >= 2 * LANES else 1


def routes_of(n):
    bits = list(range(1, n.bit_length() - 1))
    return [bits, bits[::-1]][: ways_of(n)]


def block_slots(n):
    count, ways = n // 2, ways_of(n)
    return [(h, 0) for h in range(ways)] + [(h, s) for h in range(ways) for s in range(1, count)]


def width_order(n):
    routes, ways = routes_of(n), ways_of(n)
    order = []
    for core in range(2):
        for h, s in block_slots(n):
            j = core
            for t, b in enumerate(routes[h]):
                j |= ((s >> t) & 1) << b
            order.append(ways * j + h)
    return order


def swap(x, axis, n, b):
    return lax.ppermute(x, axis, [(i, i ^ (1 << b)) for i in range(n)])


def dp_gather(shard, n):
    routes, ways = routes_of(n), ways_of(n)
    size = shard.shape[0] // ways
    parts = [[shard[h * size : (h + 1) * size]] for h in range(ways)]
    for t in range(len(routes[0])):
        for h in range(ways):
            parts[h] += [swap(p, DP, n, routes[h][t]) for p in parts[h]]
    own = [shard] + [p for part in parts for p in part[1:]]
    return own + [swap(p, DP, n, 0) for p in own]


def scatter_segments(n):
    count, ways = n // 2, ways_of(n)
    size = WIDTH // n // ways
    half = count // 2
    cuts = [(ways + half - 1) * size, half * size]
    if ways > 1:
        cuts += [(half - 1) * size, half * size]
    return size, cuts


def add_kernel(*refs, spans):
    count = len(spans)
    for i, (at, rows, size) in enumerate(spans):
        kept, got, out = refs[2 * i], refs[2 * i + 1], refs[2 * count + i]
        total = kept[pl.ds(at, rows), :].astype(f32) + got[pl.ds(size, rows), :].astype(f32)
        out[...] = total.astype(bf16)


def add_rows(pairs, size):
    tile = 1024
    columns = pairs[0][0].shape[1]
    arrays = [x for array, _, _, got in pairs for x in (array, got)]
    return pl.pallas_call(
        partial(add_kernel, spans=[(at, rows, size) for _, at, rows, _ in pairs]),
        grid=(columns // tile,),
        in_specs=[pl.BlockSpec((x.shape[0], tile), lambda i: (0, i)) for x in arrays],
        out_specs=tuple(pl.BlockSpec((rows, tile), lambda i: (0, i)) for _, _, rows, _ in pairs),
        out_shape=tuple(jax.ShapeDtypeStruct((rows, columns), bf16) for _, _, rows, _ in pairs),
        compiler_params=pltpu.CompilerParams(vmem_limit_bytes=VMEM_LIMIT),
    )(*arrays)


def dp_scatter(pieces, n):
    routes, ways = routes_of(n), ways_of(n)
    size, _ = scatter_segments(n)
    kept = [(pieces[0], ways * size)] + ([(pieces[2], 0)] if ways > 1 else [])
    send = [pieces[1]] + ([pieces[3]] if ways > 1 else [])
    terms = [[] for _ in range(ways)]
    slots = n // 4
    for t in reversed(range(len(routes[0]))):
        for h in range(ways):
            terms[h].append(swap(send[h], DP, n, routes[h][t]))
        if t:
            rows = (slots - 1) * size
            sums = add_rows([(*kept[h], rows, terms[h][-1]) for h in range(ways)], size)
            slots //= 2
            send = [x[(slots - 1) * size :] if slots > 1 else x for x in sums]
            kept = [(x, 0) for x in sums]
    return pieces[0], terms


def width_at(order_ref, k, width):
    return pl.ds(pl.multiple_of(order_ref[k] * width, width), width)


def reorder_kernel(order_ref, *refs, inverse):
    ins, outs = refs[: len(refs) // 2], refs[len(refs) // 2 :]
    count = order_ref.shape[0]
    for src, dst in zip(ins, outs):
        width = src.shape[1] // count
        for k in range(count):
            here = pl.ds(k * width, width)
            if inverse:
                dst[:, width_at(order_ref, k, width)] = src[:, here]
            else:
                dst[:, here] = src[:, width_at(order_ref, k, width)]


SMEM_SPEC = pl.BlockSpec(memory_space=pltpu.SMEM)
VMEM_SPEC = pl.BlockSpec(memory_space=pltpu.VMEM)


def reorder(order, arrays, inverse):
    return pl.pallas_call(
        partial(reorder_kernel, inverse=inverse),
        out_shape=tuple(jax.ShapeDtypeStruct(a.shape, a.dtype) for a in arrays),
        in_specs=[SMEM_SPEC] + [VMEM_SPEC] * len(arrays),
        out_specs=tuple(VMEM_SPEC for _ in arrays),
    )(order, *arrays)


def unpack_kernel(me_ref, *refs, kv):
    out_ref = refs[-1]
    count = len(refs) - 1
    for s, ref in enumerate(refs[:-1]):
        z = jnp.bitwise_xor(me_ref[0], s)
        for i in range(2):
            at = pl.ds(pl.multiple_of((i * count + z) * kv, kv), kv)
            out_ref[:, at] = ref[:, pl.ds(i * kv, kv)]


def unpack_kv(me, slots, kv):
    rows = slots[0].shape[0]
    return pl.pallas_call(
        partial(unpack_kernel, kv=kv),
        out_shape=jax.ShapeDtypeStruct((rows, 2 * kv * len(slots)), bf16),
        in_specs=[SMEM_SPEC] + [VMEM_SPEC] * len(slots),
        out_specs=VMEM_SPEC,
        name="uk",
    )(me, *slots)


def unpack_pair_kernel(in_ref, *outs):
    rows, width = outs[0].shape[0], in_ref.shape[1] // len(outs)
    for z in range(in_ref.shape[0] // rows):
        for i, out in enumerate(outs):
            out[:, pl.ds(z * width, width)] = in_ref[pl.ds(z * rows, rows), pl.ds(i * width, width)]


def unpack_pair(x, n_tensor):
    rows, total = x.shape[0] // n_tensor, x.shape[1] * n_tensor // 2
    return pl.pallas_call(
        unpack_pair_kernel,
        out_shape=tuple(jax.ShapeDtypeStruct((rows, total), x.dtype) for _ in range(2)),
        in_specs=[VMEM_SPEC],
        out_specs=(VMEM_SPEC, VMEM_SPEC),
        name="uq",
    )(x)


def shard_sum(first_ref, terms, ways, at):
    parts = []
    for h in range(ways):
        size = terms[h][-1].shape[0]
        total = first_ref[pl.ds(h * size, size), at].astype(f32)
        for t in terms[h]:
            total = total + t[pl.ds(0, size), at].astype(f32)
        parts.append(total)
    return parts[0] if ways == 1 else jnp.concatenate(parts, axis=0)


def split_terms(refs, ways):
    each = len(refs) // ways
    return [refs[h * each : (h + 1) * each] for h in range(ways)]


def flat(scattered):
    first, terms = scattered
    return [first] + [t for part in terms for t in part]


def pack_kernel(*refs, n_tensor, ways, groups):
    out_ref = refs[-1]
    rows = out_ref.shape[0] // n_tensor
    count = (len(refs) - 1) // len(groups)
    for i, cuts in enumerate(groups):
        mine = refs[i * count : (i + 1) * count]
        terms = split_terms(mine[1:], ways)
        for z in range(n_tensor):
            for at, width, start in cuts:
                total = shard_sum(mine[0], terms, ways, pl.ds(start + z * width, width))
                out_ref[pl.ds(z * rows, rows), pl.ds(at, width)] = total.astype(out_ref.dtype)


def pack(scattered, groups, n_tensor, ways, columns, rows):
    arrays = [a for s in scattered for a in flat(s)]
    return pl.pallas_call(
        partial(pack_kernel, n_tensor=n_tensor, ways=ways, groups=groups),
        out_shape=jax.ShapeDtypeStruct((n_tensor * rows, columns), bf16),
        in_specs=[VMEM_SPEC] * len(arrays),
        out_specs=VMEM_SPEC,
        compiler_params=pltpu.CompilerParams(vmem_limit_bytes=VMEM_LIMIT),
    )(*arrays)


def final_kernel(*refs, ways, transposed):
    out_ref = refs[-1]
    total = shard_sum(refs[0], split_terms(refs[1:-1], ways), ways, slice(None))
    out_ref[...] = total.T if transposed else total


def finish(scattered, start, columns, ways, transposed):
    arrays = flat(scattered)
    size = scattered[1][0][-1].shape[0]
    rows = ways * size
    tile = 512
    base = start // tile
    blocks = [rows] + [size] * (len(arrays) - 1)
    return pl.pallas_call(
        partial(final_kernel, ways=ways, transposed=transposed),
        grid=(columns // tile,),
        out_shape=jax.ShapeDtypeStruct((columns, rows) if transposed else (rows, columns), f32),
        in_specs=[pl.BlockSpec((b, tile), lambda i: (0, base + i)) for b in blocks],
        out_specs=pl.BlockSpec((tile, rows) if transposed else (rows, tile), (lambda i: (i, 0)) if transposed else (lambda i: (0, i))),
    )(*arrays)


def joined(refs):
    return jnp.concatenate([r[...] for r in refs], axis=0)


def piece_specs(pieces, tile, column):
    return [pl.BlockSpec((p.shape[0], tile), lambda i, *_: (0, column(i))) for p in pieces]


def swap_halves(u):
    lane = lax.broadcasted_iota(jnp.int32, u.shape, 1)
    up = pltpu.roll(u, HD // 2, 1)
    down = pltpu.roll(u, LANES - HD // 2, 1)
    return jnp.where((lane % HD) < HD // 2, down, up)


def turn(u, cosine, signed_sine, back):
    s = swap_halves(u) * signed_sine
    return u * cosine - s if back else u * cosine + s


def proj_kv_kernel(x_ref, cos_ref, sin_ref, *refs, key_tiles):
    out_ref = refs[-1]
    raw = dot(x_ref[...], joined(refs[:-1]), ((1,), (0,)))
    is_key = pl.program_id(0) < key_tiles
    cosine = jnp.where(is_key, cos_ref[...], 1.0)
    sine = jnp.where(is_key, sin_ref[...], 0.0)
    for c in range(raw.shape[1] // LANES):
        part = raw[:, c * LANES : (c + 1) * LANES]
        out_ref[:, pl.ds(c * LANES, LANES)] = turn(part, cosine, sine, False).astype(bf16)


def proj_kv(x, cosine, sine, pieces):
    rows = x.shape[0]
    whole = lambda shape: pl.BlockSpec(shape, lambda i: (0, 0))
    return pl.pallas_call(
        partial(proj_kv_kernel, key_tiles=KVH * HD // TILE),
        grid=(2 * KVH * HD // TILE,),
        in_specs=[whole(x.shape), whole(cosine.shape), whole(sine.shape)] + piece_specs(pieces, TILE, lambda i: i),
        out_specs=pl.BlockSpec((rows, TILE), lambda i: (0, i)),
        out_shape=jax.ShapeDtypeStruct((rows, 2 * KVH * HD), bf16),
        cost_estimate=pl.CostEstimate(flops=4 * rows * WIDTH * KVH * HD, bytes_accessed=6 << 20, transcendentals=0),
        compiler_params=pltpu.CompilerParams(vmem_limit_bytes=VMEM_LIMIT),
        name="pk",
    )(x, cosine, sine, *pieces)


def rope_kv_kernel(kv_ref, cos_ref, sin_ref, out_ref, *, key_width):
    cosine, sine = cos_ref[...], sin_ref[...]
    for c in range(key_width // LANES):
        at = pl.ds(c * LANES, LANES)
        out_ref[:, at] = turn(kv_ref[:, at].astype(f32), cosine, sine, True).astype(bf16)
    out_ref[:, key_width:] = kv_ref[:, key_width:]


def rope_kv_back(kv, cosine, sine):
    return pl.pallas_call(
        partial(rope_kv_kernel, key_width=kv.shape[1] // 2),
        out_shape=jax.ShapeDtypeStruct(kv.shape, bf16),
        name="rk",
    )(kv, cosine, sine)


def split_halves(block, odd):
    wide = block.astype(f32)
    rolled = pltpu.roll(wide, HD, 1)
    lane = lax.broadcasted_iota(jnp.int32, wide.shape, 1)
    low = lane < HD
    first = jnp.where(odd, rolled, wide)
    second = jnp.where(odd, wide, rolled)
    zero = jnp.zeros_like(wide)
    return jnp.where(low, first, zero).astype(bf16), jnp.where(low, zero, second).astype(bf16)


def attn_fwd_kernel(row0_ref, seg_ref, x_ref, k_ref, v_ref, cos_ref, sin_ref, *refs, count):
    w_query = refs[:count]
    ctx_ref, rot_ref, lse_ref, bias_ref = refs[-4:]
    g = pl.program_id(0)
    rows = x_ref.shape[0]

    @pl.when(g == 0)
    def _():
        t = row0_ref[0] + lax.broadcasted_iota(jnp.int32, bias_ref.shape, 0)
        s = lax.broadcasted_iota(jnp.int32, bias_ref.shape, 1)
        allowed = (s <= t) & (s >= seg_ref[...])
        bias_ref[...] = jnp.where(allowed, 0.0, NEG)

    q_raw = dot(x_ref[...], joined(w_query), ((1,), (0,)))
    odd = lax.rem(g, 2) == 1
    keys = split_halves(k_ref[...], odd)
    values = split_halves(v_ref[...], odd)
    lane = lax.broadcasted_iota(jnp.int32, (rows, LANES), 1)
    log_sums = jnp.zeros((rows, LANES), f32)
    for c in range(GROUP // 2):
        at = pl.ds(c * LANES, LANES)
        turned = turn(q_raw[:, c * LANES : (c + 1) * LANES], cos_ref[...], sin_ref[...], False)
        query = (turned * (HD**-0.5)).astype(bf16)
        rot_ref[:, at] = query
        total = jnp.zeros((rows, LANES), f32)
        for e in range(2):
            scores = dot(query, keys[e], ((1,), (1,))) + bias_ref[...]
            peak = jnp.max(scores, axis=1, keepdims=True)
            weights = jnp.exp(scores - peak)
            mass = jnp.sum(weights, axis=1, keepdims=True)
            part = dot(weights.astype(bf16), values[e], ((1,), (0,)))
            total = total + part * (1.0 / mass)
            log_sums = jnp.where(lane == 2 * c + e, peak + jnp.log(mass), log_sums)
        ctx_ref[:, at] = total.astype(bf16)
    lse_ref[...] = log_sums


FWD_PARTS = 2


def attn_forward(row0, seg_col, x, kv, cosine, sine, pieces, part, before):
    rows = x.shape[0]
    half = KVH * HD // LANES
    heads = KVH // FWD_PARTS
    base = part * heads
    args = [row0, seg_col, x, kv, kv, cosine, sine, *pieces]
    whole = lambda shape: pl.BlockSpec(shape, lambda g, r: (0, 0))
    grid_spec = pltpu.PrefetchScalarGridSpec(
        num_scalar_prefetch=1,
        grid=(heads,),
        in_specs=[
            whole((rows, 1)),
            whole(x.shape),
            pl.BlockSpec((LEN, LANES), lambda g, r: (0, (base + g) // 2)),
            pl.BlockSpec((LEN, LANES), lambda g, r: (0, half + (base + g) // 2)),
            whole((rows, LANES)),
            whole((rows, LANES)),
        ]
        + piece_specs(pieces, TILE, lambda g: base + g)
        + [pl.BlockSpec(memory_space=pl.ANY)] * len(before),
        out_specs=[
            pl.BlockSpec((rows, TILE), lambda g, r: (0, base + g)),
            pl.BlockSpec((rows, TILE), lambda g, r: (0, base + g)),
            pl.BlockSpec((rows, LANES), lambda g, r: (0, base + g)),
        ],
        scratch_shapes=[pltpu.VMEM((rows, LEN), f32)],
    )
    return pl.pallas_call(
        partial(attn_fwd_kernel, count=len(pieces)),
        grid_spec=grid_spec,
        out_shape=(
            jax.ShapeDtypeStruct((rows, QH * HD), bf16),
            jax.ShapeDtypeStruct((rows, QH * HD), bf16),
            jax.ShapeDtypeStruct((rows, KVH * LANES), f32),
        ),
        cost_estimate=pl.CostEstimate(
            flops=8 * rows * LEN * QH * HD, bytes_accessed=12 << 20, transcendentals=rows * LEN * QH // FWD_PARTS
        ),
        compiler_params=pltpu.CompilerParams(vmem_limit_bytes=VMEM_LIMIT),
        input_output_aliases={len(args) + i: i for i in range(len(before))},
    )(*args, *before)


def out_proj_kernel(ctx_ref, tok_ref, gain_ref, *refs):
    mid_ref, norm_ref, sum_ref = refs[-3:]
    i = pl.program_id(0)

    @pl.when(i == 0)
    def _():
        sum_ref[...] = tok_ref[...].astype(f32)

    sum_ref[...] += dot(ctx_ref[...], joined(refs[:-3]), ((1,), (1,)))

    @pl.when(i == pl.num_programs(0) - 1)
    def _():
        middle = sum_ref[...]
        mid_ref[...] = middle
        inverse = lax.rsqrt(jnp.mean(middle * middle, axis=1, keepdims=True) + EPS)
        norm_ref[...] = (middle * inverse * gain_ref[...]).astype(bf16)


def out_proj(context, tokens, gain, pieces):
    rows = context.shape[0]
    tile = 512
    whole = lambda shape: pl.BlockSpec(shape, lambda i: (0, 0))
    return pl.pallas_call(
        out_proj_kernel,
        grid=(QH * HD // tile,),
        in_specs=[pl.BlockSpec((rows, tile), lambda i: (0, i)), whole(tokens.shape), whole(gain.shape)]
        + piece_specs(pieces, tile, lambda i: i),
        out_specs=(whole((rows, WIDTH)), whole((rows, WIDTH))),
        out_shape=(jax.ShapeDtypeStruct((rows, WIDTH), f32), jax.ShapeDtypeStruct((rows, WIDTH), bf16)),
        scratch_shapes=[pltpu.VMEM((rows, WIDTH), f32)],
        cost_estimate=pl.CostEstimate(flops=2 * rows * WIDTH * QH * HD, bytes_accessed=14 << 20, transcendentals=0),
        compiler_params=pltpu.CompilerParams(vmem_limit_bytes=VMEM_LIMIT),
        name="op",
    )(context, tokens, gain, *pieces)


def rms_back(values, gain, grad):
    inverse = lax.rsqrt(jnp.mean(values * values, axis=1, keepdims=True) + EPS)
    scaled = gain * grad
    along = jnp.mean(scaled * values, axis=1, keepdims=True)
    d_values = inverse * scaled - values * (inverse * inverse * inverse) * along
    d_gain = jnp.sum(grad * values * inverse, axis=0, keepdims=True)
    return d_values, d_gain


def mid_back_kernel(mid_ref, gain_ref, cot_ref, *refs):
    dmid_ref, db_ref, dg_ref = refs[-3:]
    d_values, d_gain = rms_back(mid_ref[...], gain_ref[...], joined(refs[:-3]).astype(f32))
    d_middle = cot_ref[...].astype(f32) + d_values
    dmid_ref[...] = d_middle
    db_ref[...] = d_middle.astype(bf16)
    dg_ref[...] = jnp.broadcast_to(d_gain, dg_ref.shape)


def mid_back(d_normed, middle, gain, cot):
    rows = middle.shape[0]
    return pl.pallas_call(
        mid_back_kernel,
        out_shape=(
            jax.ShapeDtypeStruct((rows, WIDTH), f32),
            jax.ShapeDtypeStruct((rows, WIDTH), bf16),
            jax.ShapeDtypeStruct((8, WIDTH), f32),
        ),
        name="mb",
    )(middle, gain, cot, *d_normed)


def attn_bwd_kernel(
    row0_ref, seg_ref, q_ref, k_ref, v_ref, db_ref, ctx_ref, lse_ref, cos_ref, sin_ref, *refs, count
):
    w_query, w_out = refs[:count], refs[count : 2 * count]
    dq_ref, dk_ref, dv_ref, dn_ref, bias_ref = refs[2 * count :]
    g = pl.program_id(0)
    rows = q_ref.shape[0]

    @pl.when(g == 0)
    def _():
        s = lax.broadcasted_iota(jnp.int32, bias_ref.shape, 0)
        t = row0_ref[0] + lax.broadcasted_iota(jnp.int32, bias_ref.shape, 1)
        allowed = (s <= t) & (s >= seg_ref[...])
        bias_ref[...] = jnp.where(allowed, 0.0, NEG)
        dn_ref[...] = jnp.zeros_like(dn_ref)

    d_context = dot(db_ref[...], joined(w_out), ((1,), (0,))).astype(bf16)
    odd = lax.rem(g, 2) == 1
    keys = split_halves(k_ref[...], odd)
    values = split_halves(v_ref[...], odd)
    log_sums = lse_ref[...].T
    low = lax.broadcasted_iota(jnp.int32, (rows, LANES), 1) < HD
    dk_sum = jnp.zeros((LEN, LANES), f32)
    dv_sum = jnp.zeros((LEN, LANES), f32)
    for c in range(GROUP // 2):
        at = pl.ds(c * LANES, LANES)
        query, d_rows = q_ref[:, at], d_context[:, c * LANES : (c + 1) * LANES]
        both = (d_rows.astype(f32) * ctx_ref[:, at].astype(f32)).T
        dq = jnp.zeros((rows, LANES), f32)
        for e in range(2):
            mine = low if e == 0 else jnp.logical_not(low)
            delta = jnp.sum(both[e * HD : (e + 1) * HD], axis=0, keepdims=True)
            h = 2 * c + e
            scores = dot(keys[e], query, ((1,), (1,))) + bias_ref[...]
            probs = jnp.exp(scores - log_sums[h : h + 1])
            d_probs = dot(values[e], d_rows, ((1,), (1,)))
            d_scores = (probs * (d_probs - delta)).astype(bf16)
            zero = jnp.zeros_like(query)
            dv_sum = dv_sum + dot(probs.astype(bf16), jnp.where(mine, d_rows, zero), ((1,), (0,)))
            dk_sum = dk_sum + dot(d_scores, jnp.where(mine, query, zero), ((1,), (0,)))
            dq = dq + dot(d_scores, keys[e], ((0,), (0,)))
        dq_ref[:, at] = turn(dq * (HD**-0.5), cos_ref[...], sin_ref[...], True).astype(bf16)
    dn_ref[...] += dot(dq_ref[...], joined(w_query), ((1,), (1,)))
    wide_low = lax.broadcasted_iota(jnp.int32, (LEN, LANES), 1) < HD
    keep = wide_low == odd
    for total, out in ((dk_sum, dk_ref), (dv_sum, dv_ref)):
        folded = (total + pltpu.roll(total, HD, 1)).astype(bf16)
        out[...] = jnp.where(keep, out[...], folded)


def attn_backward(row0, seg_row, query, kv, d_branch, context, lse, cosine, sine, q_pieces, out_pieces):
    rows = query.shape[0]
    half = KVH * HD // LANES
    whole = lambda shape: pl.BlockSpec(shape, lambda g, r: (0, 0))
    grid_spec = pltpu.PrefetchScalarGridSpec(
        num_scalar_prefetch=1,
        grid=(KVH,),
        in_specs=[
            whole((1, rows)),
            pl.BlockSpec((rows, TILE), lambda g, r: (0, g)),
            pl.BlockSpec((LEN, LANES), lambda g, r: (0, g // 2)),
            pl.BlockSpec((LEN, LANES), lambda g, r: (0, half + g // 2)),
            whole((rows, WIDTH)),
            pl.BlockSpec((rows, TILE), lambda g, r: (0, g)),
            pl.BlockSpec((rows, LANES), lambda g, r: (0, g)),
            whole((rows, LANES)),
            whole((rows, LANES)),
        ]
        + piece_specs(q_pieces, TILE, lambda g: g)
        + piece_specs(out_pieces, TILE, lambda g: g),
        out_specs=[
            pl.BlockSpec((rows, TILE), lambda g, r: (0, g)),
            pl.BlockSpec((LEN, LANES), lambda g, r: (0, g // 2)),
            pl.BlockSpec((LEN, LANES), lambda g, r: (0, g // 2)),
            whole((rows, WIDTH)),
        ],
        scratch_shapes=[pltpu.VMEM((LEN, rows), f32)],
    )
    return pl.pallas_call(
        partial(attn_bwd_kernel, count=len(q_pieces)),
        grid_spec=grid_spec,
        out_shape=(
            jax.ShapeDtypeStruct((rows, QH * HD), bf16),
            jax.ShapeDtypeStruct((LEN, KVH * HD), bf16),
            jax.ShapeDtypeStruct((LEN, KVH * HD), bf16),
            jax.ShapeDtypeStruct((rows, WIDTH), f32),
        ),
        cost_estimate=pl.CostEstimate(
            flops=28 * rows * LEN * QH * HD, bytes_accessed=28 << 20, transcendentals=rows * LEN * QH
        ),
        compiler_params=pltpu.CompilerParams(vmem_limit_bytes=VMEM_LIMIT),
        name="ab",
    )(row0, seg_row, query, kv, kv, d_branch, context, lse, cosine, sine, *q_pieces, *out_pieces)


def in_back_kernel(order_ref, dkv_ref, part_ref, tok_ref, gain_ref, dmid_ref, dg_mlp_ref, *refs):
    out_ref, dg_ref, sum_ref = refs[-3:]
    i = pl.program_id(0)

    @pl.when(i == 0)
    def _():
        sum_ref[...] = part_ref[...]
        dg_ref[...] = jnp.zeros_like(dg_ref)

    sum_ref[...] += dot(dkv_ref[...], joined(refs[:-3]), ((1,), (1,)))

    @pl.when(i == pl.num_programs(0) - 1)
    def _():
        d_values, d_gain = rms_back(tok_ref[...].astype(f32), gain_ref[...], sum_ref[...])
        d_values = d_values + dmid_ref[...]
        count = order_ref.shape[0]
        width = d_values.shape[1] // count
        for k in range(count):
            at = width_at(order_ref, k, width)
            out_ref[:, at] = d_values[:, k * width : (k + 1) * width]
            dg_ref[0:1, at] = d_gain[:, k * width : (k + 1) * width]
            dg_ref[1:2, at] = dg_mlp_ref[0:1, k * width : (k + 1) * width]


def in_back(order, d_kv, part, tokens, gain, d_middle, mlp_gain, pieces):
    rows = tokens.shape[0]
    whole = lambda shape: pl.BlockSpec(shape, lambda i: (0, 0))
    return pl.pallas_call(
        in_back_kernel,
        grid=(2 * KVH * HD // TILE,),
        in_specs=[SMEM_SPEC, pl.BlockSpec((rows, TILE), lambda i: (0, i))]
        + [whole(a.shape) for a in (part, tokens, gain, d_middle, mlp_gain)]
        + piece_specs(pieces, TILE, lambda i: i),
        out_specs=(whole((rows, WIDTH)), whole((8, WIDTH))),
        out_shape=(jax.ShapeDtypeStruct((rows, WIDTH), f32), jax.ShapeDtypeStruct((8, WIDTH), f32)),
        scratch_shapes=[pltpu.VMEM((rows, WIDTH), f32)],
        cost_estimate=pl.CostEstimate(flops=4 * rows * WIDTH * KVH * HD, bytes_accessed=16 << 20, transcendentals=0),
        compiler_params=pltpu.CompilerParams(vmem_limit_bytes=VMEM_LIMIT),
        name="ib",
    )(order, d_kv, part, tokens, gain, d_middle, mlp_gain, *pieces)


def mlp_kernel(me_ref, x_ref, *refs, slots, count):
    cots, refs = refs[: 2 * slots - 1], refs[2 * slots - 1 :]
    hidden_ref, grads_ref, cot_ref = refs[3 * count :]
    rows = cots[0].shape[0]

    @pl.when(pl.program_id(0) == 0)
    def _():
        for r in range(slots):
            z = lax.rem(me_ref[0] - r + slots, slots)
            value = cots[r][...] + cots[2 * slots - 1 - r][...] if r else cots[0][...]
            cot_ref[pl.ds(pl.multiple_of(z * rows, rows), rows), :] = value

    gate = dot(x_ref[...], joined(refs[:count]), ((1,), (0,)))
    up = dot(x_ref[...], joined(refs[count : 2 * count]), ((1,), (0,)))
    d_hidden = dot(cot_ref[...], joined(refs[2 * count : 3 * count]), ((1,), (0,)))
    sig = jax.nn.sigmoid(gate)
    silu = gate * sig
    hidden_ref[...] = (silu * up).astype(bf16)
    grads_ref[0] = (d_hidden * up * (sig + silu * (1.0 - sig))).astype(bf16)
    grads_ref[1] = (d_hidden * silu).astype(bf16)


def mlp(me, x, cots, chunk, pieces, down_pieces):
    rows = x.shape[0]
    slots = (len(cots) + 1) // 2
    ff = down_pieces[0].shape[1]
    tiles = ff // TILE
    whole = pl.BlockSpec((rows, WIDTH), lambda i: (0, 0))
    specs = [SMEM_SPEC, whole] + [pl.BlockSpec((rows // slots, WIDTH), lambda i: (chunk, 0))] * len(cots)
    for some, base in ((pieces, 0), (pieces, tiles), (down_pieces, 0)):
        specs += piece_specs(some, TILE, partial(lambda i, base: base + i, base=base))
    return pl.pallas_call(
        partial(mlp_kernel, slots=slots, count=len(pieces)),
        grid=(tiles,),
        in_specs=specs,
        out_specs=(
            pl.BlockSpec((rows, TILE), lambda i: (0, i)),
            pl.BlockSpec((2, rows, TILE), lambda i: (0, 0, i)),
            whole,
        ),
        out_shape=(
            jax.ShapeDtypeStruct((rows, ff), bf16),
            jax.ShapeDtypeStruct((2, rows, ff), bf16),
            jax.ShapeDtypeStruct((rows, WIDTH), bf16),
        ),
        cost_estimate=pl.CostEstimate(flops=6 * rows * WIDTH * ff, bytes_accessed=40 << 20, transcendentals=rows * ff),
        compiler_params=pltpu.CompilerParams(vmem_limit_bytes=VMEM_LIMIT),
    )(me, x, *cots, *pieces, *pieces, *down_pieces)


def back_kernel(x_ref, *refs):
    out_ref, sum_ref = refs[-2:]
    i = pl.program_id(0)
    part = dot(x_ref[...].reshape(x_ref.shape[-2:]), joined(refs[:-2]), ((1,), (1,)))

    @pl.when(i == 0)
    def _():
        sum_ref[...] = part

    @pl.when(i > 0)
    def _():
        sum_ref[...] += part

    @pl.when(i == pl.num_programs(0) - 1)
    def _():
        out_ref[...] = sum_ref[...].astype(bf16)


def back(x, pieces):
    many, rows, ff = x.shape
    tile = min(1024, ff)
    per = ff // tile
    return pl.pallas_call(
        back_kernel,
        grid=(many * per,),
        in_specs=[pl.BlockSpec((1, rows, tile), lambda i: (i // per, 0, i % per))]
        + piece_specs(pieces, tile, lambda i: i),
        out_specs=pl.BlockSpec((rows, WIDTH), lambda i: (0, 0)),
        out_shape=jax.ShapeDtypeStruct((rows, WIDTH), bf16),
        scratch_shapes=[pltpu.VMEM((rows, WIDTH), f32)],
        cost_estimate=pl.CostEstimate(flops=2 * many * rows * WIDTH * ff, bytes_accessed=(12 << 20) * many, transcendentals=0),
        compiler_params=pltpu.CompilerParams(vmem_limit_bytes=VMEM_LIMIT),
    )(x, *pieces)


def grad_kernel(*refs, chunks, received, cuts):
    lefts, rights = refs[:chunks], refs[chunks : 2 * chunks]
    outs, turned_ref = refs[2 * chunks + received : -1], refs[-1]

    @pl.when(pl.program_id(0) == 0)
    def _():
        depth = lefts[0].shape[0]
        for c, left in enumerate(lefts):
            turned_ref[:, pl.ds(c * depth, depth)] = left[...].T

    right = jnp.concatenate([r[...].reshape(r.shape[-2:]) for r in rights], axis=0)
    total = dot(turned_ref[...], right, ((1,), (0,)))
    if received:
        total = total + refs[2 * chunks][...].astype(f32)
    at = 0
    for out, rows in zip(outs, cuts):
        out[...] = total[at : at + rows].astype(bf16)
        at += rows


def weight_grad(lefts, rights, block, got, cuts):
    many, depth, columns = rights[0].shape
    rows = WIDTH // 2
    tile = min(512, columns)
    per = columns // tile
    chunks = len(lefts)
    column = lambda i: (0, i)
    extra = [got] if got is not None else []
    specs = [pl.BlockSpec((depth, rows), lambda i: (0, block))] * chunks
    specs += [pl.BlockSpec((1, depth, tile), lambda i: (i // per, 0, i % per))] * chunks
    specs += [pl.BlockSpec((rows, tile), column)] * len(extra)
    return pl.pallas_call(
        partial(grad_kernel, chunks=chunks, received=len(extra), cuts=cuts),
        grid=(many * per,),
        in_specs=specs,
        out_specs=tuple(pl.BlockSpec((c, tile), column) for c in cuts),
        out_shape=tuple(jax.ShapeDtypeStruct((c, many * columns), bf16) for c in cuts),
        scratch_shapes=[pltpu.VMEM((rows, depth * chunks), bf16)],
        cost_estimate=pl.CostEstimate(
            flops=2 * rows * depth * chunks * many * columns, bytes_accessed=8 * rows * many * columns, transcendentals=0
        ),
        compiler_params=pltpu.CompilerParams(vmem_limit_bytes=VMEM_LIMIT),
    )(*lefts, *rights, *extra)


def over_tensor(x, axis=0):
    return lax.all_gather(x, TENSOR, axis=axis, tiled=True)


def sum_tensor(x):
    return lax.psum_scatter(x, TENSOR, scatter_dimension=0, tiled=True)


def layer(
    tokens, segments, positions, norm_attn, w_query, w_key, w_value, w_out,
    norm_mlp, w_gate, w_up, w_down, cotangent, *, n_dp, n_tensor,
):
    me_dp, me_z = lax.axis_index(DP), lax.axis_index(TENSOR)
    rows, width = tokens.shape
    assert rows * n_tensor == LEN and width == WIDTH
    kv, q = w_key.shape[1], w_query.shape[1]
    ways = ways_of(n_dp)
    ff = w_gate.shape[1]
    order = jnp.bitwise_xor(jnp.array(width_order(n_dp), jnp.int32), ways * me_dp)
    row0 = (me_z * rows).reshape(1)
    own_positions = lax.dynamic_slice_in_dim(positions, me_z * rows, rows, 0)
    own_segs = lax.dynamic_slice_in_dim(segments, me_z * rows, rows, 0)

    if kv % LANES == 0:
        slots = [jnp.concatenate([w_key, w_value], axis=1)]
        for b in range(n_tensor.bit_length() - 1):
            slots += [swap(jnp.concatenate(slots, axis=0), TENSOR, n_tensor, b)]
            slots = [jnp.concatenate(slots, axis=0)]
        shard_rows = w_key.shape[0]
        slots = [slots[0][i * shard_rows : (i + 1) * shard_rows] for i in range(n_tensor)]
        kv_rows = unpack_kv(me_z.reshape(1), slots, kv)
    else:
        kv_rows = jnp.concatenate([over_tensor(w_key, 1), over_tensor(w_value, 1)], axis=1)
    kv_pieces = dp_gather(kv_rows, n_dp)
    q_rows, out_rows = unpack_pair(over_tensor(jnp.concatenate([w_query, w_out.T], axis=1)), n_tensor)
    q_pieces = dp_gather(q_rows, n_dp)
    out_pieces = dp_gather(out_rows, n_dp)
    gu_pieces = dp_gather(jnp.concatenate([w_gate, w_up], axis=1), n_dp)
    down_pieces = dp_gather(w_down.T, n_dp)

    gains = jnp.concatenate([norm_attn[None], norm_mlp[None], jnp.zeros((6, width), f32)], axis=0)
    tokens_here, cot_here, gains_here = reorder(order, (tokens, cotangent, gains), False)
    gain_attn, gain_mlp = gains_here[:1], gains_here[1:2]
    chunk = rows // 2
    chunks = [slice(i * chunk, (i + 1) * chunk) for i in range(2)]
    below, above = [cot_here], [cot_here]
    for r in range(1, n_tensor):
        below.append(lax.ppermute(below[-1], TENSOR, [(i, i + 1) for i in range(r - 1, n_tensor - 1)]))
        above.append(lax.ppermute(above[-1], TENSOR, [(i + 1, i) for i in range(n_tensor - r)]))
    cots = below + above[1:]

    freq_index = jnp.arange(HD // 2, dtype=jnp.int32).astype(f32)
    inverse = jnp.exp(freq_index * (-2.0 * math.log(500000.0) / HD))
    angles = own_positions.astype(f32)[:, None] * inverse[None, :]
    cosine = jnp.tile(jnp.cos(angles), (1, LANES // (HD // 2)))
    sine = jnp.sin(angles)
    sine = jnp.tile(jnp.concatenate([-sine, sine], axis=1), (1, LANES // HD))

    inputs = tokens_here.astype(f32)
    scale_in = lax.rsqrt(jnp.mean(inputs * inputs, axis=-1, keepdims=True) + EPS)
    normed_local = (inputs * scale_in * gain_attn).astype(bf16)
    kv_all = over_tensor(proj_kv(normed_local, cosine, sine, kv_pieces))
    attended = ()
    for i in range(FWD_PARTS):
        attended = attn_forward(row0, own_segs[:, None], normed_local, kv_all, cosine, sine, q_pieces, i, attended)
    context, query, lse = attended
    middle, normed_mid_local = out_proj(context, tokens_here, gain_mlp, out_pieces)
    normed_mid = [over_tensor(normed_mid_local[c]) for c in chunks]
    hidden, mlp_grads, cot_all, d_normed_mid, mlp_branch = [], [], [], [], []
    for i in range(2):
        h, g, c = mlp(me_z.reshape(1), normed_mid[i], cots, i, gu_pieces, down_pieces)
        cot_all.append(c)
        hidden.append(h[None])
        mlp_grads.append(g)
        d_normed_mid.append(sum_tensor(back(g, gu_pieces)))
        mlp_branch.append(sum_tensor(back(h[None], down_pieces)))
    _, cuts = scatter_segments(n_dp)
    half = [WIDTH // 2]

    def scattered(lefts, rights):
        other = weight_grad(lefts, rights, 1, None, half)[0]
        got = swap(other, DP, n_dp, 0)
        return dp_scatter(weight_grad(lefts, rights, 0, got, cuts), n_dp)

    down_parts = scattered(cot_all, hidden)
    gu_parts = scattered(normed_mid, mlp_grads)

    d_middle, d_branch, mlp_gain_part = mid_back(d_normed_mid, middle, gain_mlp, cot_here)
    dq, dk, dv, d_normed_part = attn_backward(
        row0, own_segs[None, :], query, kv_all, d_branch, context, lse, cosine, sine, q_pieces, out_pieces
    )
    out_parts = scattered([d_branch], [context[None]])
    d_kv = sum_tensor(jnp.concatenate([dk, dv], axis=1))
    query_parts = scattered([normed_local], [dq[None]])
    d_kv = rope_kv_back(d_kv, cosine, sine)
    kv_parts = scattered([normed_local], [d_kv[None]])
    input_grad, gain_parts = in_back(
        order, d_kv, d_normed_part, tokens_here, gain_attn, d_middle, mlp_gain_part, kv_pieces
    )

    grad_down = finish(down_parts, 0, ff, ways, True)
    grad_gate = finish(gu_parts, 0, ff, ways, False)
    grad_up = finish(gu_parts, ff, ff, ways, False)
    shard_rows = WIDTH // n_dp
    packed_qo = pack([query_parts, out_parts], [[(0, q, 0)], [(q, q, 0)]], n_tensor, ways, 2 * q, shard_rows)
    packed_qo = sum_tensor(packed_qo).astype(f32)
    grad_query, grad_output = packed_qo[:, :q], packed_qo[:, q:].T
    packed_kv = pack([kv_parts], [[(0, kv, 0), (kv, kv, kv * n_tensor)]], n_tensor, ways, 2 * kv, shard_rows)
    packed_kv = sum_tensor(packed_kv).astype(f32)
    grad_key, grad_value = packed_kv[:, :kv], packed_kv[:, kv:]

    def sum_all(x):
        for b in range(n_tensor.bit_length() - 1):
            x = x + swap(x, TENSOR, n_tensor, b)
        for b in range(n_dp.bit_length() - 1):
            x = x + swap(x, DP, n_dp, b)
        return x

    layer_out = (middle + jnp.concatenate(mlp_branch, axis=0).astype(f32)).astype(bf16)
    layer_out = reorder(order, (layer_out,), True)[0]
    gain_grads = sum_all(gain_parts)
    return (
        layer_out, input_grad, gain_grads[0], grad_query, grad_key, grad_value, grad_output,
        gain_grads[1], grad_gate, grad_up, grad_down,
    )


def solution(mesh):
    sizes = dict(mesh.shape)
    in_specs = (
        P((DP, TENSOR), None),
        P(DP),
        P(DP),
        P(),
        P(DP, TENSOR),
        P(DP, TENSOR),
        P(DP, TENSOR),
        P(TENSOR, DP),
        P(),
        P(DP, TENSOR),
        P(DP, TENSOR),
        P(TENSOR, DP),
        P((DP, TENSOR), None),
    )
    out_specs = (
        P((DP, TENSOR), None),
        P((DP, TENSOR), None),
        P(),
        P(DP, TENSOR),
        P(DP, TENSOR),
        P(DP, TENSOR),
        P(TENSOR, DP),
        P(),
        P(DP, TENSOR),
        P(DP, TENSOR),
        P(TENSOR, DP),
    )
    body = partial(layer, n_dp=sizes[DP], n_tensor=sizes[TENSOR])
    return jax.shard_map(body, mesh=mesh, in_specs=in_specs, out_specs=out_specs, check_vma=False)
```

time: 1360 us -> 887 us (0.65)
  waiting for transfers between devices: 874 us -> 416 us
  Pallas kernels: 0 us -> 321 us
  matrix products: 253 us -> 0 us
  starting transfers between devices: 1.21 us -> 84.1 us
  blocking collectives: 67 us -> 0 us
  other arithmetic: 68.7 us -> 14.7 us
  local copies, waits for them, and re-layouts: 65 us -> 30 us
    all_gather x9 -> x4, waiting for transfers between devices: 420 us -> 0.06 us  [over_tensor(): return lax.all_gather(x, TENSOR, axis=axis, tiled=True)]
    reduce_scatter x11 -> x7, waiting for transfers between devices: 450 us -> 51.9 us  [sum_tensor(): return lax.psum_scatter(x, TENSOR, scatter_dimension=0, tiled=True)]
    ppermute x0 -> x103, waiting for transfers between devices: none -> 364 us  [the longest x97 273 us: swap(): return lax.ppermute(x, axis, [(i, i ^ 1 << b) for i in range(n)])]
    pallas_call x0 -> x38, Pallas kernels: none -> 321 us  [the longest x10 79.2 us: weight_grad(): pl.pallas_call(partial(grad_kernel, chunks=chunks, received=len(extra), c...]
    dot_general x35 -> x0, matrix products: 253 us -> none  [the longest x2 22.1 us: backward_block(): jnp.einsum('qhgd,khd->hgqk', d_rows, near_values, preferred_element_type=...]
    ppermute x0 -> x103, starting transfers between devices: none -> 82.7 us  [the longest x97 71.9 us: swap(): return lax.ppermute(x, axis, [(i, i ^ 1 << b) for i in range(n)])]
    psum x1 -> x0, blocking collectives: 45.8 us -> none  [local(): lax.psum((attn_gain_part, mlp_gain_part), ('dp', 'tensor'))]
    dynamic_update_slice x8 -> x0, local copies, waits for them, and re-layouts: 43.6 us -> none  [the longest x4 41.5 us: local(): lax.scan(backward_block, (empty_grads, empty_grads), jnp.arange(block_cou...]
  transfers between devices with their start and end apart: 20 -> 114, of which waited for: 17 -> 42; matrix products, arithmetic and copies ran while one was open for 22% -> 3% of each run, Pallas kernels for 0% -> 31%
where the time goes in v1:
time: 887 us; the launch traced here: 880 us
  waiting for transfers between devices  416 us (47%)
  Pallas kernels  321 us (36%)
  starting transfers between devices  84.1 us (9%)
  local copies, waits for them, and re-layouts  30 us (3%)
  between operations  15.1 us (2%)
  other arithmetic  14.7 us (2%)
    ppermute x97, waiting for transfers between devices, swap(): return lax.ppermute(x, axis, [(i, i ^ 1 << b) for i in range(n)])  273 us
    ppermute x3, waiting for transfers between devices, layer(): lax.ppermute(above[-1], TENSOR, [(i + 1, i) for i in range(n_tensor - r)])  90.3 us
    pallas_call x10, Pallas kernels, weight_grad(): pl.pallas_call(partial(grad_kernel, chunks=chunks, received=len(extra), c...  79.2 us
    ppermute x97, starting transfers between devices, swap(): return lax.ppermute(x, axis, [(i, i ^ 1 << b) for i in range(n)])  71.9 us
    reduce_scatter x7, waiting for transfers between devices, sum_tensor(): return lax.psum_scatter(x, TENSOR, scatter_dimension=0, tiled=True)  51.9 us
    pallas_call x4, Pallas kernels, back(): pl.pallas_call(back_kernel, grid=(many * per,), in_specs=[pl.BlockSpec((1...  49.8 us
    pallas_call x2, Pallas kernels, mlp(): pl.pallas_call(partial(mlp_kernel, slots=slots, count=len(pieces)), grid=...  41.8 us
    pallas_call x1, Pallas kernels, attn_backward(): pl.pallas_call(partial(attn_bwd_kernel, count=len(q_pieces)), grid_spec=g...  38.7 us
  transfers between devices with their start and end apart: 114, of which 42 were waited for; matrix products, arithmetic and copies ran while one was open for 3% of the time, Pallas kernels for 31%

profile of v1, /device:TPU:0, one launch (start us, length us, event | category | flops | bytes accessed | tf_op | source)
XLA Modules:
  0.0 880.4 jit_solution(16320066478678609053)
XLA Ops:
  25.7 25.7 %collective-permute-done.1 = bf16[512,256]{1,0:T(8,128)(2,1)S(1)} collective-permute-done((bf16[512,256]{1,0:T(8,128)(2,1)S(1)}, bf16[512,256]{1,0:T(8,128)(2,1)S(1)}, u32[]{:S(2)}, u32[]{:S(2)}) %collective-permute-start.1) | collective-permute-done | bytes 262176 | tf_op jit(solution)/shard_map/ppermute | solution.py:61
  61.5 4.6 collective-permute-done.5.refs_4_
  82.3 5.6 pk.1
  97.7 10.0 %collective-permute-done.32.refs_5_.refs_19_ = bf16[128,2048]{1,0:T(8,128)(2,1)S(1)} collective-permute-done((bf16[128,2048]{1,0:T(8,128)(2,1)S(1)}, bf16[128,2048]{1,0:T(8,128)(2,1)S(1)}, u32[]{:S(2)}, u32[]{:S(2)}) %collective-permute-start.32) | collective-permute-done | bytes 524320 | tf_op jit(solution)/shard_map/ppermute | solution.py:61
  109.7 9.9 %collective-permute-done.29.refs_2_.refs_16_ = bf16[128,2048]{1,0:T(8,128)(2,1)} collective-permute-done((bf16[128,2048]{1,0:T(8,128)(2,1)S(1)}, bf16[128,2048]{1,0:T(8,128)(2,1)}, u32[]{:S(2)}, u32[]{:S(2)}) %collective-permute-start.29) | collective-permute-done | bytes 524320 | tf_op jit(solution)/shard_map/ppermute | solution.py:61
  121.0 9.1 %collective-permute-done.19.refs_5_ = bf16[128,2048]{1,0:T(8,128)(2,1)S(1)} collective-permute-done((bf16[128,2048]{1,0:T(8,128)(2,1)S(1)}, bf16[128,2048]{1,0:T(8,128)(2,1)S(1)}, u32[]{:S(2)}, u32[]{:S(2)}) %collective-permute-start.19) | collective-permute-done | bytes 524320 | tf_op jit(solution)/shard_map/ppermute | solution.py:61
  132.1 8.5 collective-permute-done.16.refs_2_
  142.7 8.9 %collective-permute-done.33.refs_6_.refs_20_ = bf16[128,2048]{1,0:T(8,128)(2,1)S(1)} collective-permute-done((bf16[128,2048]{1,0:T(8,128)(2,1)S(1)}, bf16[128,2048]{1,0:T(8,128)(2,1)S(1)}, u32[]{:S(2)}, u32[]{:S(2)}) %collective-permute-start.33) | collective-permute-done | bytes 524320 | tf_op jit(solution)/shard_map/ppermute | solution.py:61
  154.5 10.1 %collective-permute-done.20.refs_6_ = bf16[128,2048]{1,0:T(8,128)(2,1)} collective-permute-done((bf16[128,2048]{1,0:T(8,128)(2,1)S(1)}, bf16[128,2048]{1,0:T(8,128)(2,1)}, u32[]{:S(2)}, u32[]{:S(2)}) %collective-permute-start.20) | collective-permute-done | bytes 524320 | tf_op jit(solution)/shard_map/ppermute | solution.py:61
  169.5 15.8 %shard_map.222 = (bf16[256,2048]{1,0:T(8,128)(2,1)}, bf16[256,2048]{1,0:T(8,128)(2,1)}, f32[256,1024]{1,0:T(8,128)}) custom-call(s32[1]{0:T(128)} %bitcast.row0_ref, s32[256,1]{1,0:T(8,128)} %copy.37.seg_ref, bf16[256,2048]{1,0:T(8,128)(2,1)} %fusion.2.x_ref.refs_0_, bf16[1024,1024]{1,0:T(8,128)(2,1)} %all-gather.5.cloned.1.call-done.k_ref.v_ref, ...), custom_call_target="tpu_custom_call" | custom-call | flops 4294967296 | bytes 12582912 | tf_op jit(solution)/shard_map/pallas_call | solution.py:402
  187.4 15.8 %shard_map.223 = (bf16[256,2048]{1,0:T(8,128)(2,1)}, bf16[256,2048]{1,0:T(8,128)(2,1)}, f32[256,1024]{1,0:T(8,128)}) custom-call(s32[1]{0:T(128)} %bitcast.row0_ref, s32[256,1]{1,0:T(8,128)} %copy.37.seg_ref, bf16[256,2048]{1,0:T(8,128)(2,1)} %fusion.2.x_ref.refs_0_, ...), custom_call_target="tpu_custom_call", output_to_operand_aliasing={{0}: (21, {}), {1}: (22, {}), {2}: (23, {})} | custom-call | flops 4294967296 | bytes 12582912 | tf_op jit(solution)/shard_map/pallas_call | solution.py:402
  204.0 8.3 op.1
  221.7 4.5 collective-permute-start.41
  227.8 4.5 collective-permute-done.62.refs_38_.refs_3_
  234.3 36.5 %collective-permute-done.44.refs_4_ = bf16[256,2048]{1,0:T(8,128)(2,1)} collective-permute-done((bf16[256,2048]{1,0:T(8,128)(2,1)}, bf16[256,2048]{1,0:T(8,128)(2,1)}, u32[]{:S(2)}, u32[]{:S(2)}) %collective-permute-start.44) | collective-permute-done | bytes 1048608 | tf_op jit(solution)/shard_map/ppermute | solution.py:800
  274.5 4.7 collective-permute-done.48.refs_9_.refs_23_.refs_2_
  279.2 14.6 %collective-permute-done.47.refs_8_.refs_22_.refs_1_ = bf16[128,4096]{1,0:T(8,128)(2,1)} collective-permute-done((bf16[128,4096]{1,0:T(8,128)(2,1)S(1)}, bf16[128,4096]{1,0:T(8,128)(2,1)}, u32[]{:S(2)}, u32[]{:S(2)}) %collective-permute-start.47) | collective-permute-done | bytes 1048608 | tf_op jit(solution)/shard_map/ppermute | solution.py:61
  297.6 11.3 %collective-permute-done.45.refs_5_ = bf16[256,2048]{1,0:T(8,128)(2,1)S(1)} collective-permute-done((bf16[256,2048]{1,0:T(8,128)(2,1)}, bf16[256,2048]{1,0:T(8,128)(2,1)S(1)}, u32[]{:S(2)}, u32[]{:S(2)}) %collective-permute-start.45) | collective-permute-done | bytes 1048608 | tf_op jit(solution)/shard_map/ppermute | solution.py:800
  311.4 22.9 %collective-permute-done.52.refs_13_.refs_27_.refs_6_ = bf16[128,4096]{1,0:T(8,128)(2,1)} collective-permute-done((bf16[128,4096]{1,0:T(8,128)(2,1)}, bf16[128,4096]{1,0:T(8,128)(2,1)}, u32[]{:S(2)}, u32[]{:S(2)}) %collective-permute-start.52) | collective-permute-done | bytes 1048608 | tf_op jit(solution)/shard_map/ppermute | solution.py:61
  337.7 42.4 %collective-permute-done.46.refs_6_ = bf16[256,2048]{1,0:T(8,128)(2,1)} collective-permute-done((bf16[256,2048]{1,0:T(8,128)(2,1)}, bf16[256,2048]{1,0:T(8,128)(2,1)}, u32[]{:S(2)}, u32[]{:S(2)}) %collective-permute-start.46) | collective-permute-done | bytes 1048608 | tf_op jit(solution)/shard_map/ppermute | solution.py:800
  380.2 20.8 %shard_map.226 = (bf16[512,2048]{1,0:T(8,128)(2,1)}, bf16[2,512,2048]{2,1,0:T(8,128)(2,1)}, bf16[512,2048]{1,0:T(8,128)(2,1)}) custom-call(s32[1]{0:T(128)} %bitcast.7.me_ref, bf16[512,2048]{1,0:T(8,128)(2,1)} %all-gather.11.cloned.1.call-done.x_ref.refs_1_, bf16[256,2048]{1,0:T(8,128)(2,1)} %get-tuple-element.79.refs_0_.cot_ref, ...), custom_call_target="tpu_custom_call" | custom-call | flops 12884901888 | bytes 41943040 | tf_op jit(solution)/shard_map/pallas_call | solution.py:653
  401.0 15.5 %shard_map.230 = bf16[512,2048]{1,0:T(8,128)(2,1)} custom-call(bf16[2,512,2048]{2,1,0:T(8,128)(2,1)} %get-tuple-element.84.x_ref.refs_3_, bf16[256,4096]{1,0:T(8,128)(2,1)} %copy-done, bf16[128,4096]{1,0:T(8,128)(2,1)} %collective-permute-done.47.refs_8_.refs_22_.refs_1_, bf16[128,4096]{1,0:T(8,128)(2,1)} %copy-done.6, ...), custom_call_target="tpu_custom_call" | custom-call | flops 8589934592 | bytes 25165824 | tf_op jit(solution)/shard_map/pallas_call | solution.py:694
  416.6 21.0 %shard_map.224 = (bf16[512,2048]{1,0:T(8,128)(2,1)}, bf16[2,512,2048]{2,1,0:T(8,128)(2,1)}, bf16[512,2048]{1,0:T(8,128)(2,1)}) custom-call(s32[1]{0:T(128)} %bitcast.7.me_ref, bf16[512,2048]{1,0:T(8,128)(2,1)} %all-gather.9.cloned.1.call-done.x_ref.refs_0_, bf16[256,2048]{1,0:T(8,128)(2,1)} %get-tuple-element.79.refs_0_.cot_ref, ...), custom_call_target="tpu_custom_call" | custom-call | flops 12884901888 | bytes 41943040 | tf_op jit(solution)/shard_map/pallas_call | solution.py:653
  437.6 15.2 %shard_map.229 = bf16[512,2048]{1,0:T(8,128)(2,1)} custom-call(bf16[2,512,2048]{2,1,0:T(8,128)(2,1)} %get-tuple-element.83.x_ref.refs_2_, bf16[256,4096]{1,0:T(8,128)(2,1)} %copy-done, bf16[128,4096]{1,0:T(8,128)(2,1)} %collective-permute-done.47.refs_8_.refs_22_.refs_1_, bf16[128,4096]{1,0:T(8,128)(2,1)} %copy-done.6, ...), custom_call_target="tpu_custom_call" | custom-call | flops 8589934592 | bytes 25165824 | tf_op jit(solution)/shard_map/pallas_call | solution.py:694
  453.4 6.9 reduce-scatter.14.cloned.1.call-done.refs_1_
  460.3 45.0 %reduce-scatter.12.cloned.1.call-done.refs_0_ = bf16[128,2048]{1,0:T(8,128)(2,1)} async-done(((bf16[512,2048]{1,0:T(8,128)(2,1)}), bf16[128,2048]{1,0:T(8,128)(2,1)}) %reduce-scatter.12.cloned.1.call-update) | async-done | bytes 524304 | tf_op jit(solution)/shard_map/reduce_scatter | solution.py:757
  505.3 5.2 mb.1
  510.5 38.7 %ab.1 = (bf16[256,2048]{1,0:T(8,128)(2,1)}, bf16[1024,512]{1,0:T(8,128)(2,1)}, bf16[1024,512]{1,0:T(8,128)(2,1)}, f32[256,2048]{1,0:T(8,128)}) custom-call(s32[1]{0:T(128)} %bitcast.row0_ref, s32[1,256]{1,0:T(1,128)} %bitcast.41, bf16[256,2048]{1,0:T(8,128)(2,1)} %get-tuple-element.82.q_ref, bf16[1024,1024]{1,0:T(8,128)(2,1)} %all-gather.5.cloned.1.call-done.k_ref.v_ref, ...), custom_call_target="tpu_custom_call" | custom-call | flops 15032385536 | bytes 29360128 | tf_op jit(solution)/shard_map/ab/pallas_call | solution.py:563
  552.5 9.5 %shard_map.227 = bf16[512,2048]{1,0:T(8,128)(2,1)} custom-call(bf16[1,512,2048]{2,1,0:T(8,128)(2,1)} %bitcast.42, bf16[256,2048]{1,0:T(8,128)(2,1)} %bitcast.26, bf16[128,2048]{1,0:T(8,128)(2,1)} %copy-done.24, bf16[128,2048]{1,0:T(8,128)(2,1)} %copy-done.23, bf16[128,2048]{1,0:T(8,128)(2,1)} %copy-done.26, ...), custom_call_target="tpu_custom_call" | custom-call | flops 4294967296 | bytes 12582912 | tf_op jit(solution)/shard_map/pallas_call | solution.py:694
  562.3 14.9 %shard_map.242 = bf16[1024,4096]{1,0:T(8,128)(2,1)} custom-call(bf16[512,2048]{1,0:T(8,128)(2,1)} %all-gather.9.cloned.1.call-done.x_ref.refs_0_, bf16[512,2048]{1,0:T(8,128)(2,1)} %all-gather.11.cloned.1.call-done.x_ref.refs_1_, bf16[2,512,2048]{2,1,0:T(8,128)(2,1)} %get-tuple-element.83.x_ref.refs_2_, bf16[2,512,2048]{2,1,0:T(8,128)(2,1)} %get-tuple-element.84.x_ref.refs_3_), custom_call_target="tpu_custom_call" | custom-call | flops 8589934592 | bytes 33554432 | tf_op jit(solution)/shard_map/pallas_call | solution.py:738
  577.2 5.3 shard_map.234
  583.0 5.1 shard_map.231
  588.2 9.5 %shard_map.225 = bf16[512,2048]{1,0:T(8,128)(2,1)} custom-call(bf16[1,512,2048]{2,1,0:T(8,128)(2,1)} %bitcast.45, bf16[256,2048]{1,0:T(8,128)(2,1)} %bitcast.27, bf16[128,2048]{1,0:T(8,128)(2,1)} %copy-done.24, bf16[128,2048]{1,0:T(8,128)(2,1)} %copy-done.23, bf16[128,2048]{1,0:T(8,128)(2,1)} %copy-done.26, ...), custom_call_target="tpu_custom_call" | custom-call | flops 4294967296 | bytes 12582912 | tf_op jit(solution)/shard_map/pallas_call | solution.py:694
  603.8 9.0 %shard_map.247 = bf16[1024,2048]{1,0:T(8,128)(2,1)} custom-call(bf16[512,2048]{1,0:T(8,128)(2,1)} %get-tuple-element.119.refs_0_, bf16[512,2048]{1,0:T(8,128)(2,1)} %get-tuple-element.120.refs_1_, bf16[1,512,2048]{2,1,0:T(8,128)(2,1)} %bitcast.46, bf16[1,512,2048]{2,1,0:T(8,128)(2,1)} %bitcast.43), custom_call_target="tpu_custom_call" | custom-call | flops 4294967296 | bytes 16777216 | tf_op jit(solution)/shard_map/pallas_call | solution.py:738
  619.2 6.0 shard_map.235
  627.3 5.4 collective-permute-done.89.refs_1_
  634.2 6.0 shard_map.232
  640.2 21.9 %collective-permute-done.90.refs_3_ = bf16[256,1024]{1,0:T(8,128)(2,1)S(1)} collective-permute-done((bf16[256,1024]{1,0:T(8,128)(2,1)S(1)}, bf16[256,1024]{1,0:T(8,128)(2,1)S(1)}, u32[]{:S(2)}, u32[]{:S(2)}) %collective-permute-start.90) | collective-permute-done | bytes 524320 | tf_op jit(solution)/shard_map/ppermute | solution.py:61
  668.2 27.5 %collective-permute-done.91.refs_2_ = bf16[128,1024]{1,0:T(8,128)(2,1)S(1)} collective-permute-done((bf16[128,1024]{1,0:T(8,128)(2,1)}, bf16[128,1024]{1,0:T(8,128)(2,1)S(1)}, u32[]{:S(2)}, u32[]{:S(2)}) %collective-permute-start.91) | collective-permute-done | bytes 262176 | tf_op jit(solution)/shard_map/ppermute | solution.py:61
  729.1 5.7 shard_map.237
  734.9 16.4 %shard_map.243 = (bf16[384,4096]{1,0:T(8,128)(2,1)}, bf16[256,4096]{1,0:T(8,128)(2,1)}, bf16[128,4096]{1,0:T(8,128)(2,1)}, bf16[256,4096]{1,0:T(8,128)(2,1)}) custom-call(bf16[512,2048]{1,0:T(8,128)(2,1)} %all-gather.9.cloned.1.call-done.x_ref.refs_0_, bf16[512,2048]{1,0:T(8,128)(2,1)} %all-gather.11.cloned.1.call-done.x_ref.refs_1_, ...), custom_call_target="tpu_custom_call" | custom-call | flops 8589934592 | bytes 33554432 | tf_op jit(solution)/shard_map/pallas_call | solution.py:738
  753.8 9.7 %shard_map.248 = (bf16[384,2048]{1,0:T(8,128)(2,1)}, bf16[256,2048]{1,0:T(8,128)(2,1)}, bf16[128,2048]{1,0:T(8,128)(2,1)}, bf16[256,2048]{1,0:T(8,128)(2,1)}) custom-call(bf16[512,2048]{1,0:T(8,128)(2,1)} %get-tuple-element.119.refs_0_, bf16[512,2048]{1,0:T(8,128)(2,1)} %get-tuple-element.120.refs_1_, bf16[1,512,2048]{2,1,0:T(8,128)(2,1)} %bitcast.47, ...), custom_call_target="tpu_custom_call" | custom-call | flops 4294967296 | bytes 16777216 | tf_op jit(solution)/shard_map/pallas_call | solution.py:738
  765.1 9.3 %ib.1 = (f32[256,2048]{1,0:T(8,128)}, f32[8,2048]{1,0:T(8,128)}) custom-call(s32[16]{0:T(128)} %broadcast_xor_fusion.order_ref, bf16[256,1024]{1,0:T(8,128)(2,1)} %rk.1.dkv_ref, f32[256,2048]{1,0:T(8,128)} %get-tuple-element.89.part_ref, bf16[256,2048]{1,0:T(8,128)(2,1)} %get-tuple-element.69.tok_ref, f32[1,2048]{1,0:T(1,128)} %copy-done.67, ...), custom_call_target="tpu_custom_call" | custom-call | flops 1073741824 | bytes 16777216 | tf_op jit(solution)/shard_map/ib/pallas_call | solution.py:607
  785.8 14.2 %collective-permute-done.94.refs_1_ = bf16[256,4096]{1,0:T(8,128)(2,1)S(1)} collective-permute-done((bf16[256,4096]{1,0:T(8,128)(2,1)}, bf16[256,4096]{1,0:T(8,128)(2,1)S(1)}, u32[]{:S(2)}, u32[]{:S(2)}) %collective-permute-start.94) | collective-permute-done | bytes 2097184 | tf_op jit(solution)/shard_map/ppermute | solution.py:61
  803.0 5.1 shard_map.244
  810.8 11.7 %collective-permute-done.99.refs_1_ = bf16[256,2048]{1,0:T(8,128)(2,1)S(1)} collective-permute-done((bf16[256,2048]{1,0:T(8,128)(2,1)}, bf16[256,2048]{1,0:T(8,128)(2,1)S(1)}, u32[]{:S(2)}, u32[]{:S(2)}) %collective-permute-start.99) | collective-permute-done | bytes 1048608 | tf_op jit(solution)/shard_map/ppermute | solution.py:61
  829.2 18.8 %collective-permute-done.76 = f32[8,2048]{1,0:T(8,128)S(1)} collective-permute-done((f32[8,2048]{1,0:T(8,128)S(1)}, f32[8,2048]{1,0:T(8,128)S(1)}, u32[]{:S(2)}, u32[]{:S(2)}) %collective-permute-start.76) | collective-permute-done | bytes 65568 | tf_op jit(solution)/shard_map/ppermute | solution.py:61
  855.8 4.3 shard_map.250
  (425 shorter events, 207.6 us)
Async XLA Ops:
  7.2 80.9 %all-gather.7.cloned.1.call-start = ((), (), s32[]{:S(2)}) async-start(), calls=%async_computation.8 | async-start | bytes 2621440 | tf_op jit(solution)/shard_map/all_gather | solution.py:753
  15.0 154.4 %all-gather.5.cloned.1.call-start = ((), (), s32[]{:S(2)}) async-start(), calls=%async_computation.7 | async-start | bytes 2621440 | tf_op jit(solution)/shard_map/all_gather | solution.py:753
  21.5 29.9 %collective-permute-start.1 = (bf16[512,256]{1,0:T(8,128)(2,1)S(1)}, bf16[512,256]{1,0:T(8,128)(2,1)S(1)}, u32[]{:S(2)}, u32[]{:S(2)}) collective-permute-start(bf16[512,256]{1,0:T(8,128)(2,1)S(1)} %pad_maximum_fusion.2), channel_id=1, source_target_pairs={{0,2},{1,3},{2,0},{3,1},{4,6},{5,7},{6,4},{7,5},{8,10},{9,11},{10,... | collective-permute-start | bytes 786440 | tf_op jit(solution)/shard_map/ppermute | solution.py:61
  87.9 292.3 %all-gather.11.cloned.1.call-start = ((), (), s32[]{:S(2)}) async-start(), calls=%async_computation.11 | async-start | bytes 2621440 | tf_op jit(solution)/shard_map/all_gather | solution.py:753
  97.1 33.0 %collective-permute-start.19 = (bf16[128,2048]{1,0:T(8,128)(2,1)S(1)}, bf16[128,2048]{1,0:T(8,128)(2,1)S(1)}, u32[]{:S(2)}, u32[]{:S(2)}) collective-permute-start(bf16[128,2048]{1,0:T(8,128)(2,1)S(1)} %get-tuple-element.157), channel_id=1, source_target_pairs={{0,8},{4,12},{8,0},{12,4},{16,24},{20,28},{24,16},{28,20},{1,9},{5... | collective-permute-start | bytes 1572872 | tf_op jit(solution)/shard_map/ppermute | solution.py:61
  108.3 32.3 %collective-permute-start.16 = (bf16[128,2048]{1,0:T(8,128)(2,1)S(1)}, bf16[128,2048]{1,0:T(8,128)(2,1)S(1)}, u32[]{:S(2)}, u32[]{:S(2)}) collective-permute-start(bf16[128,2048]{1,0:T(8,128)(2,1)S(1)} %get-tuple-element.158), channel_id=1, source_target_pairs={{0,16},{4,20},{8,24},{12,28},{16,0},{20,4},{24,8},{28,12},{1,17},{... | collective-permute-start | bytes 1572872 | tf_op jit(solution)/shard_map/ppermute | solution.py:61
  165.6 37.6 %collective-permute-start.34 = (bf16[256,2048]{1,0:T(8,128)(2,1)}, bf16[256,2048]{1,0:T(8,128)(2,1)}, u32[]{:S(2)}, u32[]{:S(2)}) collective-permute-start(bf16[256,2048]{1,0:T(8,128)(2,1)} %get-tuple-element.76.refs_0_.refs_14_), channel_id=1, source_target_pairs={{0,4},{4,0},{8,12},{12,8},{16,20},{20,16},{24,28},{28,24},{1,5},{5... | collective-permute-start | bytes 3145736 | tf_op jit(solution)/shard_map/ppermute | solution.py:61
  168.9 34.4 %collective-permute-start.40 = (bf16[128,2048]{1,0:T(8,128)(2,1)}, bf16[128,2048]{1,0:T(8,128)(2,1)}, u32[]{:S(2)}, u32[]{:S(2)}) collective-permute-start(bf16[128,2048]{1,0:T(8,128)(2,1)} %copy-done.51), channel_id=1, source_target_pairs={{0,4},{4,0},{8,12},{12,8},{16,20},{20,16},{24,28},{28,24},{1,5},{5... | collective-permute-start | bytes 1572872 | tf_op jit(solution)/shard_map/ppermute | solution.py:61
  169.3 34.6 %collective-permute-start.37 = (bf16[128,2048]{1,0:T(8,128)(2,1)}, bf16[128,2048]{1,0:T(8,128)(2,1)}, u32[]{:S(2)}, u32[]{:S(2)}) collective-permute-start(bf16[128,2048]{1,0:T(8,128)(2,1)} %copy-done.52), channel_id=1, source_target_pairs={{0,4},{4,0},{8,12},{12,8},{16,20},{20,16},{24,28},{28,24},{1,5},{5... | collective-permute-start | bytes 1572872 | tf_op jit(solution)/shard_map/ppermute | solution.py:61
  185.9 27.3 %collective-permute-start.60 = (bf16[128,2048]{1,0:T(8,128)(2,1)S(1)}, bf16[128,2048]{1,0:T(8,128)(2,1)S(1)}, u32[]{:S(2)}, u32[]{:S(2)}) collective-permute-start(bf16[128,2048]{1,0:T(8,128)(2,1)S(1)} %copy-done.61), channel_id=1, source_target_pairs={{0,8},{4,12},{8,0},{12,4},{16,24},{20,28},{24,16},{28,20},{1,9},{5... | collective-permute-start | bytes 1572872 | tf_op jit(solution)/shard_map/ppermute | solution.py:61
  214.0 56.8 %collective-permute-start.44 = (bf16[256,2048]{1,0:T(8,128)(2,1)}, bf16[256,2048]{1,0:T(8,128)(2,1)}, u32[]{:S(2)}, u32[]{:S(2)}) collective-permute-start(bf16[256,2048]{1,0:T(8,128)(2,1)} %get-tuple-element.79.refs_0_.cot_ref), channel_id=1, source_target_pairs={{1,0},{2,1},{3,2},{5,4},{6,5},{7,6},{9,8},{10,9},{11,10},{13,12},{... | collective-permute-start | bytes 3145736 | tf_op jit(solution)/shard_map/ppermute | solution.py:800
  217.6 199.0 %all-gather.9.cloned.1.call-start = ((), (), s32[]{:S(2)}) async-start(), calls=%async_computation.9 | async-start | bytes 2621440 | tf_op jit(solution)/shard_map/all_gather | solution.py:753
  221.7 50.7 %collective-permute-start.41 = (bf16[256,2048]{1,0:T(8,128)(2,1)}, bf16[256,2048]{1,0:T(8,128)(2,1)S(1)}, u32[]{:S(2)}, u32[]{:S(2)}) collective-permute-start(bf16[256,2048]{1,0:T(8,128)(2,1)} %get-tuple-element.79.refs_0_.cot_ref), channel_id=1, source_target_pairs={{0,1},{1,2},{2,3},{4,5},{5,6},{6,7},{8,9},{9,10},{10,11},{12,13},{... | collective-permute-start | bytes 3145736 | tf_op jit(solution)/shard_map/ppermute | solution.py:799
  226.2 46.2 %collective-permute-start.51 = (bf16[128,4096]{1,0:T(8,128)(2,1)S(1)}, bf16[128,4096]{1,0:T(8,128)(2,1)S(1)}, u32[]{:S(2)}, u32[]{:S(2)}) collective-permute-start(bf16[128,4096]{1,0:T(8,128)(2,1)S(1)} %get-tuple-element.149), channel_id=1, source_target_pairs={{0,8},{4,12},{8,0},{12,4},{16,24},{20,28},{24,16},{28,20},{1,9},{5... | collective-permute-start | bytes 3145736 | tf_op jit(solution)/shard_map/ppermute | solution.py:61
  232.3 41.4 %collective-permute-start.50 = (bf16[128,4096]{1,0:T(8,128)(2,1)S(1)}, bf16[128,4096]{1,0:T(8,128)(2,1)}, u32[]{:S(2)}, u32[]{:S(2)}) collective-permute-start(bf16[128,4096]{1,0:T(8,128)(2,1)S(1)} %get-tuple-element.149), channel_id=1, source_target_pairs={{0,16},{4,20},{8,24},{12,28},{16,0},{20,4},{24,8},{28,12},{1,17},{... | collective-permute-start | bytes 3145736 | tf_op jit(solution)/shard_map/ppermute | solution.py:61
  233.7 45.5 %collective-permute-start.48 = (bf16[128,4096]{1,0:T(8,128)(2,1)S(1)}, bf16[128,4096]{1,0:T(8,128)(2,1)S(1)}, u32[]{:S(2)}, u32[]{:S(2)}) collective-permute-start(bf16[128,4096]{1,0:T(8,128)(2,1)S(1)} %get-tuple-element.150), channel_id=1, source_target_pairs={{0,16},{4,20},{8,24},{12,28},{16,0},{20,4},{24,8},{28,12},{1,17},{... | collective-permute-start | bytes 3145736 | tf_op jit(solution)/shard_map/ppermute | solution.py:61
  272.4 36.5 %collective-permute-start.45 = (bf16[256,2048]{1,0:T(8,128)(2,1)}, bf16[256,2048]{1,0:T(8,128)(2,1)S(1)}, u32[]{:S(2)}, u32[]{:S(2)}) collective-permute-start(bf16[256,2048]{1,0:T(8,128)(2,1)} %collective-permute-done.44.refs_4_), channel_id=1, source_target_pairs={{1,0},{2,1},{5,4},{6,5},{9,8},{10,9},{13,12},{14,13},{17,16},{18,1... | collective-permute-start | bytes 3145736 | tf_op jit(solution)/shard_map/ppermute | solution.py:800
  273.7 35.4 %collective-permute-start.42 = (bf16[256,2048]{1,0:T(8,128)(2,1)S(1)}, bf16[256,2048]{1,0:T(8,128)(2,1)S(1)}, u32[]{:S(2)}, u32[]{:S(2)}) collective-permute-start(bf16[256,2048]{1,0:T(8,128)(2,1)S(1)} %collective-permute-done.41.refs_1_), channel_id=1, source_target_pairs={{1,2},{2,3},{5,6},{6,7},{9,10},{10,11},{13,14},{14,15},{17,18},{18... | collective-permute-start | bytes 3145736 | tf_op jit(solution)/shard_map/ppermute | solution.py:799
  279.2 29.9 %collective-permute-start.58 = (bf16[128,4096]{1,0:T(8,128)(2,1)S(1)}, bf16[128,4096]{1,0:T(8,128)(2,1)S(1)}, u32[]{:S(2)}, u32[]{:S(2)}) collective-permute-start(bf16[128,4096]{1,0:T(8,128)(2,1)S(1)} %collective-permute-done.51.refs_12_.refs_26_.refs_5_), channel_id=1, source_target_pairs={{0,4},{4,0},{8,12},{12,8},{16,20},{20,16},{24,28},{28,24},{1,5},{5... | collective-permute-start | bytes 3145736 | tf_op jit(solution)/shard_map/ppermute | solution.py:61
  297.5 40.3 %collective-permute-start.53 = (bf16[256,4096]{1,0:T(8,128)(2,1)S(1)}, bf16[256,4096]{1,0:T(8,128)(2,1)}, u32[]{:S(2)}, u32[]{:S(2)}) collective-permute-start(bf16[256,4096]{1,0:T(8,128)(2,1)S(1)} %constant_dynamic-update-slice_fusion.2.refs_7_.refs_21_.refs_0_), channel_id=1, source_target_pairs={{0,4},{4,0},{8,12},{12,8},{16,20},{20,16},{24,28},{28,24},{1,5},{5... | collective-permute-start | bytes 6291464 | tf_op jit(solution)/shard_map/ppermute | solution.py:61
  311.3 149.0 %reduce-scatter.14.cloned.1.call-start = ((), (), s32[]{:S(2)}) async-start(), calls=%async_computation.14 | async-start | bytes 2621440 | tf_op jit(solution)/shard_map/reduce_scatter | solution.py:757
  334.2 45.9 %collective-permute-start.46 = (bf16[256,2048]{1,0:T(8,128)(2,1)}, bf16[256,2048]{1,0:T(8,128)(2,1)}, u32[]{:S(2)}, u32[]{:S(2)}) collective-permute-start(bf16[256,2048]{1,0:T(8,128)(2,1)} %copy-done.16), channel_id=1, source_target_pairs={{1,0},{5,4},{9,8},{13,12},{17,16},{21,20},{25,24},{29,28}} | collective-permute-start | bytes 3145736 | tf_op jit(solution)/shard_map/ppermute | solution.py:800
  335.5 44.6 %collective-permute-start.43 = (bf16[256,2048]{1,0:T(8,128)(2,1)}, bf16[256,2048]{1,0:T(8,128)(2,1)}, u32[]{:S(2)}, u32[]{:S(2)}) collective-permute-start(bf16[256,2048]{1,0:T(8,128)(2,1)} %copy-done.17), channel_id=1, source_target_pairs={{2,3},{6,7},{10,11},{14,15},{18,19},{22,23},{26,27},{30,31}} | collective-permute-start | bytes 3145736 | tf_op jit(solution)/shard_map/ppermute | solution.py:799
  337.2 42.9 %collective-permute-start.59 = (bf16[128,4096]{1,0:T(8,128)(2,1)}, bf16[128,4096]{1,0:T(8,128)(2,1)}, u32[]{:S(2)}, u32[]{:S(2)}) collective-permute-start(bf16[128,4096]{1,0:T(8,128)(2,1)} %collective-permute-done.52.refs_13_.refs_27_.refs_6_), channel_id=1, source_target_pairs={{0,4},{4,0},{8,12},{12,8},{16,20},{20,16},{24,28},{28,24},{1,5},{5... | collective-permute-start | bytes 3145736 | tf_op jit(solution)/shard_map/ppermute | solution.py:61
  337.2 42.9 %collective-permute-start.56 = (bf16[128,4096]{1,0:T(8,128)(2,1)}, bf16[128,4096]{1,0:T(8,128)(2,1)}, u32[]{:S(2)}, u32[]{:S(2)}) collective-permute-start(bf16[128,4096]{1,0:T(8,128)(2,1)} %collective-permute-done.49.refs_10_.refs_24_.refs_3_), channel_id=1, source_target_pairs={{0,4},{4,0},{8,12},{12,8},{16,20},{20,16},{24,28},{28,24},{1,5},{5... | collective-permute-start | bytes 3145736 | tf_op jit(solution)/shard_map/ppermute | solution.py:61
  416.6 88.7 %reduce-scatter.12.cloned.1.call-start = ((), (), s32[]{:S(2)}) async-start(), calls=%async_computation.13 | async-start | bytes 2621440 | tf_op jit(solution)/shard_map/reduce_scatter | solution.py:757
  452.9 144.9 %reduce-scatter.16.cloned.1.call-start = ((), (), s32[]{:S(2)}) async-start(), calls=%async_computation.15 | async-start | bytes 2621440 | tf_op jit(solution)/shard_map/reduce_scatter | solution.py:757
  552.5 296.0 %reduce-scatter.10.cloned.1.call-start = ((), (), s32[]{:S(2)}) async-start(), calls=%async_computation.12 | async-start | bytes 2621440 | tf_op jit(solution)/shard_map/reduce_scatter | solution.py:757
  562.0 286.4 %reduce-scatter.8.cloned.1.call-start = ((), (), s32[]{:S(2)}) async-start(), calls=%async_computation.10 | async-start | bytes 2621440 | tf_op jit(solution)/shard_map/reduce_scatter | solution.py:757
  577.2 157.7 %collective-permute-start.93 = (bf16[1024,4096]{1,0:T(8,128)(2,1)}, bf16[1024,4096]{1,0:T(8,128)(2,1)}, u32[]{:S(2)}, u32[]{:S(2)}) collective-permute-start(bf16[1024,4096]{1,0:T(8,128)(2,1)} %shard_map.242), channel_id=1, source_target_pairs={{0,4},{4,0},{8,12},{12,8},{16,20},{20,16},{24,28},{28,24},{1,5},{5... | collective-permute-start | bytes 25165832 | tf_op jit(solution)/shard_map/ppermute | solution.py:61
  582.5 36.7 %collective-permute-start.83 = (bf16[1024,2048]{1,0:T(8,128)(2,1)}, bf16[1024,2048]{1,0:T(8,128)(2,1)}, u32[]{:S(2)}, u32[]{:S(2)}) collective-permute-start(bf16[1024,2048]{1,0:T(8,128)(2,1)} %shard_map.234), channel_id=1, source_target_pairs={{0,4},{4,0},{8,12},{12,8},{16,20},{20,16},{24,28},{28,24},{1,5},{5... | collective-permute-start | bytes 12582920 | tf_op jit(solution)/shard_map/ppermute | solution.py:61
  588.1 37.6 %collective-permute-start.78 = (bf16[1024,2048]{1,0:T(8,128)(2,1)}, bf16[1024,2048]{1,0:T(8,128)(2,1)}, u32[]{:S(2)}, u32[]{:S(2)}) collective-permute-start(bf16[1024,2048]{1,0:T(8,128)(2,1)} %shard_map.231), channel_id=1, source_target_pairs={{0,4},{4,0},{8,12},{12,8},{16,20},{20,16},{24,28},{28,24},{1,5},{5... | collective-permute-start | bytes 12582920 | tf_op jit(solution)/shard_map/ppermute | solution.py:61
  597.7 271.2 %reduce-scatter.20.cloned.1.call-start = ((), (), s32[]{:S(2)}) async-start(), calls=%async_computation.17 | async-start | bytes 655360 | tf_op jit(solution)/shard_map/reduce_scatter | solution.py:757
  612.8 141.0 %collective-permute-start.98 = (bf16[1024,2048]{1,0:T(8,128)(2,1)}, bf16[1024,2048]{1,0:T(8,128)(2,1)}, u32[]{:S(2)}, u32[]{:S(2)}) collective-permute-start(bf16[1024,2048]{1,0:T(8,128)(2,1)} %shard_map.247), channel_id=1, source_target_pairs={{0,4},{4,0},{8,12},{12,8},{16,20},{20,16},{24,28},{28,24},{1,5},{5... | collective-permute-start | bytes 12582920 | tf_op jit(solution)/shard_map/ppermute | solution.py:61
  625.2 40.8 %collective-permute-start.84 = (bf16[256,2048]{1,0:T(8,128)(2,1)}, bf16[256,2048]{1,0:T(8,128)(2,1)S(1)}, u32[]{:S(2)}, u32[]{:S(2)}) collective-permute-start(bf16[256,2048]{1,0:T(8,128)(2,1)} %get-tuple-element.102), channel_id=1, source_target_pairs={{0,16},{4,20},{8,24},{12,28},{16,0},{20,4},{24,8},{28,12},{1,17},{... | collective-permute-start | bytes 3145736 | tf_op jit(solution)/shard_map/ppermute | solution.py:61
  625.8 41.8 %collective-permute-start.85 = (bf16[256,2048]{1,0:T(8,128)(2,1)}, bf16[256,2048]{1,0:T(8,128)(2,1)S(1)}, u32[]{:S(2)}, u32[]{:S(2)}) collective-permute-start(bf16[256,2048]{1,0:T(8,128)(2,1)} %get-tuple-element.104), channel_id=1, source_target_pairs={{0,8},{4,12},{8,0},{12,4},{16,24},{20,28},{24,16},{28,20},{1,9},{5... | collective-permute-start | bytes 3145736 | tf_op jit(solution)/shard_map/ppermute | solution.py:61
  632.7 29.4 %collective-permute-start.90 = (bf16[256,1024]{1,0:T(8,128)(2,1)S(1)}, bf16[256,1024]{1,0:T(8,128)(2,1)S(1)}, u32[]{:S(2)}, u32[]{:S(2)}) collective-permute-start(bf16[256,1024]{1,0:T(8,128)(2,1)S(1)} %copy-done.73), channel_id=1, source_target_pairs={{0,8},{4,12},{8,0},{12,4},{16,24},{20,28},{24,16},{28,20},{1,9},{5... | collective-permute-start | bytes 1572872 | tf_op jit(solution)/shard_map/ppermute | solution.py:61
  662.2 44.5 %collective-permute-start.79 = (bf16[256,2048]{1,0:T(8,128)(2,1)}, bf16[256,2048]{1,0:T(8,128)(2,1)S(1)}, u32[]{:S(2)}, u32[]{:S(2)}) collective-permute-start(bf16[256,2048]{1,0:T(8,128)(2,1)} %get-tuple-element.96), channel_id=1, source_target_pairs={{0,16},{4,20},{8,24},{12,28},{16,0},{20,4},{24,8},{28,12},{1,17},{... | collective-permute-start | bytes 3145736 | tf_op jit(solution)/shard_map/ppermute | solution.py:61
  666.1 41.8 %collective-permute-start.80 = (bf16[256,2048]{1,0:T(8,128)(2,1)S(1)}, bf16[256,2048]{1,0:T(8,128)(2,1)}, u32[]{:S(2)}, u32[]{:S(2)}) collective-permute-start(bf16[256,2048]{1,0:T(8,128)(2,1)S(1)} %copy-done.71), channel_id=1, source_target_pairs={{0,8},{4,12},{8,0},{12,4},{16,24},{20,28},{24,16},{28,20},{1,9},{5... | collective-permute-start | bytes 3145736 | tf_op jit(solution)/shard_map/ppermute | solution.py:61
  667.6 28.1 %collective-permute-start.91 = (bf16[128,1024]{1,0:T(8,128)(2,1)}, bf16[128,1024]{1,0:T(8,128)(2,1)S(1)}, u32[]{:S(2)}, u32[]{:S(2)}) collective-permute-start(bf16[128,1024]{1,0:T(8,128)(2,1)} %get-tuple-element.111), channel_id=1, source_target_pairs={{0,8},{4,12},{8,0},{12,4},{16,24},{20,28},{24,16},{28,20},{1,9},{5... | collective-permute-start | bytes 786440 | tf_op jit(solution)/shard_map/ppermute | solution.py:61
  706.4 164.2 %reduce-scatter.18.cloned.1.call-start = ((), (), s32[]{:S(2)}) async-start(), calls=%async_computation.16 | async-start | bytes 2621440 | tf_op jit(solution)/shard_map/reduce_scatter | solution.py:757
  751.3 48.7 %collective-permute-start.94 = (bf16[256,4096]{1,0:T(8,128)(2,1)}, bf16[256,4096]{1,0:T(8,128)(2,1)S(1)}, u32[]{:S(2)}, u32[]{:S(2)}) collective-permute-start(bf16[256,4096]{1,0:T(8,128)(2,1)} %get-tuple-element.114), channel_id=1, source_target_pairs={{0,16},{4,20},{8,24},{12,28},{16,0},{20,4},{24,8},{28,12},{1,17},{... | collective-permute-start | bytes 6291464 | tf_op jit(solution)/shard_map/ppermute | solution.py:61
  752.9 48.7 %collective-permute-start.95 = (bf16[256,4096]{1,0:T(8,128)(2,1)}, bf16[256,4096]{1,0:T(8,128)(2,1)S(1)}, u32[]{:S(2)}, u32[]{:S(2)}) collective-permute-start(bf16[256,4096]{1,0:T(8,128)(2,1)} %get-tuple-element.116), channel_id=1, source_target_pairs={{0,8},{4,12},{8,0},{12,4},{16,24},{20,28},{24,16},{28,20},{1,9},{5... | collective-permute-start | bytes 6291464 | tf_op jit(solution)/shard_map/ppermute | solution.py:61
  763.5 59.0 %collective-permute-start.99 = (bf16[256,2048]{1,0:T(8,128)(2,1)}, bf16[256,2048]{1,0:T(8,128)(2,1)S(1)}, u32[]{:S(2)}, u32[]{:S(2)}) collective-permute-start(bf16[256,2048]{1,0:T(8,128)(2,1)} %get-tuple-element.122), channel_id=1, source_target_pairs={{0,16},{4,20},{8,24},{12,28},{16,0},{20,4},{24,8},{28,12},{1,17},{... | collective-permute-start | bytes 3145736 | tf_op jit(solution)/shard_map/ppermute | solution.py:61
  763.9 60.3 %collective-permute-start.100 = (bf16[256,2048]{1,0:T(8,128)(2,1)}, bf16[256,2048]{1,0:T(8,128)(2,1)}, u32[]{:S(2)}, u32[]{:S(2)}) collective-permute-start(bf16[256,2048]{1,0:T(8,128)(2,1)} %get-tuple-element.124), channel_id=1, source_target_pairs={{0,8},{4,12},{8,0},{12,4},{16,24},{20,28},{24,16},{28,20},{1,9},{5... | collective-permute-start | bytes 3145736 | tf_op jit(solution)/shard_map/ppermute | solution.py:61
  808.1 52.7 %collective-permute-start.96 = (bf16[128,4096]{1,0:T(8,128)(2,1)}, bf16[128,4096]{1,0:T(8,128)(2,1)}, u32[]{:S(2)}, u32[]{:S(2)}) collective-permute-start(bf16[128,4096]{1,0:T(8,128)(2,1)} %get-tuple-element.117), channel_id=1, source_target_pairs={{0,8},{4,12},{8,0},{12,4},{16,24},{20,28},{24,16},{28,20},{1,9},{5... | collective-permute-start | bytes 3145736 | tf_op jit(solution)/shard_map/ppermute | solution.py:61
  809.0 51.8 %collective-permute-start.97 = (bf16[128,4096]{1,0:T(8,128)(2,1)}, bf16[128,4096]{1,0:T(8,128)(2,1)}, u32[]{:S(2)}, u32[]{:S(2)}) collective-permute-start(bf16[128,4096]{1,0:T(8,128)(2,1)} %get-tuple-element.118), channel_id=1, source_target_pairs={{0,16},{4,20},{8,24},{12,28},{16,0},{20,4},{24,8},{28,12},{1,17},{... | collective-permute-start | bytes 3145736 | tf_op jit(solution)/shard_map/ppermute | solution.py:61
  809.6 38.3 %collective-permute-start.76 = (f32[8,2048]{1,0:T(8,128)S(1)}, f32[8,2048]{1,0:T(8,128)S(1)}, u32[]{:S(2)}, u32[]{:S(2)}) collective-permute-start(f32[8,2048]{1,0:T(8,128)S(1)} %add.53), channel_id=1, source_target_pairs={{0,8},{4,12},{8,0},{12,4},{16,24},{20,28},{24,16},{28,20},{1,9},{5... | collective-permute-start | bytes 196616 | tf_op jit(solution)/shard_map/ppermute | solution.py:61
  (141 other events, 2551.0 us)
Sparse Core Ops, SparseCore 0:
  15.2 54.7 all-gather.6
  88.0 42.0 all-gather.4
  217.7 64.8 all-gather.10
  311.4 55.5 all-gather.8
  416.7 43.5 reduce-scatter.13
  462.4 42.8 reduce-scatter.11
  552.6 42.8 reduce-scatter.15
  598.3 42.8 reduce-scatter.9
  643.5 42.8 reduce-scatter.7
  706.5 20.3 reduce-scatter.19
  735.0 43.7 reduce-scatter.17

commit v2 on v1

--- a/solution.py
+++ b/solution.py
@@ -16,7 +16,8 @@
 WIDTH = 2048
 GROUP = QH // KVH
 LANES = 128
-TILE = 256
+TILE = 2 * LANES
+ROW_STEP = 64
 NEG = -1e30
 DP, TENSOR = "dp", "tensor"
 EPS = 1e-05
@@ -61,10 +62,10 @@
     return lax.ppermute(x, axis, [(i, i ^ (1 << b)) for i in range(n)])
 
 
-def dp_gather(shard, n):
+def dp_gather(shard, n, cut=None):
     routes, ways = routes_of(n), ways_of(n)
     size = shard.shape[0] // ways
-    parts = [[shard[h * size : (h + 1) * size]] for h in range(ways)]
+    parts = [[cut[h] if cut else shard[h * size : (h + 1) * size]] for h in range(ways)]
     for t in range(len(routes[0])):
         for h in range(ways):
             parts[h] += [swap(p, DP, n, routes[h][t]) for p in parts[h]]
@@ -153,43 +154,75 @@
     )(order, *arrays)
 
 
-def unpack_kernel(me_ref, *refs, kv):
-    out_ref = refs[-1]
-    count = len(refs) - 1
-    for s, ref in enumerate(refs[:-1]):
-        z = jnp.bitwise_xor(me_ref[0], s)
-        for i in range(2):
-            at = pl.ds(pl.multiple_of((i * count + z) * kv, kv), kv)
-            out_ref[:, at] = ref[:, pl.ds(i * kv, kv)]
-
-
-def unpack_kv(me, slots, kv):
-    rows = slots[0].shape[0]
-    return pl.pallas_call(
-        partial(unpack_kernel, kv=kv),
-        out_shape=jax.ShapeDtypeStruct((rows, 2 * kv * len(slots)), bf16),
-        in_specs=[SMEM_SPEC] + [VMEM_SPEC] * len(slots),
-        out_specs=VMEM_SPEC,
-        name="uk",
-    )(me, *slots)
-
-
-def unpack_pair_kernel(in_ref, *outs):
-    rows, width = outs[0].shape[0], in_ref.shape[1] // len(outs)
-    for z in range(in_ref.shape[0] // rows):
-        for i, out in enumerate(outs):
-            out[:, pl.ds(z * width, width)] = in_ref[pl.ds(z * rows, rows), pl.ds(i * width, width)]
-
-
-def unpack_pair(x, n_tensor):
-    rows, total = x.shape[0] // n_tensor, x.shape[1] * n_tensor // 2
-    return pl.pallas_call(
-        unpack_pair_kernel,
-        out_shape=tuple(jax.ShapeDtypeStruct((rows, total), x.dtype) for _ in range(2)),
-        in_specs=[VMEM_SPEC],
-        out_specs=(VMEM_SPEC, VMEM_SPEC),
-        name="uq",
-    )(x)
+def rows_loop(count, body):
+    step = min(ROW_STEP, count)
+
+    def one(r, _):
+        body(pl.ds(pl.multiple_of(r * step, step), step))
+        return 0
+
+    lax.fori_loop(0, count // step, one, 0)
+
+
+def enter_kernel(order_ref, tok_ref, cot_ref, gain1_ref, gain2_ref, tok_out, cot_out, gain1_out, gain2_out, norm_ref):
+    count = order_ref.shape[0]
+    width = tok_ref.shape[1] // count
+    for src, dst in ((tok_ref, tok_out), (cot_ref, cot_out), (gain1_ref, gain1_out), (gain2_ref, gain2_out)):
+        for k in range(count):
+            dst[:, k * width : (k + 1) * width] = src[:, width_at(order_ref, k, width)]
+
+    def normalize(at):
+        values = tok_out[at, :].astype(f32)
+        inverse = lax.rsqrt(jnp.mean(values * values, axis=1, keepdims=True) + EPS)
+        norm_ref[at, :] = (values * inverse * gain1_out[...]).astype(bf16)
+
+    rows_loop(tok_ref.shape[0], normalize)
+
+
+def enter(order, tokens, cotangent, gain1, gain2):
+    arrays = (tokens, cotangent, gain1, gain2)
+    return pl.pallas_call(
+        enter_kernel,
+        out_shape=tuple(jax.ShapeDtypeStruct(a.shape, a.dtype) for a in (*arrays, tokens)),
+        in_specs=[SMEM_SPEC] + [VMEM_SPEC] * 4,
+        out_specs=tuple(VMEM_SPEC for _ in range(5)),
+        name="ro",
+    )(order, *arrays)
+
+
+def unpack_kernel(me_ref, *refs, groups, counts):
+    ins, outs = refs[:counts], refs[counts:]
+    per = len(outs) // groups
+    rows = outs[0].shape[0]
+    cuts = [x[pl.ds(k * rows, rows), :] for x in ins for k in range(x.shape[0] // rows)]
+    for s, cut in enumerate(cuts):
+        for i in range(groups):
+            mine = outs[i * per : (i + 1) * per]
+            width = cut.shape[1] // groups
+            value = cut[:, i * width : (i + 1) * width]
+            if counts > 1:
+                z = jnp.bitwise_xor(me_ref[0], s)
+                at = pl.ds(pl.multiple_of(z * width, width), width)
+            else:
+                at = pl.ds(s * width, width)
+            mine[0][:, at] = value
+            size = rows // max(1, per - 1)
+            for h in range(per - 1):
+                mine[h + 1][:, at] = value[h * size : (h + 1) * size]
+
+
+def unpack(me, cuts, groups, n_tensor, ways):
+    rows = sum(x.shape[0] for x in cuts) // n_tensor
+    columns = cuts[0].shape[1] // groups * n_tensor
+    shapes = [(rows, columns)] + [(rows // ways, columns)] * ways
+    outs = pl.pallas_call(
+        partial(unpack_kernel, groups=groups, counts=len(cuts)),
+        out_shape=tuple(jax.ShapeDtypeStruct(x, bf16) for x in shapes * groups),
+        in_specs=[SMEM_SPEC] + [VMEM_SPEC] * len(cuts),
+        out_specs=tuple(VMEM_SPEC for _ in shapes * groups),
+    )(me, *cuts)
+    per = len(shapes)
+    return [(outs[i * per], outs[i * per + 1 : (i + 1) * per]) for i in range(groups)]
 
 
 def shard_sum(first_ref, terms, ways, at):
@@ -203,6 +236,41 @@
     return parts[0] if ways == 1 else jnp.concatenate(parts, axis=0)
 
 
+def transpose_kernel(in_ref, out_ref, *parts):
+    value = in_ref[...].T
+    out_ref[...] = value
+    for h, part in enumerate(parts):
+        part[...] = value[h * part.shape[0] : (h + 1) * part.shape[0]]
+
+
+def beside_kernel(left_ref, right_ref, out_ref):
+    columns = left_ref.shape[1]
+    out_ref[:, :columns] = left_ref[...]
+    out_ref[:, columns:] = right_ref[...].T
+
+
+def beside(left, right):
+    return pl.pallas_call(
+        beside_kernel,
+        out_shape=jax.ShapeDtypeStruct((left.shape[0], left.shape[1] + right.shape[0]), left.dtype),
+        in_specs=[VMEM_SPEC, VMEM_SPEC],
+        out_specs=VMEM_SPEC,
+        name="cq",
+    )(left, right)
+
+
+def transposed(x, ways):
+    columns, rows = x.shape
+    shapes = [(rows, columns)] + [(rows // ways, columns)] * ways
+    out, *parts = pl.pallas_call(
+        transpose_kernel,
+        out_shape=tuple(jax.ShapeDtypeStruct(y, x.dtype) for y in shapes),
+        in_specs=[VMEM_SPEC],
+        out_specs=tuple(VMEM_SPEC for _ in shapes),
+    )(x)
+    return out, parts
+
+
 def split_terms(refs, ways):
     each = len(refs) // ways
     return [refs[h * each : (h + 1) * each] for h in range(ways)]
@@ -220,9 +288,9 @@
     for i, cuts in enumerate(groups):
         mine = refs[i * count : (i + 1) * count]
         terms = split_terms(mine[1:], ways)
-        for z in range(n_tensor):
-            for at, width, start in cuts:
-                total = shard_sum(mine[0], terms, ways, pl.ds(start + z * width, width))
+        for at, width, starts in cuts:
+            for z in range(n_tensor):
+                total = shard_sum(mine[0], terms, ways, pl.ds(starts[z], width))
                 out_ref[pl.ds(z * rows, rows), pl.ds(at, width)] = total.astype(out_ref.dtype)
 
 
@@ -237,25 +305,39 @@
     )(*arrays)
 
 
-def final_kernel(*refs, ways, transposed):
-    out_ref = refs[-1]
-    total = shard_sum(refs[0], split_terms(refs[1:-1], ways), ways, slice(None))
-    out_ref[...] = total.T if transposed else total
-
-
-def finish(scattered, start, columns, ways, transposed):
+def final_kernel(*refs, ways, outs, transposed):
+    outputs = refs[-outs:]
+    refs = refs[:-outs]
+    total = shard_sum(refs[0], split_terms(refs[1:], ways), ways, slice(None))
+    total = total.T if transposed else total
+    each = pl.num_programs(0) // outs
+    for k, out in enumerate(outputs):
+
+        @pl.when(pl.program_id(0) // each == k)
+        def _(out=out):
+            out[...] = total
+
+
+def finish(scattered, columns, outs, ways, transposed):
     arrays = flat(scattered)
     size = scattered[1][0][-1].shape[0]
     rows = ways * size
     tile = 512
-    base = start // tile
+    each = columns // tile
     blocks = [rows] + [size] * (len(arrays) - 1)
-    return pl.pallas_call(
-        partial(final_kernel, ways=ways, transposed=transposed),
-        grid=(columns // tile,),
-        out_shape=jax.ShapeDtypeStruct((columns, rows) if transposed else (rows, columns), f32),
-        in_specs=[pl.BlockSpec((b, tile), lambda i: (0, base + i)) for b in blocks],
-        out_specs=pl.BlockSpec((tile, rows) if transposed else (rows, tile), (lambda i: (i, 0)) if transposed else (lambda i: (0, i))),
+    at = [partial(lambda i, k: jnp.clip(i - k * each, 0, each - 1), k=k) for k in range(outs)]
+    specs = [
+        pl.BlockSpec((tile, rows), partial(lambda i, f: (f(i), 0), f=f))
+        if transposed
+        else pl.BlockSpec((rows, tile), partial(lambda i, f: (0, f(i)), f=f))
+        for f in at
+    ]
+    return pl.pallas_call(
+        partial(final_kernel, ways=ways, outs=outs, transposed=transposed),
+        grid=(outs * each,),
+        out_shape=tuple(jax.ShapeDtypeStruct((columns, rows) if transposed else (rows, columns), f32) for _ in at),
+        in_specs=[pl.BlockSpec((b, tile), lambda i: (0, i)) for b in blocks],
+        out_specs=tuple(specs),
     )(*arrays)
 
 
@@ -265,6 +347,27 @@
 
 def piece_specs(pieces, tile, column):
     return [pl.BlockSpec((p.shape[0], tile), lambda i, *_: (0, column(i))) for p in pieces]
+
+
+def tables_kernel(row0_ref, cos_ref, sin_ref, all_cos_ref, all_sin_ref, own_cos_ref, own_sin_ref):
+    repeat = LANES // cos_ref.shape[1]
+    cosine, sine = cos_ref[...], sin_ref[...]
+    all_cos_ref[...] = jnp.concatenate([cosine] * repeat, axis=1)
+    all_sin_ref[...] = jnp.concatenate([-sine, sine] * (repeat // 2), axis=1)
+    own = pl.ds(pl.multiple_of(row0_ref[0], own_cos_ref.shape[0]), own_cos_ref.shape[0])
+    own_cos_ref[...] = all_cos_ref[own, :]
+    own_sin_ref[...] = all_sin_ref[own, :]
+
+
+def rotary_tables(row0, cosine, sine, rows):
+    shapes = [(cosine.shape[0], LANES)] * 2 + [(rows, LANES)] * 2
+    return pl.pallas_call(
+        tables_kernel,
+        out_shape=tuple(jax.ShapeDtypeStruct(x, f32) for x in shapes),
+        in_specs=[SMEM_SPEC, VMEM_SPEC, VMEM_SPEC],
+        out_specs=tuple(VMEM_SPEC for _ in shapes),
+        name="tb",
+    )(row0, cosine, sine)
 
 
 def swap_halves(u):
@@ -279,22 +382,18 @@
     return u * cosine - s if back else u * cosine + s
 
 
-def proj_kv_kernel(x_ref, cos_ref, sin_ref, *refs, key_tiles):
+def proj_kv_kernel(x_ref, cos_ref, sin_ref, *refs):
     out_ref = refs[-1]
     raw = dot(x_ref[...], joined(refs[:-1]), ((1,), (0,)))
-    is_key = pl.program_id(0) < key_tiles
-    cosine = jnp.where(is_key, cos_ref[...], 1.0)
-    sine = jnp.where(is_key, sin_ref[...], 0.0)
-    for c in range(raw.shape[1] // LANES):
-        part = raw[:, c * LANES : (c + 1) * LANES]
-        out_ref[:, pl.ds(c * LANES, LANES)] = turn(part, cosine, sine, False).astype(bf16)
+    out_ref[:, :LANES] = turn(raw[:, :LANES], cos_ref[...], sin_ref[...], False).astype(bf16)
+    out_ref[:, LANES:] = raw[:, LANES:].astype(bf16)
 
 
 def proj_kv(x, cosine, sine, pieces):
     rows = x.shape[0]
     whole = lambda shape: pl.BlockSpec(shape, lambda i: (0, 0))
     return pl.pallas_call(
-        partial(proj_kv_kernel, key_tiles=KVH * HD // TILE),
+        proj_kv_kernel,
         grid=(2 * KVH * HD // TILE,),
         in_specs=[whole(x.shape), whole(cosine.shape), whole(sine.shape)] + piece_specs(pieces, TILE, lambda i: i),
         out_specs=pl.BlockSpec((rows, TILE), lambda i: (0, i)),
@@ -303,22 +402,6 @@
         compiler_params=pltpu.CompilerParams(vmem_limit_bytes=VMEM_LIMIT),
         name="pk",
     )(x, cosine, sine, *pieces)
-
-
-def rope_kv_kernel(kv_ref, cos_ref, sin_ref, out_ref, *, key_width):
-    cosine, sine = cos_ref[...], sin_ref[...]
-    for c in range(key_width // LANES):
-        at = pl.ds(c * LANES, LANES)
-        out_ref[:, at] = turn(kv_ref[:, at].astype(f32), cosine, sine, True).astype(bf16)
-    out_ref[:, key_width:] = kv_ref[:, key_width:]
-
-
-def rope_kv_back(kv, cosine, sine):
-    return pl.pallas_call(
-        partial(rope_kv_kernel, key_width=kv.shape[1] // 2),
-        out_shape=jax.ShapeDtypeStruct(kv.shape, bf16),
-        name="rk",
-    )(kv, cosine, sine)
 
 
 def split_halves(block, odd):
@@ -374,7 +457,6 @@
 
 def attn_forward(row0, seg_col, x, kv, cosine, sine, pieces, part, before):
     rows = x.shape[0]
-    half = KVH * HD // LANES
     heads = KVH // FWD_PARTS
     base = part * heads
     args = [row0, seg_col, x, kv, kv, cosine, sine, *pieces]
@@ -385,8 +467,8 @@
         in_specs=[
             whole((rows, 1)),
             whole(x.shape),
-            pl.BlockSpec((LEN, LANES), lambda g, r: (0, (base + g) // 2)),
-            pl.BlockSpec((LEN, LANES), lambda g, r: (0, half + (base + g) // 2)),
+            pl.BlockSpec((LEN, LANES), lambda g, r: (0, (base + g) // 2 * 2)),
+            pl.BlockSpec((LEN, LANES), lambda g, r: (0, (base + g) // 2 * 2 + 1)),
             whole((rows, LANES)),
             whole((rows, LANES)),
         ]
@@ -416,21 +498,31 @@
 
 
 def out_proj_kernel(ctx_ref, tok_ref, gain_ref, *refs):
-    mid_ref, norm_ref, sum_ref = refs[-3:]
+    mid_ref, first_ref, second_ref, sum_ref = refs[-4:]
     i = pl.program_id(0)
 
     @pl.when(i == 0)
     def _():
         sum_ref[...] = tok_ref[...].astype(f32)
 
-    sum_ref[...] += dot(ctx_ref[...], joined(refs[:-3]), ((1,), (1,)))
+    sum_ref[...] += dot(ctx_ref[...], joined(refs[:-4]), ((1,), (1,)))
 
     @pl.when(i == pl.num_programs(0) - 1)
     def _():
-        middle = sum_ref[...]
-        mid_ref[...] = middle
-        inverse = lax.rsqrt(jnp.mean(middle * middle, axis=1, keepdims=True) + EPS)
-        norm_ref[...] = (middle * inverse * gain_ref[...]).astype(bf16)
+        half = first_ref.shape[0]
+        step = min(ROW_STEP, half)
+
+        for k, out_ref in enumerate((first_ref, second_ref)):
+
+            def body(r, _, k=k, out_ref=out_ref):
+                at = pl.ds(pl.multiple_of(k * half + r * step, step), step)
+                middle = sum_ref[at, :]
+                mid_ref[at, :] = middle
+                inverse = lax.rsqrt(jnp.mean(middle * middle, axis=1, keepdims=True) + EPS)
+                out_ref[pl.ds(pl.multiple_of(r * step, step), step), :] = (middle * inverse * gain_ref[...]).astype(bf16)
+                return 0
+
+            lax.fori_loop(0, half // step, body, 0)
 
 
 def out_proj(context, tokens, gain, pieces):
@@ -442,8 +534,12 @@
         grid=(QH * HD // tile,),
         in_specs=[pl.BlockSpec((rows, tile), lambda i: (0, i)), whole(tokens.shape), whole(gain.shape)]
         + piece_specs(pieces, tile, lambda i: i),
-        out_specs=(whole((rows, WIDTH)), whole((rows, WIDTH))),
-        out_shape=(jax.ShapeDtypeStruct((rows, WIDTH), f32), jax.ShapeDtypeStruct((rows, WIDTH), bf16)),
+        out_specs=(whole((rows, WIDTH)), whole((rows // 2, WIDTH)), whole((rows // 2, WIDTH))),
+        out_shape=(
+            jax.ShapeDtypeStruct((rows, WIDTH), f32),
+            jax.ShapeDtypeStruct((rows // 2, WIDTH), bf16),
+            jax.ShapeDtypeStruct((rows // 2, WIDTH), bf16),
+        ),
         scratch_shapes=[pltpu.VMEM((rows, WIDTH), f32)],
         cost_estimate=pl.CostEstimate(flops=2 * rows * WIDTH * QH * HD, bytes_accessed=14 << 20, transcendentals=0),
         compiler_params=pltpu.CompilerParams(vmem_limit_bytes=VMEM_LIMIT),
@@ -462,11 +558,23 @@
 
 def mid_back_kernel(mid_ref, gain_ref, cot_ref, *refs):
     dmid_ref, db_ref, dg_ref = refs[-3:]
-    d_values, d_gain = rms_back(mid_ref[...], gain_ref[...], joined(refs[:-3]).astype(f32))
-    d_middle = cot_ref[...].astype(f32) + d_values
-    dmid_ref[...] = d_middle
-    db_ref[...] = d_middle.astype(bf16)
-    dg_ref[...] = jnp.broadcast_to(d_gain, dg_ref.shape)
+    each = refs[0].shape[0]
+    step = min(ROW_STEP, each)
+    dg_ref[...] = jnp.zeros_like(dg_ref)
+
+    for k, dn_ref in enumerate(refs[:-3]):
+
+        def body(r, _, k=k, dn_ref=dn_ref):
+            at = pl.ds(pl.multiple_of(k * each + r * step, step), step)
+            grad = dn_ref[pl.ds(pl.multiple_of(r * step, step), step), :].astype(f32)
+            d_values, d_gain = rms_back(mid_ref[at, :], gain_ref[...], grad)
+            d_middle = cot_ref[at, :].astype(f32) + d_values
+            dmid_ref[at, :] = d_middle
+            db_ref[at, :] = d_middle.astype(bf16)
+            dg_ref[0:1, :] += d_gain
+            return 0
+
+        lax.fori_loop(0, each // step, body, 0)
 
 
 def mid_back(d_normed, middle, gain, cot):
@@ -483,10 +591,10 @@
 
 
 def attn_bwd_kernel(
-    row0_ref, seg_ref, q_ref, k_ref, v_ref, db_ref, ctx_ref, lse_ref, cos_ref, sin_ref, *refs, count
+    row0_ref, seg_ref, q_ref, k_ref, v_ref, db_ref, ctx_ref, lse_ref, cos_ref, sin_ref, all_cos_ref, all_sin_ref, *refs, count
 ):
     w_query, w_out = refs[:count], refs[count : 2 * count]
-    dq_ref, dk_ref, dv_ref, dn_ref, bias_ref = refs[2 * count :]
+    dq_ref, dkv_ref, dn_ref, bias_ref = refs[2 * count :]
     g = pl.program_id(0)
     rows = q_ref.shape[0]
 
@@ -527,14 +635,15 @@
     dn_ref[...] += dot(dq_ref[...], joined(w_query), ((1,), (1,)))
     wide_low = lax.broadcasted_iota(jnp.int32, (LEN, LANES), 1) < HD
     keep = wide_low == odd
-    for total, out in ((dk_sum, dk_ref), (dv_sum, dv_ref)):
-        folded = (total + pltpu.roll(total, HD, 1)).astype(bf16)
-        out[...] = jnp.where(keep, out[...], folded)
-
-
-def attn_backward(row0, seg_row, query, kv, d_branch, context, lse, cosine, sine, q_pieces, out_pieces):
+    dk_sum = turn(dk_sum + pltpu.roll(dk_sum, HD, 1), all_cos_ref[...], all_sin_ref[...], True)
+    dv_sum = dv_sum + pltpu.roll(dv_sum, HD, 1)
+    for i, total in enumerate((dk_sum, dv_sum)):
+        at = pl.ds(i * LANES, LANES)
+        dkv_ref[:, at] = jnp.where(keep, dkv_ref[:, at], total.astype(bf16))
+
+
+def attn_backward(row0, seg_row, query, kv, d_branch, context, lse, cosine, sine, all_cosine, all_sine, q_pieces, out_pieces):
     rows = query.shape[0]
-    half = KVH * HD // LANES
     whole = lambda shape: pl.BlockSpec(shape, lambda g, r: (0, 0))
     grid_spec = pltpu.PrefetchScalarGridSpec(
         num_scalar_prefetch=1,
@@ -542,20 +651,21 @@
         in_specs=[
             whole((1, rows)),
             pl.BlockSpec((rows, TILE), lambda g, r: (0, g)),
-            pl.BlockSpec((LEN, LANES), lambda g, r: (0, g // 2)),
-            pl.BlockSpec((LEN, LANES), lambda g, r: (0, half + g // 2)),
+            pl.BlockSpec((LEN, LANES), lambda g, r: (0, g // 2 * 2)),
+            pl.BlockSpec((LEN, LANES), lambda g, r: (0, g // 2 * 2 + 1)),
             whole((rows, WIDTH)),
             pl.BlockSpec((rows, TILE), lambda g, r: (0, g)),
             pl.BlockSpec((rows, LANES), lambda g, r: (0, g)),
             whole((rows, LANES)),
             whole((rows, LANES)),
+            whole((LEN, LANES)),
+            whole((LEN, LANES)),
         ]
         + piece_specs(q_pieces, TILE, lambda g: g)
         + piece_specs(out_pieces, TILE, lambda g: g),
         out_specs=[
             pl.BlockSpec((rows, TILE), lambda g, r: (0, g)),
-            pl.BlockSpec((LEN, LANES), lambda g, r: (0, g // 2)),
-            pl.BlockSpec((LEN, LANES), lambda g, r: (0, g // 2)),
+            pl.BlockSpec((LEN, TILE), lambda g, r: (0, g // 2)),
             whole((rows, WIDTH)),
         ],
         scratch_shapes=[pltpu.VMEM((LEN, rows), f32)],
@@ -565,8 +675,7 @@
         grid_spec=grid_spec,
         out_shape=(
             jax.ShapeDtypeStruct((rows, QH * HD), bf16),
-            jax.ShapeDtypeStruct((LEN, KVH * HD), bf16),
-            jax.ShapeDtypeStruct((LEN, KVH * HD), bf16),
+            jax.ShapeDtypeStruct((LEN, 2 * KVH * HD), bf16),
             jax.ShapeDtypeStruct((rows, WIDTH), f32),
         ),
         cost_estimate=pl.CostEstimate(
@@ -574,11 +683,11 @@
         ),
         compiler_params=pltpu.CompilerParams(vmem_limit_bytes=VMEM_LIMIT),
         name="ab",
-    )(row0, seg_row, query, kv, kv, d_branch, context, lse, cosine, sine, *q_pieces, *out_pieces)
+    )(row0, seg_row, query, kv, kv, d_branch, context, lse, cosine, sine, all_cosine, all_sine, *q_pieces, *out_pieces)
 
 
 def in_back_kernel(order_ref, dkv_ref, part_ref, tok_ref, gain_ref, dmid_ref, dg_mlp_ref, *refs):
-    out_ref, dg_ref, sum_ref = refs[-3:]
+    out_ref, dg_ref, sum_ref, gain_ref_sum = refs[-4:]
     i = pl.program_id(0)
 
     @pl.when(i == 0)
@@ -586,19 +695,27 @@
         sum_ref[...] = part_ref[...]
         dg_ref[...] = jnp.zeros_like(dg_ref)
 
-    sum_ref[...] += dot(dkv_ref[...], joined(refs[:-3]), ((1,), (1,)))
+    sum_ref[...] += dot(dkv_ref[...], joined(refs[:-4]), ((1,), (1,)))
 
     @pl.when(i == pl.num_programs(0) - 1)
     def _():
-        d_values, d_gain = rms_back(tok_ref[...].astype(f32), gain_ref[...], sum_ref[...])
-        d_values = d_values + dmid_ref[...]
         count = order_ref.shape[0]
-        width = d_values.shape[1] // count
+        width = sum_ref.shape[1] // count
+        gain_ref_sum[...] = jnp.zeros_like(gain_ref_sum)
+
+        def body(at):
+            d_values, d_gain = rms_back(tok_ref[at, :].astype(f32), gain_ref[...], sum_ref[at, :])
+            d_values = d_values + dmid_ref[at, :]
+            gain_ref_sum[0:1, :] += d_gain
+            for k in range(count):
+                out_ref[at, width_at(order_ref, k, width)] = d_values[:, k * width : (k + 1) * width]
+
+        rows_loop(sum_ref.shape[0], body)
         for k in range(count):
             at = width_at(order_ref, k, width)
-            out_ref[:, at] = d_values[:, k * width : (k + 1) * width]
-            dg_ref[0:1, at] = d_gain[:, k * width : (k + 1) * width]
-            dg_ref[1:2, at] = dg_mlp_ref[0:1, k * width : (k + 1) * width]
+            here = pl.ds(k * width, width)
+            dg_ref[0:1, at] = gain_ref_sum[0:1, here]
+            dg_ref[1:2, at] = dg_mlp_ref[0:1, here]
 
 
 def in_back(order, d_kv, part, tokens, gain, d_middle, mlp_gain, pieces):
@@ -612,28 +729,61 @@
         + piece_specs(pieces, TILE, lambda i: i),
         out_specs=(whole((rows, WIDTH)), whole((8, WIDTH))),
         out_shape=(jax.ShapeDtypeStruct((rows, WIDTH), f32), jax.ShapeDtypeStruct((8, WIDTH), f32)),
-        scratch_shapes=[pltpu.VMEM((rows, WIDTH), f32)],
+        scratch_shapes=[pltpu.VMEM((rows, WIDTH), f32), pltpu.VMEM((8, WIDTH), f32)],
         cost_estimate=pl.CostEstimate(flops=4 * rows * WIDTH * KVH * HD, bytes_accessed=16 << 20, transcendentals=0),
         compiler_params=pltpu.CompilerParams(vmem_limit_bytes=VMEM_LIMIT),
         name="ib",
     )(order, d_kv, part, tokens, gain, d_middle, mlp_gain, *pieces)
 
 
-def mlp_kernel(me_ref, x_ref, *refs, slots, count):
-    cots, refs = refs[: 2 * slots - 1], refs[2 * slots - 1 :]
-    hidden_ref, grads_ref, cot_ref = refs[3 * count :]
-    rows = cots[0].shape[0]
+def d_hidden_kernel(me_ref, *refs, slots):
+    cots, pieces = refs[: 2 * slots - 1], refs[2 * slots - 1 : -3]
+    out_ref, first_ref, second_ref = refs[-3:]
+    half = cots[0].shape[0] // 2
 
     @pl.when(pl.program_id(0) == 0)
     def _():
         for r in range(slots):
             z = lax.rem(me_ref[0] - r + slots, slots)
-            value = cots[r][...] + cots[2 * slots - 1 - r][...] if r else cots[0][...]
-            cot_ref[pl.ds(pl.multiple_of(z * rows, rows), rows), :] = value
-
+            at = pl.ds(pl.multiple_of(z * half, half), half)
+            for k, whole_ref in enumerate((first_ref, second_ref)):
+                here = pl.ds(k * half, half)
+                value = cots[r][here, :] + cots[2 * slots - 1 - r][here, :] if r else cots[0][here, :]
+                whole_ref[at, :] = value
+
+    weights = joined(pieces)
+    rows = first_ref.shape[0]
+    out_ref[:rows, :] = dot(first_ref[...], weights, ((1,), (0,)))
+    out_ref[rows:, :] = dot(second_ref[...], weights, ((1,), (0,)))
+
+
+def d_hidden_of(me, cots, pieces):
+    slots = (len(cots) + 1) // 2
+    rows = cots[0].shape[0] * slots
+    ff = pieces[0].shape[1]
+    whole = lambda shape: pl.BlockSpec(shape, lambda i: (0, 0))
+    half = (rows // 2, WIDTH)
+    return pl.pallas_call(
+        partial(d_hidden_kernel, slots=slots),
+        grid=(ff // TILE,),
+        in_specs=[SMEM_SPEC] + [whole(c.shape) for c in cots] + piece_specs(pieces, TILE, lambda i: i),
+        out_specs=(pl.BlockSpec((rows, TILE), lambda i: (0, i)), whole(half), whole(half)),
+        out_shape=(
+            jax.ShapeDtypeStruct((rows, ff), f32),
+            jax.ShapeDtypeStruct(half, bf16),
+            jax.ShapeDtypeStruct(half, bf16),
+        ),
+        cost_estimate=pl.CostEstimate(flops=2 * rows * WIDTH * ff, bytes_accessed=24 << 20, transcendentals=0),
+        compiler_params=pltpu.CompilerParams(vmem_limit_bytes=VMEM_LIMIT),
+        name="dh",
+    )(me, *cots, *pieces)
+
+
+def mlp_kernel(x_ref, dh_ref, *refs, count):
+    hidden_ref, grads_ref = refs[2 * count :]
     gate = dot(x_ref[...], joined(refs[:count]), ((1,), (0,)))
     up = dot(x_ref[...], joined(refs[count : 2 * count]), ((1,), (0,)))
-    d_hidden = dot(cot_ref[...], joined(refs[2 * count : 3 * count]), ((1,), (0,)))
+    d_hidden = dh_ref[...]
     sig = jax.nn.sigmoid(gate)
     silu = gate * sig
     hidden_ref[...] = (silu * up).astype(bf16)
@@ -641,50 +791,44 @@
     grads_ref[1] = (d_hidden * silu).astype(bf16)
 
 
-def mlp(me, x, cots, chunk, pieces, down_pieces):
+def mlp(x, d_hidden, chunk, pieces):
     rows = x.shape[0]
-    slots = (len(cots) + 1) // 2
-    ff = down_pieces[0].shape[1]
+    ff = d_hidden.shape[1]
     tiles = ff // TILE
-    whole = pl.BlockSpec((rows, WIDTH), lambda i: (0, 0))
-    specs = [SMEM_SPEC, whole] + [pl.BlockSpec((rows // slots, WIDTH), lambda i: (chunk, 0))] * len(cots)
-    for some, base in ((pieces, 0), (pieces, tiles), (down_pieces, 0)):
-        specs += piece_specs(some, TILE, partial(lambda i, base: base + i, base=base))
-    return pl.pallas_call(
-        partial(mlp_kernel, slots=slots, count=len(pieces)),
+    specs = [pl.BlockSpec((rows, WIDTH), lambda i: (0, 0)), pl.BlockSpec((rows, TILE), lambda i: (chunk, i))]
+    for base in (0, tiles):
+        specs += piece_specs(pieces, TILE, partial(lambda i, base: base + i, base=base))
+    return pl.pallas_call(
+        partial(mlp_kernel, count=len(pieces)),
         grid=(tiles,),
         in_specs=specs,
-        out_specs=(
-            pl.BlockSpec((rows, TILE), lambda i: (0, i)),
-            pl.BlockSpec((2, rows, TILE), lambda i: (0, 0, i)),
-            whole,
-        ),
-        out_shape=(
-            jax.ShapeDtypeStruct((rows, ff), bf16),
-            jax.ShapeDtypeStruct((2, rows, ff), bf16),
-            jax.ShapeDtypeStruct((rows, WIDTH), bf16),
-        ),
-        cost_estimate=pl.CostEstimate(flops=6 * rows * WIDTH * ff, bytes_accessed=40 << 20, transcendentals=rows * ff),
+        out_specs=(pl.BlockSpec((rows, TILE), lambda i: (0, i)), pl.BlockSpec((2, rows, TILE), lambda i: (0, 0, i))),
+        out_shape=(jax.ShapeDtypeStruct((rows, ff), bf16), jax.ShapeDtypeStruct((2, rows, ff), bf16)),
+        cost_estimate=pl.CostEstimate(flops=4 * rows * WIDTH * ff, bytes_accessed=30 << 20, transcendentals=rows * ff),
         compiler_params=pltpu.CompilerParams(vmem_limit_bytes=VMEM_LIMIT),
-    )(me, x, *cots, *pieces, *pieces, *down_pieces)
+    )(x, d_hidden, *pieces, *pieces)
 
 
 def back_kernel(x_ref, *refs):
     out_ref, sum_ref = refs[-2:]
     i = pl.program_id(0)
-    part = dot(x_ref[...].reshape(x_ref.shape[-2:]), joined(refs[:-2]), ((1,), (1,)))
+    rows = sum_ref.shape[0]
 
     @pl.when(i == 0)
     def _():
-        sum_ref[...] = part
-
-    @pl.when(i > 0)
-    def _():
-        sum_ref[...] += part
+        def clear(at):
+            sum_ref[at, :] = jnp.zeros((at.size, sum_ref.shape[1]), f32)
+
+        rows_loop(rows, clear)
+
+    sum_ref[...] += dot(x_ref[...].reshape(x_ref.shape[-2:]), joined(refs[:-2]), ((1,), (1,)))
 
     @pl.when(i == pl.num_programs(0) - 1)
     def _():
-        out_ref[...] = sum_ref[...].astype(bf16)
+        def write(at):
+            out_ref[at, :] = sum_ref[at, :].astype(bf16)
+
+        rows_loop(rows, write)
 
 
 def back(x, pieces):
@@ -724,26 +868,25 @@
         at += rows
 
 
-def weight_grad(lefts, rights, block, got, cuts):
-    many, depth, columns = rights[0].shape
+def weight_grad(lefts, rights, which, block, got, cuts):
+    _, depth, columns = rights[0].shape
     rows = WIDTH // 2
     tile = min(512, columns)
-    per = columns // tile
     chunks = len(lefts)
     column = lambda i: (0, i)
     extra = [got] if got is not None else []
     specs = [pl.BlockSpec((depth, rows), lambda i: (0, block))] * chunks
-    specs += [pl.BlockSpec((1, depth, tile), lambda i: (i // per, 0, i % per))] * chunks
+    specs += [pl.BlockSpec((1, depth, tile), lambda i: (which, 0, i))] * chunks
     specs += [pl.BlockSpec((rows, tile), column)] * len(extra)
     return pl.pallas_call(
         partial(grad_kernel, chunks=chunks, received=len(extra), cuts=cuts),
-        grid=(many * per,),
+        grid=(columns // tile,),
         in_specs=specs,
         out_specs=tuple(pl.BlockSpec((c, tile), column) for c in cuts),
-        out_shape=tuple(jax.ShapeDtypeStruct((c, many * columns), bf16) for c in cuts),
+        out_shape=tuple(jax.ShapeDtypeStruct((c, columns), bf16) for c in cuts),
         scratch_shapes=[pltpu.VMEM((rows, depth * chunks), bf16)],
         cost_estimate=pl.CostEstimate(
-            flops=2 * rows * depth * chunks * many * columns, bytes_accessed=8 * rows * many * columns, transcendentals=0
+            flops=2 * rows * depth * chunks * columns, bytes_accessed=8 * rows * columns, transcendentals=0
         ),
         compiler_params=pltpu.CompilerParams(vmem_limit_bytes=VMEM_LIMIT),
     )(*lefts, *rights, *extra)
@@ -769,31 +912,28 @@
     ff = w_gate.shape[1]
     order = jnp.bitwise_xor(jnp.array(width_order(n_dp), jnp.int32), ways * me_dp)
     row0 = (me_z * rows).reshape(1)
-    own_positions = lax.dynamic_slice_in_dim(positions, me_z * rows, rows, 0)
     own_segs = lax.dynamic_slice_in_dim(segments, me_z * rows, rows, 0)
 
     if kv % LANES == 0:
         slots = [jnp.concatenate([w_key, w_value], axis=1)]
         for b in range(n_tensor.bit_length() - 1):
-            slots += [swap(jnp.concatenate(slots, axis=0), TENSOR, n_tensor, b)]
-            slots = [jnp.concatenate(slots, axis=0)]
-        shard_rows = w_key.shape[0]
-        slots = [slots[0][i * shard_rows : (i + 1) * shard_rows] for i in range(n_tensor)]
-        kv_rows = unpack_kv(me_z.reshape(1), slots, kv)
+            slots.append(swap(jnp.concatenate(slots, axis=0), TENSOR, n_tensor, b))
+        kv_rows, kv_cut = unpack(me_z.reshape(1), slots, 1, n_tensor, ways)[0]
     else:
-        kv_rows = jnp.concatenate([over_tensor(w_key, 1), over_tensor(w_value, 1)], axis=1)
-    kv_pieces = dp_gather(kv_rows, n_dp)
-    q_rows, out_rows = unpack_pair(over_tensor(jnp.concatenate([w_query, w_out.T], axis=1)), n_tensor)
-    q_pieces = dp_gather(q_rows, n_dp)
-    out_pieces = dp_gather(out_rows, n_dp)
+        pairs = [over_tensor(w, 1).reshape(w.shape[0], -1, LANES) for w in (w_key, w_value)]
+        kv_rows, kv_cut = jnp.concatenate(pairs, axis=2).reshape(w_key.shape[0], -1), None
+    kv_pieces = dp_gather(kv_rows, n_dp, kv_cut)
+    both = over_tensor(beside(w_query, w_out))
+    (q_rows, q_cut), (out_rows, out_cut) = unpack(me_z.reshape(1), [both], 2, n_tensor, ways)
+    q_pieces = dp_gather(q_rows, n_dp, q_cut)
+    out_pieces = dp_gather(out_rows, n_dp, out_cut)
     gu_pieces = dp_gather(jnp.concatenate([w_gate, w_up], axis=1), n_dp)
-    down_pieces = dp_gather(w_down.T, n_dp)
-
-    gains = jnp.concatenate([norm_attn[None], norm_mlp[None], jnp.zeros((6, width), f32)], axis=0)
-    tokens_here, cot_here, gains_here = reorder(order, (tokens, cotangent, gains), False)
-    gain_attn, gain_mlp = gains_here[:1], gains_here[1:2]
-    chunk = rows // 2
-    chunks = [slice(i * chunk, (i + 1) * chunk) for i in range(2)]
+    down_rows, down_cut = transposed(w_down, ways)
+    down_pieces = dp_gather(down_rows, n_dp, down_cut)
+
+    tokens_here, cot_here, gain_attn, gain_mlp, normed_local = enter(
+        order, tokens, cotangent, norm_attn[None], norm_mlp[None]
+    )
     below, above = [cot_here], [cot_here]
     for r in range(1, n_tensor):
         below.append(lax.ppermute(below[-1], TENSOR, [(i, i + 1) for i in range(r - 1, n_tensor - 1)]))
@@ -802,25 +942,20 @@
 
     freq_index = jnp.arange(HD // 2, dtype=jnp.int32).astype(f32)
     inverse = jnp.exp(freq_index * (-2.0 * math.log(500000.0) / HD))
-    angles = own_positions.astype(f32)[:, None] * inverse[None, :]
-    cosine = jnp.tile(jnp.cos(angles), (1, LANES // (HD // 2)))
-    sine = jnp.sin(angles)
-    sine = jnp.tile(jnp.concatenate([-sine, sine], axis=1), (1, LANES // HD))
-
-    inputs = tokens_here.astype(f32)
-    scale_in = lax.rsqrt(jnp.mean(inputs * inputs, axis=-1, keepdims=True) + EPS)
-    normed_local = (inputs * scale_in * gain_attn).astype(bf16)
+    angles = positions.astype(f32)[:, None] * inverse[None, :]
+    all_cosine, all_sine, cosine, sine = rotary_tables(row0, jnp.cos(angles), jnp.sin(angles), rows)
+
     kv_all = over_tensor(proj_kv(normed_local, cosine, sine, kv_pieces))
     attended = ()
     for i in range(FWD_PARTS):
         attended = attn_forward(row0, own_segs[:, None], normed_local, kv_all, cosine, sine, q_pieces, i, attended)
     context, query, lse = attended
-    middle, normed_mid_local = out_proj(context, tokens_here, gain_mlp, out_pieces)
-    normed_mid = [over_tensor(normed_mid_local[c]) for c in chunks]
-    hidden, mlp_grads, cot_all, d_normed_mid, mlp_branch = [], [], [], [], []
+    middle, *normed_mid_local = out_proj(context, tokens_here, gain_mlp, out_pieces)
+    normed_mid = [over_tensor(x) for x in normed_mid_local]
+    d_hidden, *cot_all = d_hidden_of(me_z.reshape(1), cots, down_pieces)
+    hidden, mlp_grads, d_normed_mid, mlp_branch = [], [], [], []
     for i in range(2):
-        h, g, c = mlp(me_z.reshape(1), normed_mid[i], cots, i, gu_pieces, down_pieces)
-        cot_all.append(c)
+        h, g = mlp(normed_mid[i], d_hidden, i, gu_pieces)
         hidden.append(h[None])
         mlp_grads.append(g)
         d_normed_mid.append(sum_tensor(back(g, gu_pieces)))
@@ -828,37 +963,40 @@
     _, cuts = scatter_segments(n_dp)
     half = [WIDTH // 2]
 
-    def scattered(lefts, rights):
-        other = weight_grad(lefts, rights, 1, None, half)[0]
+    def scattered(lefts, rights, which=0):
+        other = weight_grad(lefts, rights, which, 1, None, half)[0]
         got = swap(other, DP, n_dp, 0)
-        return dp_scatter(weight_grad(lefts, rights, 0, got, cuts), n_dp)
+        return dp_scatter(weight_grad(lefts, rights, which, 0, got, cuts), n_dp)
 
     down_parts = scattered(cot_all, hidden)
-    gu_parts = scattered(normed_mid, mlp_grads)
+    gate_parts = scattered(normed_mid, mlp_grads, 0)
+    up_parts = scattered(normed_mid, mlp_grads, 1)
 
     d_middle, d_branch, mlp_gain_part = mid_back(d_normed_mid, middle, gain_mlp, cot_here)
-    dq, dk, dv, d_normed_part = attn_backward(
-        row0, own_segs[None, :], query, kv_all, d_branch, context, lse, cosine, sine, q_pieces, out_pieces
+    dq, d_kv, d_normed_part = attn_backward(
+        row0, own_segs[None, :], query, kv_all, d_branch, context, lse, cosine, sine, all_cosine, all_sine, q_pieces, out_pieces
     )
+    d_kv = sum_tensor(d_kv)
     out_parts = scattered([d_branch], [context[None]])
-    d_kv = sum_tensor(jnp.concatenate([dk, dv], axis=1))
     query_parts = scattered([normed_local], [dq[None]])
-    d_kv = rope_kv_back(d_kv, cosine, sine)
     kv_parts = scattered([normed_local], [d_kv[None]])
     input_grad, gain_parts = in_back(
         order, d_kv, d_normed_part, tokens_here, gain_attn, d_middle, mlp_gain_part, kv_pieces
     )
 
-    grad_down = finish(down_parts, 0, ff, ways, True)
-    grad_gate = finish(gu_parts, 0, ff, ways, False)
-    grad_up = finish(gu_parts, ff, ff, ways, False)
+    grad_down = finish(down_parts, ff, 1, ways, True)[0]
+    grad_gate = finish(gate_parts, ff, 1, ways, False)[0]
+    grad_up = finish(up_parts, ff, 1, ways, False)[0]
     shard_rows = WIDTH // n_dp
-    packed_qo = pack([query_parts, out_parts], [[(0, q, 0)], [(q, q, 0)]], n_tensor, ways, 2 * q, shard_rows)
-    packed_qo = sum_tensor(packed_qo).astype(f32)
-    grad_query, grad_output = packed_qo[:, :q], packed_qo[:, q:].T
-    packed_kv = pack([kv_parts], [[(0, kv, 0), (kv, kv, kv * n_tensor)]], n_tensor, ways, 2 * kv, shard_rows)
-    packed_kv = sum_tensor(packed_kv).astype(f32)
-    grad_key, grad_value = packed_kv[:, :kv], packed_kv[:, kv:]
+    pair = LANES // kv if kv < LANES else 1
+    kv_at = [z // pair * 2 * max(kv, LANES) + z % pair * kv for z in range(n_tensor)]
+    q_at = [z * q for z in range(n_tensor)]
+    packed = pack([query_parts, out_parts], [[(0, q, q_at)], [(q, q, q_at)]], n_tensor, ways, 2 * q, shard_rows)
+    packed = sum_tensor(packed).astype(f32)
+    grad_query, grad_output = packed[:, :q], packed[:, q:].T
+    kv_cuts = [(0, kv, kv_at), (kv, kv, [x + max(kv, LANES) for x in kv_at])]
+    packed = sum_tensor(pack([kv_parts], [kv_cuts], n_tensor, ways, 2 * kv, shard_rows)).astype(f32)
+    grad_key, grad_value = packed[:, :kv], packed[:, kv:]
 
     def sum_all(x):
         for b in range(n_tensor.bit_length() - 1):

time: 887 us -> 874 us (0.985)
  Pallas kernels: 321 us -> 342 us
  waiting for transfers between devices: 416 us -> 398 us
  local copies, waits for them, and re-layouts: 30 us -> 17 us
    ppermute x97 -> x102, waiting for transfers between devices: 273 us -> 223 us  [swap(): return lax.ppermute(x, axis, [(i, i ^ 1 << b) for i in range(n)])]
    reduce_scatter x7, waiting for transfers between devices: 51.9 us -> 86 us  [sum_tensor(): return lax.psum_scatter(x, TENSOR, scatter_dimension=0, tiled=True)]
    pallas_call x9 -> x13, Pallas kernels: 67.3 us -> 86.4 us  [the longest x2 33.2 us: mlp(): pl.pallas_call(partial(mlp_kernel, count=len(pieces)), grid=(tiles,), in_...]
    pallas_call x10 -> x12, Pallas kernels: 79.2 us -> 85.3 us  [weight_grad(): pl.pallas_call(partial(grad_kernel, chunks=chunks, received=len(extra), c...]
    pallas_call x5 -> x6, Pallas kernels: 16.8 us -> 18.1 us  [add_rows(): pl.pallas_call(partial(add_kernel, spans=[(at, rows, size) for _, at, row...]
    ppermute x97 -> x102, starting transfers between devices: 71.9 us -> 71.7 us  [swap(): return lax.ppermute(x, axis, [(i, i ^ 1 << b) for i in range(n)])]
  transfers between devices with their start and end apart: 114 -> 119, of which waited for: 42 -> 47; matrix products, arithmetic and copies ran while one was open for 3% -> 2% of each run, Pallas kernels for 31% -> 34%
where the time goes in v2:
time: 874 us; the launch traced here: 867 us
  waiting for transfers between devices  398 us (46%)
  Pallas kernels  342 us (39%)
  starting transfers between devices  87.3 us (10%)
  local copies, waits for them, and re-layouts  17 us (2%)
  between operations  15.1 us (2%)
    ppermute x102, waiting for transfers between devices, swap(): return lax.ppermute(x, axis, [(i, i ^ 1 << b) for i in range(n)])  223 us
    ppermute x3, waiting for transfers between devices, layer(): lax.ppermute(above[-1], TENSOR, [(i + 1, i) for i in range(n_tensor - r)])  88.6 us
    reduce_scatter x7, waiting for transfers between devices, sum_tensor(): return lax.psum_scatter(x, TENSOR, scatter_dimension=0, tiled=True)  86 us
    pallas_call x12, Pallas kernels, weight_grad(): pl.pallas_call(partial(grad_kernel, chunks=chunks, received=len(extra), c...  85.3 us
    ppermute x102, starting transfers between devices, swap(): return lax.ppermute(x, axis, [(i, i ^ 1 << b) for i in range(n)])  71.7 us
    pallas_call x4, Pallas kernels, back(): pl.pallas_call(back_kernel, grid=(many * per,), in_specs=[pl.BlockSpec((1...  46.4 us
    pallas_call x1, Pallas kernels, attn_backward(): pl.pallas_call(partial(attn_bwd_kernel, count=len(q_pieces)), grid_spec=g...  39.8 us
    pallas_call x2, Pallas kernels, mlp(): pl.pallas_call(partial(mlp_kernel, count=len(pieces)), grid=(tiles,), in_...  33.2 us
  transfers between devices with their start and end apart: 119, of which 47 were waited for; matrix products, arithmetic and copies ran while one was open for 2% of the time, Pallas kernels for 34%

profile of v2, /device:TPU:0, one launch (start us, length us, event | category | flops | bytes accessed | tf_op | source)
XLA Modules:
  0.0 866.9 jit_solution(6513821800812446150)
XLA Ops:
  24.5 25.1 %collective-permute-done.1.refs_2_ = bf16[512,256]{1,0:T(8,128)(2,1)S(1)} collective-permute-done((bf16[512,256]{1,0:T(8,128)(2,1)S(1)}, bf16[512,256]{1,0:T(8,128)(2,1)S(1)}, u32[]{:S(2)}, u32[]{:S(2)}) %collective-permute-start.1) | collective-permute-done | bytes 262176 | tf_op jit(solution)/shard_map/ppermute | solution.py:62
  85.2 5.4 pk.1
  99.5 10.1 %collective-permute-done.16.refs_2_ = bf16[128,2048]{1,0:T(8,128)(2,1)S(1)} collective-permute-done((bf16[128,2048]{1,0:T(8,128)(2,1)}, bf16[128,2048]{1,0:T(8,128)(2,1)S(1)}, u32[]{:S(2)}, u32[]{:S(2)}) %collective-permute-start.16) | collective-permute-done | bytes 524320 | tf_op jit(solution)/shard_map/ppermute | solution.py:62
  111.7 10.0 %collective-permute-done.19.refs_5_ = bf16[128,2048]{1,0:T(8,128)(2,1)S(1)} collective-permute-done((bf16[128,2048]{1,0:T(8,128)(2,1)}, bf16[128,2048]{1,0:T(8,128)(2,1)S(1)}, u32[]{:S(2)}, u32[]{:S(2)}) %collective-permute-start.19) | collective-permute-done | bytes 524320 | tf_op jit(solution)/shard_map/ppermute | solution.py:62
  122.9 9.2 %collective-permute-done.29.refs_2_.refs_16_ = bf16[128,2048]{1,0:T(8,128)(2,1)S(1)} collective-permute-done((bf16[128,2048]{1,0:T(8,128)(2,1)}, bf16[128,2048]{1,0:T(8,128)(2,1)S(1)}, u32[]{:S(2)}, u32[]{:S(2)}) %collective-permute-start.29) | collective-permute-done | bytes 524320 | tf_op jit(solution)/shard_map/ppermute | solution.py:62
  134.2 9.2 %collective-permute-done.32.refs_5_.refs_19_ = bf16[128,2048]{1,0:T(8,128)(2,1)} collective-permute-done((bf16[128,2048]{1,0:T(8,128)(2,1)}, bf16[128,2048]{1,0:T(8,128)(2,1)}, u32[]{:S(2)}, u32[]{:S(2)}) %collective-permute-start.32) | collective-permute-done | bytes 524320 | tf_op jit(solution)/shard_map/ppermute | solution.py:62
  144.5 9.7 %collective-permute-done.17.refs_3_ = bf16[128,2048]{1,0:T(8,128)(2,1)} collective-permute-done((bf16[128,2048]{1,0:T(8,128)(2,1)S(1)}, bf16[128,2048]{1,0:T(8,128)(2,1)}, u32[]{:S(2)}, u32[]{:S(2)}) %collective-permute-start.17) | collective-permute-done | bytes 524320 | tf_op jit(solution)/shard_map/ppermute | solution.py:62
  161.8 6.7 collective-permute-done.30.refs_3_.refs_17_
  175.9 15.8 %shard_map.223 = (bf16[256,2048]{1,0:T(8,128)(2,1)}, bf16[256,2048]{1,0:T(8,128)(2,1)}, f32[256,1024]{1,0:T(8,128)}) custom-call(s32[1]{0:T(128)} %bitcast.row0_ref, s32[256,1]{1,0:T(8,128)} %copy.34.seg_ref, bf16[256,2048]{1,0:T(8,128)(2,1)} %get-tuple-element.92.x_ref.refs_0_, bf16[1024,1024]{1,0:T(8,128)(2,1)} %all-gather.5.cloned.1.call-done.k_ref.v_ref, ...), custom_call_target="tpu_custom_call" | custom-call | flops 4294967296 | bytes 12582912 | tf_op jit(solution)/shard_map/pallas_call | solution.py:484
  192.6 15.8 %shard_map.224 = (bf16[256,2048]{1,0:T(8,128)(2,1)}, bf16[256,2048]{1,0:T(8,128)(2,1)}, f32[256,1024]{1,0:T(8,128)}) custom-call(s32[1]{0:T(128)} %bitcast.row0_ref, s32[256,1]{1,0:T(8,128)} %copy.34.seg_ref, bf16[256,2048]{1,0:T(8,128)(2,1)} %get-tuple-element.92.x_ref.refs_0_, ...), custom_call_target="tpu_custom_call", output_to_operand_aliasing={{0}: (21, {}), {1}: (22, {}), {2}: (23, {})} | custom-call | flops 4294967296 | bytes 12582912 | tf_op jit(solution)/shard_map/pallas_call | solution.py:484
  210.2 8.7 op.1
  221.1 7.9 collective-permute-done.52.refs_13_.refs_6_
  230.8 6.8 collective-permute-start.41
  237.6 7.8 collective-permute-done.63.refs_4_.refs_18_
  245.4 21.8 %collective-permute-done.61.refs_2_.refs_16_ = bf16[128,4096]{1,0:T(8,128)(2,1)S(1)} collective-permute-done((bf16[128,4096]{1,0:T(8,128)(2,1)}, bf16[128,4096]{1,0:T(8,128)(2,1)S(1)}, u32[]{:S(2)}, u32[]{:S(2)}) %collective-permute-start.61) | collective-permute-done | bytes 1048608 | tf_op jit(solution)/shard_map/ppermute | solution.py:62
  267.7 23.4 %collective-permute-done.44.refs_4_ = bf16[256,2048]{1,0:T(8,128)(2,1)S(1)} collective-permute-done((bf16[256,2048]{1,0:T(8,128)(2,1)}, bf16[256,2048]{1,0:T(8,128)(2,1)S(1)}, u32[]{:S(2)}, u32[]{:S(2)}) %collective-permute-start.44) | collective-permute-done | bytes 1048608 | tf_op jit(solution)/shard_map/ppermute | solution.py:940
  300.5 17.6 %collective-permute-done.45.refs_5_ = bf16[256,2048]{1,0:T(8,128)(2,1)} collective-permute-done((bf16[256,2048]{1,0:T(8,128)(2,1)S(1)}, bf16[256,2048]{1,0:T(8,128)(2,1)}, u32[]{:S(2)}, u32[]{:S(2)}) %collective-permute-start.45) | collective-permute-done | bytes 1048608 | tf_op jit(solution)/shard_map/ppermute | solution.py:940
  324.5 47.7 %collective-permute-done.46.refs_6_ = bf16[256,2048]{1,0:T(8,128)(2,1)} collective-permute-done((bf16[256,2048]{1,0:T(8,128)(2,1)}, bf16[256,2048]{1,0:T(8,128)(2,1)}, u32[]{:S(2)}, u32[]{:S(2)}) %collective-permute-start.46) | collective-permute-done | bytes 1048608 | tf_op jit(solution)/shard_map/ppermute | solution.py:940
  372.8 16.9 %dh.1 = (f32[1024,2048]{1,0:T(8,128)}, bf16[512,2048]{1,0:T(8,128)(2,1)}, bf16[512,2048]{1,0:T(8,128)(2,1)}) custom-call(s32[1]{0:T(128)} %bitcast.4.me_ref, bf16[256,2048]{1,0:T(8,128)(2,1)} %get-tuple-element.112.refs_0_.cot_ref, bf16[256,2048]{1,0:T(8,128)(2,1)} %copy-done.62, bf16[256,2048]{1,0:T(8,128)(2,1)} %collective-permute-done.42.refs_2_, ...), custom_call_target="tpu_custom_call" | custom-call | flops 8589934592 | bytes 25165824 | tf_op jit(solution)/shard_map/dh/pallas_call | solution.py:766
  391.0 16.5 %shard_map.226 = (bf16[512,2048]{1,0:T(8,128)(2,1)}, bf16[2,512,2048]{2,1,0:T(8,128)(2,1)}) custom-call(bf16[512,2048]{1,0:T(8,128)(2,1)} %all-gather.9.cloned.1.call-done.x_ref.refs_0_, f32[1024,2048]{1,0:T(8,128)} %get-tuple-element.116.dh_ref, bf16[256,4096]{1,0:T(8,128)(2,1)} %copy-done, bf16[128,4096]{1,0:T(8,128)(2,1)} %collective-permute-done.60.refs_1_.refs_15_, ...), custom_call_target="tpu_custom_call" | custom-call | flops 8589934592 | bytes 31457280 | tf_op jit(solution)/shard_map/pallas_call | solution.py:801
  407.6 14.0 %shard_map.231 = bf16[512,2048]{1,0:T(8,128)(2,1)} custom-call(bf16[2,512,2048]{2,1,0:T(8,128)(2,1)} %get-tuple-element.121.x_ref.refs_2_, bf16[256,4096]{1,0:T(8,128)(2,1)} %copy-done, bf16[128,4096]{1,0:T(8,128)(2,1)} %collective-permute-done.60.refs_1_.refs_15_, bf16[128,4096]{1,0:T(8,128)(2,1)} %copy-done.2, ...), custom_call_target="tpu_custom_call" | custom-call | flops 8589934592 | bytes 25165824 | tf_op jit(solution)/shard_map/pallas_call | solution.py:838
  421.7 16.6 %shard_map.228 = (bf16[512,2048]{1,0:T(8,128)(2,1)}, bf16[2,512,2048]{2,1,0:T(8,128)(2,1)}) custom-call(bf16[512,2048]{1,0:T(8,128)(2,1)} %all-gather.11.cloned.1.call-done.x_ref.refs_1_, f32[1024,2048]{1,0:T(8,128)} %get-tuple-element.116.dh_ref, bf16[256,4096]{1,0:T(8,128)(2,1)} %copy-done, bf16[128,4096]{1,0:T(8,128)(2,1)} %collective-permute-done.60.refs_1_.refs_15_, ...), custom_call_target="tpu_custom_call" | custom-call | flops 8589934592 | bytes 31457280 | tf_op jit(solution)/shard_map/pallas_call | solution.py:801
  438.4 14.1 %shard_map.232 = bf16[512,2048]{1,0:T(8,128)(2,1)} custom-call(bf16[2,512,2048]{2,1,0:T(8,128)(2,1)} %get-tuple-element.122.x_ref.refs_3_, bf16[256,4096]{1,0:T(8,128)(2,1)} %copy-done, bf16[128,4096]{1,0:T(8,128)(2,1)} %collective-permute-done.60.refs_1_.refs_15_, bf16[128,4096]{1,0:T(8,128)(2,1)} %copy-done.2, ...), custom_call_target="tpu_custom_call" | custom-call | flops 8589934592 | bytes 25165824 | tf_op jit(solution)/shard_map/pallas_call | solution.py:838
  453.0 18.3 %reduce-scatter.12.cloned.1.call-done.refs_0_ = bf16[128,2048]{1,0:T(8,128)(2,1)} async-done(((bf16[512,2048]{1,0:T(8,128)(2,1)}), bf16[128,2048]{1,0:T(8,128)(2,1)}) %reduce-scatter.12.cloned.1.call-update) | async-done | bytes 524304 | tf_op jit(solution)/shard_map/reduce_scatter | solution.py:900
  471.3 45.0 %reduce-scatter.14.cloned.1.call-done.refs_1_ = bf16[128,2048]{1,0:T(8,128)(2,1)} async-done(((bf16[512,2048]{1,0:T(8,128)(2,1)}), bf16[128,2048]{1,0:T(8,128)(2,1)}) %reduce-scatter.14.cloned.1.call-update) | async-done | bytes 524304 | tf_op jit(solution)/shard_map/reduce_scatter | solution.py:900
  516.3 5.6 mb.1
  521.9 39.8 %ab.1 = (bf16[256,2048]{1,0:T(8,128)(2,1)}, bf16[1024,1024]{1,0:T(8,128)(2,1)}, f32[256,2048]{1,0:T(8,128)}) custom-call(s32[1]{0:T(128)} %bitcast.row0_ref, s32[1,256]{1,0:T(1,128)} %bitcast.26, bf16[256,2048]{1,0:T(8,128)(2,1)} %get-tuple-element.120.q_ref, bf16[1024,1024]{1,0:T(8,128)(2,1)} %all-gather.5.cloned.1.call-done.k_ref.v_ref, ...), custom_call_target="tpu_custom_call" | custom-call | flops 15032385536 | bytes 29360128 | tf_op jit(solution)/shard_map/ab/pallas_call | solution.py:673
  561.7 9.1 %shard_map.229 = bf16[512,2048]{1,0:T(8,128)(2,1)} custom-call(bf16[1,512,2048]{2,1,0:T(8,128)(2,1)} %bitcast.30, bf16[256,2048]{1,0:T(8,128)(2,1)} %get-tuple-element.113.refs_7_.refs_0_, bf16[128,2048]{1,0:T(8,128)(2,1)} %copy-done.64, bf16[128,2048]{1,0:T(8,128)(2,1)} %collective-permute-done.48.refs_9_.refs_2_, ...), custom_call_target="tpu_custom_call" | custom-call | flops 4294967296 | bytes 12582912 | tf_op jit(solution)/shard_map/pallas_call | solution.py:838
  570.9 5.3 shard_map.236
  582.0 22.7 %reduce-scatter.16.cloned.1.call-done.dkv_ref = bf16[256,1024]{1,0:T(8,128)(2,1)} async-done(((bf16[1024,1024]{1,0:T(8,128)(2,1)}), bf16[256,1024]{1,0:T(8,128)(2,1)}) %reduce-scatter.16.cloned.1.call-update) | async-done | bytes 524304 | tf_op jit(solution)/shard_map/reduce_scatter | solution.py:900
  607.8 9.1 %shard_map.227 = bf16[512,2048]{1,0:T(8,128)(2,1)} custom-call(bf16[1,512,2048]{2,1,0:T(8,128)(2,1)} %bitcast.27, bf16[256,2048]{1,0:T(8,128)(2,1)} %get-tuple-element.113.refs_7_.refs_0_, bf16[128,2048]{1,0:T(8,128)(2,1)} %copy-done.64, bf16[128,2048]{1,0:T(8,128)(2,1)} %collective-permute-done.48.refs_9_.refs_2_, ...), custom_call_target="tpu_custom_call" | custom-call | flops 4294967296 | bytes 12582912 | tf_op jit(solution)/shard_map/pallas_call | solution.py:838
  617.1 5.9 shard_map.237
  624.6 9.0 %shard_map.244 = bf16[1024,2048]{1,0:T(8,128)(2,1)} custom-call(bf16[512,2048]{1,0:T(8,128)(2,1)} %all-gather.9.cloned.1.call-done.x_ref.refs_0_, bf16[512,2048]{1,0:T(8,128)(2,1)} %all-gather.11.cloned.1.call-done.x_ref.refs_1_, bf16[2,512,2048]{2,1,0:T(8,128)(2,1)} %get-tuple-element.121.x_ref.refs_2_, bf16[2,512,2048]{2,1,0:T(8,128)(2,1)} %get-tuple-element.122.x_ref.refs_3_), custom_call_target="tpu_custom_call" | custom-call | flops 4294967296 | bytes 16777216 | tf_op jit(solution)/shard_map/pallas_call | solution.py:881
  635.1 9.1 %shard_map.248 = bf16[1024,2048]{1,0:T(8,128)(2,1)} custom-call(bf16[512,2048]{1,0:T(8,128)(2,1)} %all-gather.9.cloned.1.call-done.x_ref.refs_0_, bf16[512,2048]{1,0:T(8,128)(2,1)} %all-gather.11.cloned.1.call-done.x_ref.refs_1_, bf16[2,512,2048]{2,1,0:T(8,128)(2,1)} %get-tuple-element.121.x_ref.refs_2_, bf16[2,512,2048]{2,1,0:T(8,128)(2,1)} %get-tuple-element.122.x_ref.refs_3_), custom_call_target="tpu_custom_call" | custom-call | flops 4294967296 | bytes 16777216 | tf_op jit(solution)/shard_map/pallas_call | solution.py:881
  650.4 9.0 %shard_map.252 = bf16[1024,2048]{1,0:T(8,128)(2,1)} custom-call(bf16[512,2048]{1,0:T(8,128)(2,1)} %get-tuple-element.165.refs_0_, bf16[512,2048]{1,0:T(8,128)(2,1)} %get-tuple-element.166.refs_1_, bf16[1,512,2048]{2,1,0:T(8,128)(2,1)} %bitcast.28, bf16[1,512,2048]{2,1,0:T(8,128)(2,1)} %bitcast.31), custom_call_target="tpu_custom_call" | custom-call | flops 4294967296 | bytes 16777216 | tf_op jit(solution)/shard_map/pallas_call | solution.py:881
  659.6 6.2 shard_map.234
  674.1 17.3 %collective-permute-done.79.refs_1_ = bf16[256,2048]{1,0:T(8,128)(2,1)S(1)} collective-permute-done((bf16[256,2048]{1,0:T(8,128)(2,1)}, bf16[256,2048]{1,0:T(8,128)(2,1)S(1)}, u32[]{:S(2)}, u32[]{:S(2)}) %collective-permute-start.79) | collective-permute-done | bytes 1048608 | tf_op jit(solution)/shard_map/ppermute | solution.py:62
  715.4 9.7 %collective-permute-done.81.refs_2_ = bf16[128,2048]{1,0:T(8,128)(2,1)S(1)} collective-permute-done((bf16[128,2048]{1,0:T(8,128)(2,1)}, bf16[128,2048]{1,0:T(8,128)(2,1)S(1)}, u32[]{:S(2)}, u32[]{:S(2)}) %collective-permute-start.81) | collective-permute-done | bytes 524320 | tf_op jit(solution)/shard_map/ppermute | solution.py:62
  727.2 5.7 shard_map.239
  732.9 9.7 %shard_map.245 = (bf16[384,2048]{1,0:T(8,128)(2,1)}, bf16[256,2048]{1,0:T(8,128)(2,1)}, bf16[128,2048]{1,0:T(8,128)(2,1)}, bf16[256,2048]{1,0:T(8,128)(2,1)}) custom-call(bf16[512,2048]{1,0:T(8,128)(2,1)} %all-gather.9.cloned.1.call-done.x_ref.refs_0_, bf16[512,2048]{1,0:T(8,128)(2,1)} %all-gather.11.cloned.1.call-done.x_ref.refs_1_, ...), custom_call_target="tpu_custom_call" | custom-call | flops 4294967296 | bytes 16777216 | tf_op jit(solution)/shard_map/pallas_call | solution.py:881
  744.6 9.5 %shard_map.249 = (bf16[384,2048]{1,0:T(8,128)(2,1)}, bf16[256,2048]{1,0:T(8,128)(2,1)}, bf16[128,2048]{1,0:T(8,128)(2,1)}, bf16[256,2048]{1,0:T(8,128)(2,1)}) custom-call(bf16[512,2048]{1,0:T(8,128)(2,1)} %all-gather.9.cloned.1.call-done.x_ref.refs_0_, bf16[512,2048]{1,0:T(8,128)(2,1)} %all-gather.11.cloned.1.call-done.x_ref.refs_1_, ...), custom_call_target="tpu_custom_call" | custom-call | flops 4294967296 | bytes 16777216 | tf_op jit(solution)/shard_map/pallas_call | solution.py:881
  755.6 9.2 %ib.1 = (f32[256,2048]{1,0:T(8,128)}, f32[8,2048]{1,0:T(8,128)}) custom-call(s32[16]{0:T(128)} %broadcast_xor_fusion.order_ref, bf16[256,1024]{1,0:T(8,128)(2,1)} %reduce-scatter.16.cloned.1.call-done.dkv_ref, f32[256,2048]{1,0:T(8,128)} %get-tuple-element.128.part_ref, bf16[256,2048]{1,0:T(8,128)(2,1)} %get-tuple-element.105.tok_ref, ...), custom_call_target="tpu_custom_call" | custom-call | flops 1073741824 | bytes 16777216 | tf_op jit(solution)/shard_map/ib/pallas_call | solution.py:724
  765.5 7.0 collective-permute-done.73
  774.4 9.6 %shard_map.253 = (bf16[384,2048]{1,0:T(8,128)(2,1)}, bf16[256,2048]{1,0:T(8,128)(2,1)}, bf16[128,2048]{1,0:T(8,128)(2,1)}, bf16[256,2048]{1,0:T(8,128)(2,1)}) custom-call(bf16[512,2048]{1,0:T(8,128)(2,1)} %get-tuple-element.165.refs_0_, bf16[512,2048]{1,0:T(8,128)(2,1)} %get-tuple-element.166.refs_1_, bf16[1,512,2048]{2,1,0:T(8,128)(2,1)} %bitcast.29, ...), custom_call_target="tpu_custom_call" | custom-call | flops 4294967296 | bytes 16777216 | tf_op jit(solution)/shard_map/pallas_call | solution.py:881
  793.3 5.4 collective-permute-done.100.refs_3_
  802.8 11.0 %collective-permute-done.104.refs_1_ = bf16[256,2048]{1,0:T(8,128)(2,1)S(1)} collective-permute-done((bf16[256,2048]{1,0:T(8,128)(2,1)}, bf16[256,2048]{1,0:T(8,128)(2,1)S(1)}, u32[]{:S(2)}, u32[]{:S(2)}) %collective-permute-start.104) | collective-permute-done | bytes 1048608 | tf_op jit(solution)/shard_map/ppermute | solution.py:62
  815.2 6.2 collective-permute-done.105.refs_3_
  825.0 8.9 %collective-permute-done.76 = f32[8,2048]{1,0:T(8,128)S(1)} collective-permute-done((f32[8,2048]{1,0:T(8,128)S(1)}, f32[8,2048]{1,0:T(8,128)S(1)}, u32[]{:S(2)}, u32[]{:S(2)}) %collective-permute-start.76) | collective-permute-done | bytes 65568 | tf_op jit(solution)/shard_map/ppermute | solution.py:62
  (405 shorter events, 211.6 us)
Async XLA Ops:
  7.2 83.6 %all-gather.7.cloned.1.call-start = ((), (), s32[]{:S(2)}) async-start(), calls=%async_computation.8 | async-start | bytes 2621440 | tf_op jit(solution)/shard_map/all_gather | solution.py:896
  9.2 166.7 %all-gather.5.cloned.1.call-start = ((), (), s32[]{:S(2)}) async-start(), calls=%async_computation.7 | async-start | bytes 2621440 | tf_op jit(solution)/shard_map/all_gather | solution.py:896
  12.2 42.9 %collective-permute-start.48 = (bf16[128,2048]{1,0:T(8,128)(2,1)}, bf16[128,2048]{1,0:T(8,128)(2,1)}, u32[]{:S(2)}, u32[]{:S(2)}) collective-permute-start(bf16[128,2048]{1,0:T(8,128)(2,1)} %get-tuple-element.114), channel_id=1, source_target_pairs={{0,16},{4,20},{8,24},{12,28},{16,0},{20,4},{24,8},{28,12},{1,17},{... | collective-permute-start | bytes 1572872 | tf_op jit(solution)/shard_map/ppermute | solution.py:62
  23.0 36.7 %collective-permute-start.47 = (bf16[128,2048]{1,0:T(8,128)(2,1)}, bf16[128,2048]{1,0:T(8,128)(2,1)S(1)}, u32[]{:S(2)}, u32[]{:S(2)}) collective-permute-start(bf16[128,2048]{1,0:T(8,128)(2,1)} %get-tuple-element.114), channel_id=1, source_target_pairs={{0,8},{4,12},{8,0},{12,4},{16,24},{20,28},{24,16},{28,20},{1,9},{5... | collective-permute-start | bytes 1572872 | tf_op jit(solution)/shard_map/ppermute | solution.py:62
  90.6 300.4 %all-gather.9.cloned.1.call-start = ((), (), s32[]{:S(2)}) async-start(), calls=%async_computation.9 | async-start | bytes 2621440 | tf_op jit(solution)/shard_map/all_gather | solution.py:896
  98.7 33.4 %collective-permute-start.29 = (bf16[128,2048]{1,0:T(8,128)(2,1)}, bf16[128,2048]{1,0:T(8,128)(2,1)S(1)}, u32[]{:S(2)}, u32[]{:S(2)}) collective-permute-start(bf16[128,2048]{1,0:T(8,128)(2,1)} %get-tuple-element.108), channel_id=1, source_target_pairs={{0,16},{4,20},{8,24},{12,28},{16,0},{20,4},{24,8},{28,12},{1,17},{... | collective-permute-start | bytes 1572872 | tf_op jit(solution)/shard_map/ppermute | solution.py:62
  110.5 32.9 %collective-permute-start.32 = (bf16[128,2048]{1,0:T(8,128)(2,1)}, bf16[128,2048]{1,0:T(8,128)(2,1)}, u32[]{:S(2)}, u32[]{:S(2)}) collective-permute-start(bf16[128,2048]{1,0:T(8,128)(2,1)} %get-tuple-element.109), channel_id=1, source_target_pairs={{0,8},{4,12},{8,0},{12,4},{16,24},{20,28},{24,16},{28,20},{1,9},{5... | collective-permute-start | bytes 1572872 | tf_op jit(solution)/shard_map/ppermute | solution.py:62
  161.3 47.2 %collective-permute-start.34 = (bf16[256,2048]{1,0:T(8,128)(2,1)}, bf16[256,2048]{1,0:T(8,128)(2,1)}, u32[]{:S(2)}, u32[]{:S(2)}) collective-permute-start(bf16[256,2048]{1,0:T(8,128)(2,1)} %get-tuple-element.107.refs_0_.refs_14_), channel_id=1, source_target_pairs={{0,4},{4,0},{8,12},{12,8},{16,20},{20,16},{24,28},{28,24},{1,5},{5... | collective-permute-start | bytes 3145736 | tf_op jit(solution)/shard_map/ppermute | solution.py:62
  161.4 30.7 %collective-permute-start.38 = (bf16[128,2048]{1,0:T(8,128)(2,1)}, bf16[128,2048]{1,0:T(8,128)(2,1)}, u32[]{:S(2)}, u32[]{:S(2)}) collective-permute-start(bf16[128,2048]{1,0:T(8,128)(2,1)} %collective-permute-done.31.refs_4_.refs_18_), channel_id=1, source_target_pairs={{0,4},{4,0},{8,12},{12,8},{16,20},{20,16},{24,28},{28,24},{1,5},{5... | collective-permute-start | bytes 1572872 | tf_op jit(solution)/shard_map/ppermute | solution.py:62
  175.4 33.2 %collective-permute-start.37 = (bf16[128,2048]{1,0:T(8,128)(2,1)}, bf16[128,2048]{1,0:T(8,128)(2,1)}, u32[]{:S(2)}, u32[]{:S(2)}) collective-permute-start(bf16[128,2048]{1,0:T(8,128)(2,1)} %copy-done.46), channel_id=1, source_target_pairs={{0,4},{4,0},{8,12},{12,8},{16,20},{20,16},{24,28},{28,24},{1,5},{5... | collective-permute-start | bytes 1572872 | tf_op jit(solution)/shard_map/ppermute | solution.py:62
  175.7 34.4 %collective-permute-start.40 = (bf16[128,2048]{1,0:T(8,128)(2,1)}, bf16[128,2048]{1,0:T(8,128)(2,1)}, u32[]{:S(2)}, u32[]{:S(2)}) collective-permute-start(bf16[128,2048]{1,0:T(8,128)(2,1)} %copy-done.47), channel_id=1, source_target_pairs={{0,4},{4,0},{8,12},{12,8},{16,20},{20,16},{24,28},{28,24},{1,5},{5... | collective-permute-start | bytes 1572872 | tf_op jit(solution)/shard_map/ppermute | solution.py:62
  191.7 37.8 %collective-permute-start.53 = (bf16[256,2048]{1,0:T(8,128)(2,1)}, bf16[256,2048]{1,0:T(8,128)(2,1)}, u32[]{:S(2)}, u32[]{:S(2)}) collective-permute-start(bf16[256,2048]{1,0:T(8,128)(2,1)} %get-tuple-element.113.refs_7_.refs_0_), channel_id=1, source_target_pairs={{0,4},{4,0},{8,12},{12,8},{16,20},{20,16},{24,28},{28,24},{1,5},{5... | collective-permute-start | bytes 3145736 | tf_op jit(solution)/shard_map/ppermute | solution.py:62
  192.1 38.7 %collective-permute-start.64 = (bf16[128,4096]{1,0:T(8,128)(2,1)}, bf16[128,4096]{1,0:T(8,128)(2,1)S(1)}, u32[]{:S(2)}, u32[]{:S(2)}) collective-permute-start(bf16[128,4096]{1,0:T(8,128)(2,1)} %get-tuple-element.206), channel_id=1, source_target_pairs={{0,8},{4,12},{8,0},{12,4},{16,24},{20,28},{24,16},{28,20},{1,9},{5... | collective-permute-start | bytes 3145736 | tf_op jit(solution)/shard_map/ppermute | solution.py:62
  218.9 202.8 %all-gather.11.cloned.1.call-start = ((), (), s32[]{:S(2)}) async-start(), calls=%async_computation.11 | async-start | bytes 2621440 | tf_op jit(solution)/shard_map/all_gather | solution.py:896
  220.3 46.9 %collective-permute-start.61 = (bf16[128,4096]{1,0:T(8,128)(2,1)}, bf16[128,4096]{1,0:T(8,128)(2,1)S(1)}, u32[]{:S(2)}, u32[]{:S(2)}) collective-permute-start(bf16[128,4096]{1,0:T(8,128)(2,1)} %get-tuple-element.207), channel_id=1, source_target_pairs={{0,16},{4,20},{8,24},{12,28},{16,0},{20,4},{24,8},{28,12},{1,17},{... | collective-permute-start | bytes 3145736 | tf_op jit(solution)/shard_map/ppermute | solution.py:62
  228.9 38.2 %collective-permute-start.60 = (bf16[128,4096]{1,0:T(8,128)(2,1)}, bf16[128,4096]{1,0:T(8,128)(2,1)}, u32[]{:S(2)}, u32[]{:S(2)}) collective-permute-start(bf16[128,4096]{1,0:T(8,128)(2,1)} %get-tuple-element.207), channel_id=1, source_target_pairs={{0,8},{4,12},{8,0},{12,4},{16,24},{20,28},{24,16},{28,20},{1,9},{5... | collective-permute-start | bytes 3145736 | tf_op jit(solution)/shard_map/ppermute | solution.py:62
  229.5 61.5 %collective-permute-start.44 = (bf16[256,2048]{1,0:T(8,128)(2,1)}, bf16[256,2048]{1,0:T(8,128)(2,1)S(1)}, u32[]{:S(2)}, u32[]{:S(2)}) collective-permute-start(bf16[256,2048]{1,0:T(8,128)(2,1)} %get-tuple-element.112.refs_0_.cot_ref), channel_id=1, source_target_pairs={{1,0},{2,1},{3,2},{5,4},{6,5},{7,6},{9,8},{10,9},{11,10},{13,12},{... | collective-permute-start | bytes 3145736 | tf_op jit(solution)/shard_map/ppermute | solution.py:940
  230.8 61.5 %collective-permute-start.41 = (bf16[256,2048]{1,0:T(8,128)(2,1)}, bf16[256,2048]{1,0:T(8,128)(2,1)S(1)}, u32[]{:S(2)}, u32[]{:S(2)}) collective-permute-start(bf16[256,2048]{1,0:T(8,128)(2,1)} %get-tuple-element.112.refs_0_.cot_ref), channel_id=1, source_target_pairs={{0,1},{1,2},{2,3},{4,5},{5,6},{6,7},{8,9},{9,10},{10,11},{12,13},{... | collective-permute-start | bytes 3145736 | tf_op jit(solution)/shard_map/ppermute | solution.py:939
  245.4 48.8 %collective-permute-start.56 = (bf16[128,2048]{1,0:T(8,128)(2,1)}, bf16[128,2048]{1,0:T(8,128)(2,1)S(1)}, u32[]{:S(2)}, u32[]{:S(2)}) collective-permute-start(bf16[128,2048]{1,0:T(8,128)(2,1)} %collective-permute-done.49.refs_10_.refs_3_), channel_id=1, source_target_pairs={{0,4},{4,0},{8,12},{12,8},{16,20},{20,16},{24,28},{28,24},{1,5},{5... | collective-permute-start | bytes 1572872 | tf_op jit(solution)/shard_map/ppermute | solution.py:62
  267.1 29.4 %collective-permute-start.71 = (bf16[128,4096]{1,0:T(8,128)(2,1)S(1)}, bf16[128,4096]{1,0:T(8,128)(2,1)S(1)}, u32[]{:S(2)}, u32[]{:S(2)}) collective-permute-start(bf16[128,4096]{1,0:T(8,128)(2,1)S(1)} %collective-permute-done.64.refs_5_.refs_19_), channel_id=1, source_target_pairs={{0,4},{4,0},{8,12},{12,8},{16,20},{20,16},{24,28},{28,24},{1,5},{5... | collective-permute-start | bytes 3145736 | tf_op jit(solution)/shard_map/ppermute | solution.py:62
  267.2 30.9 %collective-permute-start.70 = (bf16[128,4096]{1,0:T(8,128)(2,1)}, bf16[128,4096]{1,0:T(8,128)(2,1)S(1)}, u32[]{:S(2)}, u32[]{:S(2)}) collective-permute-start(bf16[128,4096]{1,0:T(8,128)(2,1)} %collective-permute-done.63.refs_4_.refs_18_), channel_id=1, source_target_pairs={{0,4},{4,0},{8,12},{12,8},{16,20},{20,16},{24,28},{28,24},{1,5},{5... | collective-permute-start | bytes 3145736 | tf_op jit(solution)/shard_map/ppermute | solution.py:62
  296.4 93.3 %collective-permute-start.66 = (bf16[256,4096]{1,0:T(8,128)(2,1)S(1)}, bf16[256,4096]{1,0:T(8,128)(2,1)}, u32[]{:S(2)}, u32[]{:S(2)}) collective-permute-start(bf16[256,4096]{1,0:T(8,128)(2,1)S(1)} %constant_dynamic-update-slice_fusion.2.refs_0_.refs_14_), channel_id=1, source_target_pairs={{0,4},{4,0},{8,12},{12,8},{16,20},{20,16},{24,28},{28,24},{1,5},{5... | collective-permute-start | bytes 6291464 | tf_op jit(solution)/shard_map/ppermute | solution.py:62
  318.0 54.2 %collective-permute-start.46 = (bf16[256,2048]{1,0:T(8,128)(2,1)}, bf16[256,2048]{1,0:T(8,128)(2,1)}, u32[]{:S(2)}, u32[]{:S(2)}) collective-permute-start(bf16[256,2048]{1,0:T(8,128)(2,1)} %collective-permute-done.45.refs_5_), channel_id=1, source_target_pairs={{1,0},{5,4},{9,8},{13,12},{17,16},{21,20},{25,24},{29,28}} | collective-permute-start | bytes 3145736 | tf_op jit(solution)/shard_map/ppermute | solution.py:940
  319.4 52.9 %collective-permute-start.43 = (bf16[256,2048]{1,0:T(8,128)(2,1)}, bf16[256,2048]{1,0:T(8,128)(2,1)}, u32[]{:S(2)}, u32[]{:S(2)}) collective-permute-start(bf16[256,2048]{1,0:T(8,128)(2,1)} %collective-permute-done.42.refs_2_), channel_id=1, source_target_pairs={{2,3},{6,7},{10,11},{14,15},{18,19},{22,23},{26,27},{30,31}} | collective-permute-start | bytes 3145736 | tf_op jit(solution)/shard_map/ppermute | solution.py:939
  321.0 150.3 %reduce-scatter.12.cloned.1.call-start = ((), (), s32[]{:S(2)}) async-start(), calls=%async_computation.13 | async-start | bytes 2621440 | tf_op jit(solution)/shard_map/reduce_scatter | solution.py:900
  322.3 67.4 %collective-permute-start.67 = (bf16[128,4096]{1,0:T(8,128)(2,1)}, bf16[128,4096]{1,0:T(8,128)(2,1)S(1)}, u32[]{:S(2)}, u32[]{:S(2)}) collective-permute-start(bf16[128,4096]{1,0:T(8,128)(2,1)} %collective-permute-done.60.refs_1_.refs_15_), channel_id=1, source_target_pairs={{0,4},{4,0},{8,12},{12,8},{16,20},{20,16},{24,28},{28,24},{1,5},{5... | collective-permute-start | bytes 3145736 | tf_op jit(solution)/shard_map/ppermute | solution.py:62
  324.5 65.2 %collective-permute-start.68 = (bf16[128,4096]{1,0:T(8,128)(2,1)}, bf16[128,4096]{1,0:T(8,128)(2,1)S(1)}, u32[]{:S(2)}, u32[]{:S(2)}) collective-permute-start(bf16[128,4096]{1,0:T(8,128)(2,1)} %copy-done.2), channel_id=1, source_target_pairs={{0,4},{4,0},{8,12},{12,8},{16,20},{20,16},{24,28},{28,24},{1,5},{5... | collective-permute-start | bytes 3145736 | tf_op jit(solution)/shard_map/ppermute | solution.py:62
  421.6 94.6 %reduce-scatter.14.cloned.1.call-start = ((), (), s32[]{:S(2)}) async-start(), calls=%async_computation.14 | async-start | bytes 2621440 | tf_op jit(solution)/shard_map/reduce_scatter | solution.py:900
  452.5 152.1 %reduce-scatter.16.cloned.1.call-start = ((), (), s32[]{:S(2)}) async-start(), calls=%async_computation.15 | async-start | bytes 2621440 | tf_op jit(solution)/shard_map/reduce_scatter | solution.py:900
  561.7 274.9 %reduce-scatter.10.cloned.1.call-start = ((), (), s32[]{:S(2)}) async-start(), calls=%async_computation.12 | async-start | bytes 2621440 | tf_op jit(solution)/shard_map/reduce_scatter | solution.py:900
  570.8 265.7 %reduce-scatter.8.cloned.1.call-start = ((), (), s32[]{:S(2)}) async-start(), calls=%async_computation.10 | async-start | bytes 2621440 | tf_op jit(solution)/shard_map/reduce_scatter | solution.py:900
  576.2 40.9 %collective-permute-start.83 = (bf16[1024,2048]{1,0:T(8,128)(2,1)}, bf16[1024,2048]{1,0:T(8,128)(2,1)}, u32[]{:S(2)}, u32[]{:S(2)}) collective-permute-start(bf16[1024,2048]{1,0:T(8,128)(2,1)} %shard_map.236), channel_id=1, source_target_pairs={{0,4},{4,0},{8,12},{12,8},{16,20},{20,16},{24,28},{28,24},{1,5},{5... | collective-permute-start | bytes 12582920 | tf_op jit(solution)/shard_map/ppermute | solution.py:62
  581.5 66.6 %collective-permute-start.78 = (bf16[1024,2048]{1,0:T(8,128)(2,1)}, bf16[1024,2048]{1,0:T(8,128)(2,1)}, u32[]{:S(2)}, u32[]{:S(2)}) collective-permute-start(bf16[1024,2048]{1,0:T(8,128)(2,1)} %shard_map.233), channel_id=1, source_target_pairs={{0,4},{4,0},{8,12},{12,8},{16,20},{20,16},{24,28},{28,24},{1,5},{5... | collective-permute-start | bytes 12582920 | tf_op jit(solution)/shard_map/ppermute | solution.py:62
  607.8 36.4 %collective-permute-start.88 = (bf16[1024,1024]{1,0:T(8,128)(2,1)}, bf16[1024,1024]{1,0:T(8,128)(2,1)}, u32[]{:S(2)}, u32[]{:S(2)}) collective-permute-start(bf16[1024,1024]{1,0:T(8,128)(2,1)} %shard_map.240), channel_id=1, source_target_pairs={{0,4},{4,0},{8,12},{12,8},{16,20},{20,16},{24,28},{28,24},{1,5},{5... | collective-permute-start | bytes 6291464 | tf_op jit(solution)/shard_map/ppermute | solution.py:62
  616.9 238.5 %reduce-scatter.20.cloned.1.call-start = ((), (), s32[]{:S(2)}) async-start(), calls=%async_computation.17 | async-start | bytes 655360 | tf_op jit(solution)/shard_map/reduce_scatter | solution.py:900
  635.1 97.9 %collective-permute-start.93 = (bf16[1024,2048]{1,0:T(8,128)(2,1)}, bf16[1024,2048]{1,0:T(8,128)(2,1)}, u32[]{:S(2)}, u32[]{:S(2)}) collective-permute-start(bf16[1024,2048]{1,0:T(8,128)(2,1)} %shard_map.244), channel_id=1, source_target_pairs={{0,4},{4,0},{8,12},{12,8},{16,20},{20,16},{24,28},{28,24},{1,5},{5... | collective-permute-start | bytes 12582920 | tf_op jit(solution)/shard_map/ppermute | solution.py:62
  644.2 100.4 %collective-permute-start.98 = (bf16[1024,2048]{1,0:T(8,128)(2,1)}, bf16[1024,2048]{1,0:T(8,128)(2,1)}, u32[]{:S(2)}, u32[]{:S(2)}) collective-permute-start(bf16[1024,2048]{1,0:T(8,128)(2,1)} %shard_map.248), channel_id=1, source_target_pairs={{0,4},{4,0},{8,12},{12,8},{16,20},{20,16},{24,28},{28,24},{1,5},{5... | collective-permute-start | bytes 12582920 | tf_op jit(solution)/shard_map/ppermute | solution.py:62
  659.6 114.3 %collective-permute-start.103 = (bf16[1024,2048]{1,0:T(8,128)(2,1)}, bf16[1024,2048]{1,0:T(8,128)(2,1)}, u32[]{:S(2)}, u32[]{:S(2)}) collective-permute-start(bf16[1024,2048]{1,0:T(8,128)(2,1)} %shard_map.252), channel_id=1, source_target_pairs={{0,4},{4,0},{8,12},{12,8},{16,20},{20,16},{24,28},{28,24},{1,5},{5... | collective-permute-start | bytes 12582920 | tf_op jit(solution)/shard_map/ppermute | solution.py:62
  706.3 150.7 %reduce-scatter.18.cloned.1.call-start = ((), (), s32[]{:S(2)}) async-start(), calls=%async_computation.16 | async-start | bytes 2621440 | tf_op jit(solution)/shard_map/reduce_scatter | solution.py:900
  742.6 41.4 %collective-permute-start.94 = (bf16[256,2048]{1,0:T(8,128)(2,1)}, bf16[256,2048]{1,0:T(8,128)(2,1)S(1)}, u32[]{:S(2)}, u32[]{:S(2)}) collective-permute-start(bf16[256,2048]{1,0:T(8,128)(2,1)} %get-tuple-element.154), channel_id=1, source_target_pairs={{0,16},{4,20},{8,24},{12,28},{16,0},{20,4},{24,8},{28,12},{1,17},{... | collective-permute-start | bytes 3145736 | tf_op jit(solution)/shard_map/ppermute | solution.py:62
  743.5 42.9 %collective-permute-start.95 = (bf16[256,2048]{1,0:T(8,128)(2,1)}, bf16[256,2048]{1,0:T(8,128)(2,1)S(1)}, u32[]{:S(2)}, u32[]{:S(2)}) collective-permute-start(bf16[256,2048]{1,0:T(8,128)(2,1)} %get-tuple-element.156), channel_id=1, source_target_pairs={{0,8},{4,12},{8,0},{12,4},{16,24},{20,28},{24,16},{28,20},{1,9},{5... | collective-permute-start | bytes 3145736 | tf_op jit(solution)/shard_map/ppermute | solution.py:62
  754.1 37.2 %collective-permute-start.99 = (bf16[256,2048]{1,0:T(8,128)(2,1)}, bf16[256,2048]{1,0:T(8,128)(2,1)S(1)}, u32[]{:S(2)}, u32[]{:S(2)}) collective-permute-start(bf16[256,2048]{1,0:T(8,128)(2,1)} %get-tuple-element.160), channel_id=1, source_target_pairs={{0,16},{4,20},{8,24},{12,28},{16,0},{20,4},{24,8},{28,12},{1,17},{... | collective-permute-start | bytes 3145736 | tf_op jit(solution)/shard_map/ppermute | solution.py:62
  784.1 29.7 %collective-permute-start.104 = (bf16[256,2048]{1,0:T(8,128)(2,1)}, bf16[256,2048]{1,0:T(8,128)(2,1)S(1)}, u32[]{:S(2)}, u32[]{:S(2)}) collective-permute-start(bf16[256,2048]{1,0:T(8,128)(2,1)} %get-tuple-element.168), channel_id=1, source_target_pairs={{0,16},{4,20},{8,24},{12,28},{16,0},{20,4},{24,8},{28,12},{1,17},{... | collective-permute-start | bytes 3145736 | tf_op jit(solution)/shard_map/ppermute | solution.py:62
  785.3 36.1 %collective-permute-start.105 = (bf16[256,2048]{1,0:T(8,128)(2,1)}, bf16[256,2048]{1,0:T(8,128)(2,1)}, u32[]{:S(2)}, u32[]{:S(2)}) collective-permute-start(bf16[256,2048]{1,0:T(8,128)(2,1)} %get-tuple-element.170), channel_id=1, source_target_pairs={{0,8},{4,12},{8,0},{12,4},{16,24},{20,28},{24,16},{28,20},{1,9},{5... | collective-permute-start | bytes 3145736 | tf_op jit(solution)/shard_map/ppermute | solution.py:62
  791.3 43.1 %collective-permute-start.96 = (bf16[128,2048]{1,0:T(8,128)(2,1)}, bf16[128,2048]{1,0:T(8,128)(2,1)S(1)}, u32[]{:S(2)}, u32[]{:S(2)}) collective-permute-start(bf16[128,2048]{1,0:T(8,128)(2,1)} %get-tuple-element.157), channel_id=1, source_target_pairs={{0,8},{4,12},{8,0},{12,4},{16,24},{20,28},{24,16},{28,20},{1,9},{5... | collective-permute-start | bytes 1572872 | tf_op jit(solution)/shard_map/ppermute | solution.py:62
  792.7 42.8 %collective-permute-start.97 = (bf16[128,2048]{1,0:T(8,128)(2,1)}, bf16[128,2048]{1,0:T(8,128)(2,1)}, u32[]{:S(2)}, u32[]{:S(2)}) collective-permute-start(bf16[128,2048]{1,0:T(8,128)(2,1)} %get-tuple-element.158), channel_id=1, source_target_pairs={{0,16},{4,20},{8,24},{12,28},{16,0},{20,4},{24,8},{28,12},{1,17},{... | collective-permute-start | bytes 1572872 | tf_op jit(solution)/shard_map/ppermute | solution.py:62
  798.8 35.1 %collective-permute-start.76 = (f32[8,2048]{1,0:T(8,128)S(1)}, f32[8,2048]{1,0:T(8,128)S(1)}, u32[]{:S(2)}, u32[]{:S(2)}) collective-permute-start(f32[8,2048]{1,0:T(8,128)S(1)} %add.39), channel_id=1, source_target_pairs={{0,8},{4,12},{8,0},{12,4},{16,24},{20,28},{24,16},{28,20},{1,9},{5... | collective-permute-start | bytes 196616 | tf_op jit(solution)/shard_map/ppermute | solution.py:62
  813.8 31.8 %collective-permute-start.101 = (bf16[128,2048]{1,0:T(8,128)(2,1)}, bf16[128,2048]{1,0:T(8,128)(2,1)}, u32[]{:S(2)}, u32[]{:S(2)}) collective-permute-start(bf16[128,2048]{1,0:T(8,128)(2,1)} %get-tuple-element.163), channel_id=1, source_target_pairs={{0,8},{4,12},{8,0},{12,4},{16,24},{20,28},{24,16},{28,20},{1,9},{5... | collective-permute-start | bytes 1572872 | tf_op jit(solution)/shard_map/ppermute | solution.py:62
  (139 other events, 2370.0 us)
Sparse Core Ops, SparseCore 0:
  10.2 58.0 all-gather.6
  90.7 51.0 all-gather.4
  219.0 70.0 all-gather.8
  321.1 57.2 all-gather.10
  421.8 49.4 reduce-scatter.11
  473.4 42.8 reduce-scatter.13
  561.8 42.7 reduce-scatter.15
  606.9 42.8 reduce-scatter.9
  652.1 42.8 reduce-scatter.7
  706.4 21.1 reduce-scatter.19
  733.1 44.4 reduce-scatter.17

commit v3 on v2

--- a/solution.py
+++ b/solution.py
@@ -809,8 +809,8 @@
     )(x, d_hidden, *pieces, *pieces)
 
 
-def back_kernel(x_ref, *refs):
-    out_ref, sum_ref = refs[-2:]
+def back_kernel(x_ref, *refs, count):
+    pieces, (out_ref, sum_ref) = refs[:count], refs[-2:]
     i = pl.program_id(0)
     rows = sum_ref.shape[0]
 
@@ -821,31 +821,38 @@
 
         rows_loop(rows, clear)
 
-    sum_ref[...] += dot(x_ref[...].reshape(x_ref.shape[-2:]), joined(refs[:-2]), ((1,), (1,)))
+    sum_ref[...] += dot(x_ref[...].reshape(x_ref.shape[-2:]), joined(pieces), ((1,), (1,)))
 
     @pl.when(i == pl.num_programs(0) - 1)
     def _():
-        def write(at):
-            out_ref[at, :] = sum_ref[at, :].astype(bf16)
-
-        rows_loop(rows, write)
-
-
-def back(x, pieces):
+        each = rows // out_ref.shape[0]
+
+        for z in range(out_ref.shape[0]):
+            def write(at, z=z):
+                out_ref[z, 0, at, :] = sum_ref[pl.ds(z * each + at.start, at.size), :].astype(bf16)
+
+            rows_loop(each, write)
+
+
+def back(x, pieces, n_tensor, chunk=0, chunks=1, before=()):
     many, rows, ff = x.shape
     tile = min(1024, ff)
     per = ff // tile
-    return pl.pallas_call(
-        back_kernel,
+    each = rows // n_tensor
+    out = pl.pallas_call(
+        partial(back_kernel, count=len(pieces)),
         grid=(many * per,),
         in_specs=[pl.BlockSpec((1, rows, tile), lambda i: (i // per, 0, i % per))]
-        + piece_specs(pieces, tile, lambda i: i),
-        out_specs=pl.BlockSpec((rows, WIDTH), lambda i: (0, 0)),
-        out_shape=jax.ShapeDtypeStruct((rows, WIDTH), bf16),
+        + piece_specs(pieces, tile, lambda i: i)
+        + [pl.BlockSpec(memory_space=pl.ANY)] * len(before),
+        out_specs=pl.BlockSpec((n_tensor, 1, each, WIDTH), lambda i: (0, chunk, 0, 0)),
+        out_shape=jax.ShapeDtypeStruct((n_tensor, chunks, each, WIDTH), bf16),
         scratch_shapes=[pltpu.VMEM((rows, WIDTH), f32)],
         cost_estimate=pl.CostEstimate(flops=2 * many * rows * WIDTH * ff, bytes_accessed=(12 << 20) * many, transcendentals=0),
         compiler_params=pltpu.CompilerParams(vmem_limit_bytes=VMEM_LIMIT),
-    )(x, *pieces)
+        input_output_aliases={1 + len(pieces): 0} if before else {},
+    )(x, *pieces, *before)
+    return out
 
 
 def grad_kernel(*refs, chunks, received, cuts):
@@ -953,13 +960,14 @@
     middle, *normed_mid_local = out_proj(context, tokens_here, gain_mlp, out_pieces)
     normed_mid = [over_tensor(x) for x in normed_mid_local]
     d_hidden, *cot_all = d_hidden_of(me_z.reshape(1), cots, down_pieces)
-    hidden, mlp_grads, d_normed_mid, mlp_branch = [], [], [], []
+    hidden, mlp_grads, d_normed_mid, mlp_full = [], [], [], ()
     for i in range(2):
         h, g = mlp(normed_mid[i], d_hidden, i, gu_pieces)
         hidden.append(h[None])
         mlp_grads.append(g)
-        d_normed_mid.append(sum_tensor(back(g, gu_pieces)))
-        mlp_branch.append(sum_tensor(back(h[None], down_pieces)))
+        d_normed_mid.append(sum_tensor(back(g, gu_pieces, n_tensor).reshape(LEN // 2, width)))
+        mlp_full = (back(h[None], down_pieces, n_tensor, i, 2, mlp_full),)
+    mlp_branch = sum_tensor(mlp_full[0].reshape(LEN, width))
     _, cuts = scatter_segments(n_dp)
     half = [WIDTH // 2]
 
@@ -991,11 +999,15 @@
     pair = LANES // kv if kv < LANES else 1
     kv_at = [z // pair * 2 * max(kv, LANES) + z % pair * kv for z in range(n_tensor)]
     q_at = [z * q for z in range(n_tensor)]
-    packed = pack([query_parts, out_parts], [[(0, q, q_at)], [(q, q, q_at)]], n_tensor, ways, 2 * q, shard_rows)
-    packed = sum_tensor(packed).astype(f32)
-    grad_query, grad_output = packed[:, :q], packed[:, q:].T
+
+    def over_all(parts, cuts, columns):
+        packed = pack([parts], [cuts], n_tensor, ways, columns, shard_rows)
+        return sum_tensor(packed).astype(f32)
+
+    grad_output = over_all(out_parts, [(0, q, q_at)], q).T
+    grad_query = over_all(query_parts, [(0, q, q_at)], q)
     kv_cuts = [(0, kv, kv_at), (kv, kv, [x + max(kv, LANES) for x in kv_at])]
-    packed = sum_tensor(pack([kv_parts], [kv_cuts], n_tensor, ways, 2 * kv, shard_rows)).astype(f32)
+    packed = over_all(kv_parts, kv_cuts, 2 * kv)
     grad_key, grad_value = packed[:, :kv], packed[:, kv:]
 
     def sum_all(x):
@@ -1005,7 +1017,7 @@
             x = x + swap(x, DP, n_dp, b)
         return x
 
-    layer_out = (middle + jnp.concatenate(mlp_branch, axis=0).astype(f32)).astype(bf16)
+    layer_out = (middle + mlp_branch.astype(f32)).astype(bf16)
     layer_out = reorder(order, (layer_out,), True)[0]
     gain_grads = sum_all(gain_parts)
     return (

time: 874 us -> 906 us (1.037)
  waiting for transfers between devices: 398 us -> 423 us
    ppermute x102, waiting for transfers between devices: 223 us -> 261 us  [swap(): return lax.ppermute(x, axis, [(i, i ^ 1 << b) for i in range(n)])]
    reduce_scatter x7, waiting for transfers between devices: 86 us -> 73.9 us  [sum_tensor(): return lax.psum_scatter(x, TENSOR, scatter_dimension=0, tiled=True)]
  transfers between devices with their start and end apart: 119 -> 119, of which waited for: 47 -> 44; matrix products, arithmetic and copies ran while one was open for 2% -> 2% of each run, Pallas kernels for 34% -> 33%
where the time goes in v3:
time: 906 us; the launch traced here: 900 us
  waiting for transfers between devices  423 us (47%)
  Pallas kernels  343 us (38%)
  starting transfers between devices  90.5 us (10%)
  local copies, waits for them, and re-layouts  18.9 us (2%)
  between operations  15.1 us (2%)
    ppermute x102, waiting for transfers between devices, swap(): return lax.ppermute(x, axis, [(i, i ^ 1 << b) for i in range(n)])  261 us
    ppermute x3, waiting for transfers between devices, layer(): lax.ppermute(above[-1], TENSOR, [(i + 1, i) for i in range(n_tensor - r)])  88.5 us
    pallas_call x12, Pallas kernels, weight_grad(): pl.pallas_call(partial(grad_kernel, chunks=chunks, received=len(extra), c...  85.1 us
    ppermute x102, starting transfers between devices, swap(): return lax.ppermute(x, axis, [(i, i ^ 1 << b) for i in range(n)])  75 us
    reduce_scatter x7, waiting for transfers between devices, sum_tensor(): return lax.psum_scatter(x, TENSOR, scatter_dimension=0, tiled=True)  73.9 us
    pallas_call x4, Pallas kernels, back(): pl.pallas_call(partial(back_kernel, count=len(pieces)), grid=(many * per,...  46.6 us
    pallas_call x1, Pallas kernels, attn_backward(): pl.pallas_call(partial(attn_bwd_kernel, count=len(q_pieces)), grid_spec=g...  39.8 us
    pallas_call x2, Pallas kernels, mlp(): pl.pallas_call(partial(mlp_kernel, count=len(pieces)), grid=(tiles,), in_...  33.1 us
  transfers between devices with their start and end apart: 119, of which 44 were waited for; matrix products, arithmetic and copies ran while one was open for 2% of the time, Pallas kernels for 33%

profile of v3, /device:TPU:0, one launch (start us, length us, event | category | flops | bytes accessed | tf_op | source)
XLA Modules:
  0.0 899.7 jit_solution(8564979898801103378)
XLA Ops:
  24.5 25.1 %collective-permute-done.1.refs_2_ = bf16[512,256]{1,0:T(8,128)(2,1)S(1)} collective-permute-done((bf16[512,256]{1,0:T(8,128)(2,1)S(1)}, bf16[512,256]{1,0:T(8,128)(2,1)S(1)}, u32[]{:S(2)}, u32[]{:S(2)}) %collective-permute-start.1) | collective-permute-done | bytes 262176 | tf_op jit(solution)/shard_map/ppermute | solution.py:62
  85.2 5.4 pk.1
  99.6 10.1 %collective-permute-done.16.refs_2_ = bf16[128,2048]{1,0:T(8,128)(2,1)S(1)} collective-permute-done((bf16[128,2048]{1,0:T(8,128)(2,1)}, bf16[128,2048]{1,0:T(8,128)(2,1)S(1)}, u32[]{:S(2)}, u32[]{:S(2)}) %collective-permute-start.16) | collective-permute-done | bytes 524320 | tf_op jit(solution)/shard_map/ppermute | solution.py:62
  111.7 10.0 %collective-permute-done.19.refs_5_ = bf16[128,2048]{1,0:T(8,128)(2,1)S(1)} collective-permute-done((bf16[128,2048]{1,0:T(8,128)(2,1)}, bf16[128,2048]{1,0:T(8,128)(2,1)S(1)}, u32[]{:S(2)}, u32[]{:S(2)}) %collective-permute-start.19) | collective-permute-done | bytes 524320 | tf_op jit(solution)/shard_map/ppermute | solution.py:62
  123.0 9.2 %collective-permute-done.29.refs_2_.refs_16_ = bf16[128,2048]{1,0:T(8,128)(2,1)S(1)} collective-permute-done((bf16[128,2048]{1,0:T(8,128)(2,1)}, bf16[128,2048]{1,0:T(8,128)(2,1)S(1)}, u32[]{:S(2)}, u32[]{:S(2)}) %collective-permute-start.29) | collective-permute-done | bytes 524320 | tf_op jit(solution)/shard_map/ppermute | solution.py:62
  134.2 9.2 %collective-permute-done.32.refs_5_.refs_19_ = bf16[128,2048]{1,0:T(8,128)(2,1)} collective-permute-done((bf16[128,2048]{1,0:T(8,128)(2,1)}, bf16[128,2048]{1,0:T(8,128)(2,1)}, u32[]{:S(2)}, u32[]{:S(2)}) %collective-permute-start.32) | collective-permute-done | bytes 524320 | tf_op jit(solution)/shard_map/ppermute | solution.py:62
  144.5 9.7 %collective-permute-done.17.refs_3_ = bf16[128,2048]{1,0:T(8,128)(2,1)} collective-permute-done((bf16[128,2048]{1,0:T(8,128)(2,1)S(1)}, bf16[128,2048]{1,0:T(8,128)(2,1)}, u32[]{:S(2)}, u32[]{:S(2)}) %collective-permute-start.17) | collective-permute-done | bytes 524320 | tf_op jit(solution)/shard_map/ppermute | solution.py:62
  161.9 6.7 collective-permute-done.30.refs_3_.refs_17_
  176.0 15.8 %shard_map.223 = (bf16[256,2048]{1,0:T(8,128)(2,1)}, bf16[256,2048]{1,0:T(8,128)(2,1)}, f32[256,1024]{1,0:T(8,128)}) custom-call(s32[1]{0:T(128)} %bitcast.row0_ref, s32[256,1]{1,0:T(8,128)} %copy.35.seg_ref, bf16[256,2048]{1,0:T(8,128)(2,1)} %get-tuple-element.92.x_ref.refs_0_, bf16[1024,1024]{1,0:T(8,128)(2,1)} %all-gather.5.cloned.1.call-done.k_ref.v_ref, ...), custom_call_target="tpu_custom_call" | custom-call | flops 4294967296 | bytes 12582912 | tf_op jit(solution)/shard_map/pallas_call | solution.py:484
  192.7 15.8 %shard_map.224 = (bf16[256,2048]{1,0:T(8,128)(2,1)}, bf16[256,2048]{1,0:T(8,128)(2,1)}, f32[256,1024]{1,0:T(8,128)}) custom-call(s32[1]{0:T(128)} %bitcast.row0_ref, s32[256,1]{1,0:T(8,128)} %copy.35.seg_ref, bf16[256,2048]{1,0:T(8,128)(2,1)} %get-tuple-element.92.x_ref.refs_0_, ...), custom_call_target="tpu_custom_call", output_to_operand_aliasing={{0}: (21, {}), {1}: (22, {}), {2}: (23, {})} | custom-call | flops 4294967296 | bytes 12582912 | tf_op jit(solution)/shard_map/pallas_call | solution.py:484
  210.3 8.6 op.1
  221.1 7.9 collective-permute-done.52.refs_13_.refs_6_
  230.9 6.8 collective-permute-start.41
  237.6 7.8 collective-permute-done.63.refs_4_.refs_18_
  245.4 21.8 %collective-permute-done.61.refs_2_.refs_16_ = bf16[128,4096]{1,0:T(8,128)(2,1)S(1)} collective-permute-done((bf16[128,4096]{1,0:T(8,128)(2,1)}, bf16[128,4096]{1,0:T(8,128)(2,1)S(1)}, u32[]{:S(2)}, u32[]{:S(2)}) %collective-permute-start.61) | collective-permute-done | bytes 1048608 | tf_op jit(solution)/shard_map/ppermute | solution.py:62
  267.7 23.3 %collective-permute-done.44.refs_4_ = bf16[256,2048]{1,0:T(8,128)(2,1)S(1)} collective-permute-done((bf16[256,2048]{1,0:T(8,128)(2,1)}, bf16[256,2048]{1,0:T(8,128)(2,1)S(1)}, u32[]{:S(2)}, u32[]{:S(2)}) %collective-permute-start.44) | collective-permute-done | bytes 1048608 | tf_op jit(solution)/shard_map/ppermute | solution.py:947
  300.5 17.5 %collective-permute-done.45.refs_5_ = bf16[256,2048]{1,0:T(8,128)(2,1)} collective-permute-done((bf16[256,2048]{1,0:T(8,128)(2,1)S(1)}, bf16[256,2048]{1,0:T(8,128)(2,1)}, u32[]{:S(2)}, u32[]{:S(2)}) %collective-permute-start.45) | collective-permute-done | bytes 1048608 | tf_op jit(solution)/shard_map/ppermute | solution.py:947
  324.5 47.7 %collective-permute-done.46.refs_6_ = bf16[256,2048]{1,0:T(8,128)(2,1)} collective-permute-done((bf16[256,2048]{1,0:T(8,128)(2,1)}, bf16[256,2048]{1,0:T(8,128)(2,1)}, u32[]{:S(2)}, u32[]{:S(2)}) %collective-permute-start.46) | collective-permute-done | bytes 1048608 | tf_op jit(solution)/shard_map/ppermute | solution.py:947
  372.7 17.0 %dh.1 = (f32[1024,2048]{1,0:T(8,128)}, bf16[512,2048]{1,0:T(8,128)(2,1)}, bf16[512,2048]{1,0:T(8,128)(2,1)}) custom-call(s32[1]{0:T(128)} %bitcast.4.me_ref, bf16[256,2048]{1,0:T(8,128)(2,1)} %get-tuple-element.112.refs_0_.cot_ref, bf16[256,2048]{1,0:T(8,128)(2,1)} %copy-done.70, bf16[256,2048]{1,0:T(8,128)(2,1)} %collective-permute-done.42.refs_2_, ...), custom_call_target="tpu_custom_call" | custom-call | flops 8589934592 | bytes 25165824 | tf_op jit(solution)/shard_map/dh/pallas_call | solution.py:766
  391.1 16.5 %shard_map.227 = (bf16[512,2048]{1,0:T(8,128)(2,1)}, bf16[2,512,2048]{2,1,0:T(8,128)(2,1)}) custom-call(bf16[512,2048]{1,0:T(8,128)(2,1)} %all-gather.11.cloned.1.call-done.x_ref.refs_0_, f32[1024,2048]{1,0:T(8,128)} %get-tuple-element.116.dh_ref, bf16[256,4096]{1,0:T(8,128)(2,1)} %copy-done, bf16[128,4096]{1,0:T(8,128)(2,1)} %collective-permute-done.60.refs_1_.refs_15_, ...), custom_call_target="tpu_custom_call" | custom-call | flops 8589934592 | bytes 31457280 | tf_op jit(solution)/shard_map/pallas_call | solution.py:801
  407.6 14.1 %shard_map.231 = bf16[4,1,128,2048]{3,2,1,0:T(8,128)(2,1)} custom-call(bf16[2,512,2048]{2,1,0:T(8,128)(2,1)} %get-tuple-element.121.x_ref.refs_2_, bf16[256,4096]{1,0:T(8,128)(2,1)} %copy-done, bf16[128,4096]{1,0:T(8,128)(2,1)} %collective-permute-done.60.refs_1_.refs_15_, bf16[128,4096]{1,0:T(8,128)(2,1)} %copy-done.2, ...), custom_call_target="tpu_custom_call" | custom-call | flops 8589934592 | bytes 25165824 | tf_op jit(solution)/shard_map/pallas_call | solution.py:842
  421.8 16.6 %shard_map.226 = (bf16[512,2048]{1,0:T(8,128)(2,1)}, bf16[2,512,2048]{2,1,0:T(8,128)(2,1)}) custom-call(bf16[512,2048]{1,0:T(8,128)(2,1)} %all-gather.9.cloned.1.call-done.x_ref.refs_1_, f32[1024,2048]{1,0:T(8,128)} %get-tuple-element.116.dh_ref, bf16[256,4096]{1,0:T(8,128)(2,1)} %copy-done, bf16[128,4096]{1,0:T(8,128)(2,1)} %collective-permute-done.60.refs_1_.refs_15_, ...), custom_call_target="tpu_custom_call" | custom-call | flops 8589934592 | bytes 31457280 | tf_op jit(solution)/shard_map/pallas_call | solution.py:801
  438.5 14.2 %shard_map.232 = bf16[4,1,128,2048]{3,2,1,0:T(8,128)(2,1)} custom-call(bf16[2,512,2048]{2,1,0:T(8,128)(2,1)} %get-tuple-element.122.x_ref.refs_3_, bf16[256,4096]{1,0:T(8,128)(2,1)} %copy-done, bf16[128,4096]{1,0:T(8,128)(2,1)} %collective-permute-done.60.refs_1_.refs_15_, bf16[128,4096]{1,0:T(8,128)(2,1)} %copy-done.2, ...), custom_call_target="tpu_custom_call" | custom-call | flops 8589934592 | bytes 25165824 | tf_op jit(solution)/shard_map/pallas_call | solution.py:842
  453.1 18.2 %reduce-scatter.10.cloned.1.call-done.refs_0_ = bf16[128,2048]{1,0:T(8,128)(2,1)} async-done(((bf16[512,2048]{1,0:T(8,128)(2,1)}), bf16[128,2048]{1,0:T(8,128)(2,1)}) %reduce-scatter.10.cloned.1.call-update) | async-done | bytes 524304 | tf_op jit(solution)/shard_map/reduce_scatter | solution.py:907
  471.4 45.0 %reduce-scatter.12.cloned.1.call-done.refs_1_ = bf16[128,2048]{1,0:T(8,128)(2,1)} async-done(((bf16[512,2048]{1,0:T(8,128)(2,1)}), bf16[128,2048]{1,0:T(8,128)(2,1)}) %reduce-scatter.12.cloned.1.call-update) | async-done | bytes 524304 | tf_op jit(solution)/shard_map/reduce_scatter | solution.py:907
  516.4 5.6 mb.1
  521.9 39.8 %ab.1 = (bf16[256,2048]{1,0:T(8,128)(2,1)}, bf16[1024,1024]{1,0:T(8,128)(2,1)}, f32[256,2048]{1,0:T(8,128)}) custom-call(s32[1]{0:T(128)} %bitcast.row0_ref, s32[1,256]{1,0:T(1,128)} %bitcast.35, bf16[256,2048]{1,0:T(8,128)(2,1)} %get-tuple-element.120.q_ref, bf16[1024,1024]{1,0:T(8,128)(2,1)} %all-gather.5.cloned.1.call-done.k_ref.v_ref, ...), custom_call_target="tpu_custom_call" | custom-call | flops 15032385536 | bytes 29360128 | tf_op jit(solution)/shard_map/ab/pallas_call | solution.py:673
  561.8 9.1 %shard_map.228.refs_14_ = bf16[4,2,128,2048]{3,2,1,0:T(8,128)(2,1)} custom-call(bf16[1,512,2048]{2,1,0:T(8,128)(2,1)} %bitcast.36, bf16[256,2048]{1,0:T(8,128)(2,1)} %get-tuple-element.113.refs_7_.refs_0_, bf16[128,2048]{1,0:T(8,128)(2,1)} %copy-done.33, bf16[128,2048]{1,0:T(8,128)(2,1)} %collective-permute-done.48.refs_9_.refs_2_, ...), custom_call_target="tpu_custom_call" | custom-call | flops 4294967296 | bytes 12582912 | tf_op jit(solution)/shard_map/pallas_call | solution.py:842
  570.9 9.1 %shard_map.229 = bf16[4,2,128,2048]{3,2,1,0:T(8,128)(2,1)} custom-call(bf16[1,512,2048]{2,1,0:T(8,128)(2,1)} %bitcast.25, bf16[256,2048]{1,0:T(8,128)(2,1)} %get-tuple-element.113.refs_7_.refs_0_, bf16[128,2048]{1,0:T(8,128)(2,1)} %copy-done.33, bf16[128,2048]{1,0:T(8,128)(2,1)} %collective-permute-done.48.refs_9_.refs_2_, ...), custom_call_target="tpu_custom_call", output_to_operand_aliasing={{}: (15, {})} | custom-call | flops 4294967296 | bytes 12582912 | tf_op jit(solution)/shard_map/pallas_call | solution.py:842
  580.3 5.3 shard_map.241
  591.3 9.0 shard_map.245
  600.3 9.0 %shard_map.249 = bf16[1024,2048]{1,0:T(8,128)(2,1)} custom-call(bf16[512,2048]{1,0:T(8,128)(2,1)} %all-gather.11.cloned.1.call-done.x_ref.refs_0_, bf16[512,2048]{1,0:T(8,128)(2,1)} %all-gather.9.cloned.1.call-done.x_ref.refs_1_, bf16[2,512,2048]{2,1,0:T(8,128)(2,1)} %get-tuple-element.121.x_ref.refs_2_, bf16[2,512,2048]{2,1,0:T(8,128)(2,1)} %get-tuple-element.122.x_ref.refs_3_), custom_call_target="tpu_custom_call" | custom-call | flops 4294967296 | bytes 16777216 | tf_op jit(solution)/shard_map/pallas_call | solution.py:888
  609.8 6.0 shard_map.242
  617.4 9.1 %shard_map.253 = bf16[1024,2048]{1,0:T(8,128)(2,1)} custom-call(bf16[512,2048]{1,0:T(8,128)(2,1)} %get-tuple-element.165.refs_0_, bf16[512,2048]{1,0:T(8,128)(2,1)} %get-tuple-element.166.refs_1_, bf16[1,512,2048]{2,1,0:T(8,128)(2,1)} %bitcast.37, bf16[1,512,2048]{2,1,0:T(8,128)(2,1)} %bitcast.26), custom_call_target="tpu_custom_call" | custom-call | flops 4294967296 | bytes 16777216 | tf_op jit(solution)/shard_map/pallas_call | solution.py:888
  626.5 14.7 %collective-permute-done.89.refs_1_ = bf16[256,2048]{1,0:T(8,128)(2,1)S(1)} collective-permute-done((bf16[256,2048]{1,0:T(8,128)(2,1)}, bf16[256,2048]{1,0:T(8,128)(2,1)S(1)}, u32[]{:S(2)}, u32[]{:S(2)}) %collective-permute-start.89) | collective-permute-done | bytes 1048608 | tf_op jit(solution)/shard_map/ppermute | solution.py:62
  642.7 23.1 %collective-permute-done.90.refs_3_ = bf16[256,2048]{1,0:T(8,128)(2,1)} collective-permute-done((bf16[256,2048]{1,0:T(8,128)(2,1)}, bf16[256,2048]{1,0:T(8,128)(2,1)}, u32[]{:S(2)}, u32[]{:S(2)}) %collective-permute-start.90) | collective-permute-done | bytes 1048608 | tf_op jit(solution)/shard_map/ppermute | solution.py:62
  672.5 5.9 shard_map.234
  688.3 16.9 %collective-permute-done.79.refs_1_ = bf16[256,2048]{1,0:T(8,128)(2,1)S(1)} collective-permute-done((bf16[256,2048]{1,0:T(8,128)(2,1)}, bf16[256,2048]{1,0:T(8,128)(2,1)S(1)}, u32[]{:S(2)}, u32[]{:S(2)}) %collective-permute-start.79) | collective-permute-done | bytes 1048608 | tf_op jit(solution)/shard_map/ppermute | solution.py:62
  714.6 9.8 %shard_map.246 = (bf16[384,2048]{1,0:T(8,128)(2,1)}, bf16[256,2048]{1,0:T(8,128)(2,1)}, bf16[128,2048]{1,0:T(8,128)(2,1)}, bf16[256,2048]{1,0:T(8,128)(2,1)}) custom-call(bf16[512,2048]{1,0:T(8,128)(2,1)} %all-gather.11.cloned.1.call-done.x_ref.refs_0_, bf16[512,2048]{1,0:T(8,128)(2,1)} %all-gather.9.cloned.1.call-done.x_ref.refs_1_, ...), custom_call_target="tpu_custom_call" | custom-call | flops 4294967296 | bytes 16777216 | tf_op jit(solution)/shard_map/pallas_call | solution.py:888
  727.0 9.6 %shard_map.250 = (bf16[384,2048]{1,0:T(8,128)(2,1)}, bf16[256,2048]{1,0:T(8,128)(2,1)}, bf16[128,2048]{1,0:T(8,128)(2,1)}, bf16[256,2048]{1,0:T(8,128)(2,1)}) custom-call(bf16[512,2048]{1,0:T(8,128)(2,1)} %all-gather.11.cloned.1.call-done.x_ref.refs_0_, bf16[512,2048]{1,0:T(8,128)(2,1)} %all-gather.9.cloned.1.call-done.x_ref.refs_1_, ...), custom_call_target="tpu_custom_call" | custom-call | flops 4294967296 | bytes 16777216 | tf_op jit(solution)/shard_map/pallas_call | solution.py:888
  736.5 24.8 %collective-permute-done.82.refs_4_ = bf16[128,2048]{1,0:T(8,128)(2,1)S(1)} collective-permute-done((bf16[128,2048]{1,0:T(8,128)(2,1)S(1)}, bf16[128,2048]{1,0:T(8,128)(2,1)S(1)}, u32[]{:S(2)}, u32[]{:S(2)}) %collective-permute-start.82) | collective-permute-done | bytes 524320 | tf_op jit(solution)/shard_map/ppermute | solution.py:62
  767.1 9.7 %shard_map.254 = (bf16[384,2048]{1,0:T(8,128)(2,1)}, bf16[256,2048]{1,0:T(8,128)(2,1)}, bf16[128,2048]{1,0:T(8,128)(2,1)}, bf16[256,2048]{1,0:T(8,128)(2,1)}) custom-call(bf16[512,2048]{1,0:T(8,128)(2,1)} %get-tuple-element.165.refs_0_, bf16[512,2048]{1,0:T(8,128)(2,1)} %get-tuple-element.166.refs_1_, bf16[1,512,2048]{2,1,0:T(8,128)(2,1)} %bitcast.38, ...), custom_call_target="tpu_custom_call" | custom-call | flops 4294967296 | bytes 16777216 | tf_op jit(solution)/shard_map/pallas_call | solution.py:888
  782.3 5.2 collective-permute-done.99.refs_1_
  793.6 9.2 %ib.1 = (f32[256,2048]{1,0:T(8,128)}, f32[8,2048]{1,0:T(8,128)}) custom-call(s32[16]{0:T(128)} %broadcast_xor_fusion.order_ref, bf16[256,1024]{1,0:T(8,128)(2,1)} %reduce-scatter.14.cloned.1.call-done.dkv_ref, f32[256,2048]{1,0:T(8,128)} %get-tuple-element.128.part_ref, bf16[256,2048]{1,0:T(8,128)(2,1)} %get-tuple-element.105.tok_ref, ...), custom_call_target="tpu_custom_call" | custom-call | flops 1073741824 | bytes 16777216 | tf_op jit(solution)/shard_map/ib/pallas_call | solution.py:724
  802.9 7.2 collective-permute-done.104.refs_1_
  820.1 6.0 collective-permute-done.96.refs_2_
  840.5 8.1 collective-permute-done.101.refs_2_
  880.7 10.6 %reduce-scatter.18.cloned.1.call-done = bf16[256,256]{1,0:T(8,128)(2,1)} async-done(((bf16[1024,256]{1,0:T(8,128)(2,1)}), bf16[256,256]{1,0:T(8,128)(2,1)}) %reduce-scatter.18.cloned.1.call-update) | async-done | bytes 131088 | tf_op jit(solution)/shard_map/reduce_scatter | solution.py:907
  (415 shorter events, 221.8 us)
Async XLA Ops:
  7.2 83.7 %all-gather.7.cloned.1.call-start = ((), (), s32[]{:S(2)}) async-start(), calls=%async_computation.8 | async-start | bytes 2621440 | tf_op jit(solution)/shard_map/all_gather | solution.py:903
  9.2 166.7 %all-gather.5.cloned.1.call-start = ((), (), s32[]{:S(2)}) async-start(), calls=%async_computation.7 | async-start | bytes 2621440 | tf_op jit(solution)/shard_map/all_gather | solution.py:903
  12.2 42.9 %collective-permute-start.48 = (bf16[128,2048]{1,0:T(8,128)(2,1)}, bf16[128,2048]{1,0:T(8,128)(2,1)}, u32[]{:S(2)}, u32[]{:S(2)}) collective-permute-start(bf16[128,2048]{1,0:T(8,128)(2,1)} %get-tuple-element.114), channel_id=1, source_target_pairs={{0,16},{4,20},{8,24},{12,28},{16,0},{20,4},{24,8},{28,12},{1,17},{... | collective-permute-start | bytes 1572872 | tf_op jit(solution)/shard_map/ppermute | solution.py:62
  20.4 29.3 %collective-permute-start.1 = (bf16[512,256]{1,0:T(8,128)(2,1)S(1)}, bf16[512,256]{1,0:T(8,128)(2,1)S(1)}, u32[]{:S(2)}, u32[]{:S(2)}) collective-permute-start(bf16[512,256]{1,0:T(8,128)(2,1)S(1)} %pad_maximum_fusion), channel_id=1, source_target_pairs={{0,2},{1,3},{2,0},{3,1},{4,6},{5,7},{6,4},{7,5},{8,10},{9,11},{10,... | collective-permute-start | bytes 786440 | tf_op jit(solution)/shard_map/ppermute | solution.py:62
  23.0 36.7 %collective-permute-start.47 = (bf16[128,2048]{1,0:T(8,128)(2,1)}, bf16[128,2048]{1,0:T(8,128)(2,1)S(1)}, u32[]{:S(2)}, u32[]{:S(2)}) collective-permute-start(bf16[128,2048]{1,0:T(8,128)(2,1)} %get-tuple-element.114), channel_id=1, source_target_pairs={{0,8},{4,12},{8,0},{12,4},{16,24},{20,28},{24,16},{28,20},{1,9},{5... | collective-permute-start | bytes 1572872 | tf_op jit(solution)/shard_map/ppermute | solution.py:62
  90.6 300.5 %all-gather.11.cloned.1.call-start = ((), (), s32[]{:S(2)}) async-start(), calls=%async_computation.10 | async-start | bytes 2621440 | tf_op jit(solution)/shard_map/all_gather | solution.py:903
  98.8 33.4 %collective-permute-start.29 = (bf16[128,2048]{1,0:T(8,128)(2,1)}, bf16[128,2048]{1,0:T(8,128)(2,1)S(1)}, u32[]{:S(2)}, u32[]{:S(2)}) collective-permute-start(bf16[128,2048]{1,0:T(8,128)(2,1)} %get-tuple-element.108), channel_id=1, source_target_pairs={{0,16},{4,20},{8,24},{12,28},{16,0},{20,4},{24,8},{28,12},{1,17},{... | collective-permute-start | bytes 1572872 | tf_op jit(solution)/shard_map/ppermute | solution.py:62
  110.5 32.9 %collective-permute-start.32 = (bf16[128,2048]{1,0:T(8,128)(2,1)}, bf16[128,2048]{1,0:T(8,128)(2,1)}, u32[]{:S(2)}, u32[]{:S(2)}) collective-permute-start(bf16[128,2048]{1,0:T(8,128)(2,1)} %get-tuple-element.109), channel_id=1, source_target_pairs={{0,8},{4,12},{8,0},{12,4},{16,24},{20,28},{24,16},{28,20},{1,9},{5... | collective-permute-start | bytes 1572872 | tf_op jit(solution)/shard_map/ppermute | solution.py:62
  161.3 47.2 %collective-permute-start.34 = (bf16[256,2048]{1,0:T(8,128)(2,1)}, bf16[256,2048]{1,0:T(8,128)(2,1)}, u32[]{:S(2)}, u32[]{:S(2)}) collective-permute-start(bf16[256,2048]{1,0:T(8,128)(2,1)} %get-tuple-element.107.refs_0_.refs_14_), channel_id=1, source_target_pairs={{0,4},{4,0},{8,12},{12,8},{16,20},{20,16},{24,28},{28,24},{1,5},{5... | collective-permute-start | bytes 3145736 | tf_op jit(solution)/shard_map/ppermute | solution.py:62
  161.4 30.8 %collective-permute-start.38 = (bf16[128,2048]{1,0:T(8,128)(2,1)}, bf16[128,2048]{1,0:T(8,128)(2,1)}, u32[]{:S(2)}, u32[]{:S(2)}) collective-permute-start(bf16[128,2048]{1,0:T(8,128)(2,1)} %collective-permute-done.31.refs_4_.refs_18_), channel_id=1, source_target_pairs={{0,4},{4,0},{8,12},{12,8},{16,20},{20,16},{24,28},{28,24},{1,5},{5... | collective-permute-start | bytes 1572872 | tf_op jit(solution)/shard_map/ppermute | solution.py:62
  175.4 33.1 %collective-permute-start.37 = (bf16[128,2048]{1,0:T(8,128)(2,1)}, bf16[128,2048]{1,0:T(8,128)(2,1)}, u32[]{:S(2)}, u32[]{:S(2)}) collective-permute-start(bf16[128,2048]{1,0:T(8,128)(2,1)} %copy-done.46), channel_id=1, source_target_pairs={{0,4},{4,0},{8,12},{12,8},{16,20},{20,16},{24,28},{28,24},{1,5},{5... | collective-permute-start | bytes 1572872 | tf_op jit(solution)/shard_map/ppermute | solution.py:62
  175.7 34.4 %collective-permute-start.40 = (bf16[128,2048]{1,0:T(8,128)(2,1)}, bf16[128,2048]{1,0:T(8,128)(2,1)}, u32[]{:S(2)}, u32[]{:S(2)}) collective-permute-start(bf16[128,2048]{1,0:T(8,128)(2,1)} %copy-done.47), channel_id=1, source_target_pairs={{0,4},{4,0},{8,12},{12,8},{16,20},{20,16},{24,28},{28,24},{1,5},{5... | collective-permute-start | bytes 1572872 | tf_op jit(solution)/shard_map/ppermute | solution.py:62
  191.8 37.8 %collective-permute-start.53 = (bf16[256,2048]{1,0:T(8,128)(2,1)}, bf16[256,2048]{1,0:T(8,128)(2,1)}, u32[]{:S(2)}, u32[]{:S(2)}) collective-permute-start(bf16[256,2048]{1,0:T(8,128)(2,1)} %get-tuple-element.113.refs_7_.refs_0_), channel_id=1, source_target_pairs={{0,4},{4,0},{8,12},{12,8},{16,20},{20,16},{24,28},{28,24},{1,5},{5... | collective-permute-start | bytes 3145736 | tf_op jit(solution)/shard_map/ppermute | solution.py:62
  192.1 38.7 %collective-permute-start.64 = (bf16[128,4096]{1,0:T(8,128)(2,1)}, bf16[128,4096]{1,0:T(8,128)(2,1)S(1)}, u32[]{:S(2)}, u32[]{:S(2)}) collective-permute-start(bf16[128,4096]{1,0:T(8,128)(2,1)} %get-tuple-element.206), channel_id=1, source_target_pairs={{0,8},{4,12},{8,0},{12,4},{16,24},{20,28},{24,16},{28,20},{1,9},{5... | collective-permute-start | bytes 3145736 | tf_op jit(solution)/shard_map/ppermute | solution.py:62
  218.9 202.9 %all-gather.9.cloned.1.call-start = ((), (), s32[]{:S(2)}) async-start(), calls=%async_computation.9 | async-start | bytes 2621440 | tf_op jit(solution)/shard_map/all_gather | solution.py:903
  220.3 46.9 %collective-permute-start.61 = (bf16[128,4096]{1,0:T(8,128)(2,1)}, bf16[128,4096]{1,0:T(8,128)(2,1)S(1)}, u32[]{:S(2)}, u32[]{:S(2)}) collective-permute-start(bf16[128,4096]{1,0:T(8,128)(2,1)} %get-tuple-element.207), channel_id=1, source_target_pairs={{0,16},{4,20},{8,24},{12,28},{16,0},{20,4},{24,8},{28,12},{1,17},{... | collective-permute-start | bytes 3145736 | tf_op jit(solution)/shard_map/ppermute | solution.py:62
  229.0 38.2 %collective-permute-start.60 = (bf16[128,4096]{1,0:T(8,128)(2,1)}, bf16[128,4096]{1,0:T(8,128)(2,1)}, u32[]{:S(2)}, u32[]{:S(2)}) collective-permute-start(bf16[128,4096]{1,0:T(8,128)(2,1)} %get-tuple-element.207), channel_id=1, source_target_pairs={{0,8},{4,12},{8,0},{12,4},{16,24},{20,28},{24,16},{28,20},{1,9},{5... | collective-permute-start | bytes 3145736 | tf_op jit(solution)/shard_map/ppermute | solution.py:62
  229.5 61.4 %collective-permute-start.44 = (bf16[256,2048]{1,0:T(8,128)(2,1)}, bf16[256,2048]{1,0:T(8,128)(2,1)S(1)}, u32[]{:S(2)}, u32[]{:S(2)}) collective-permute-start(bf16[256,2048]{1,0:T(8,128)(2,1)} %get-tuple-element.112.refs_0_.cot_ref), channel_id=1, source_target_pairs={{1,0},{2,1},{3,2},{5,4},{6,5},{7,6},{9,8},{10,9},{11,10},{13,12},{... | collective-permute-start | bytes 3145736 | tf_op jit(solution)/shard_map/ppermute | solution.py:947
  230.9 61.4 %collective-permute-start.41 = (bf16[256,2048]{1,0:T(8,128)(2,1)}, bf16[256,2048]{1,0:T(8,128)(2,1)S(1)}, u32[]{:S(2)}, u32[]{:S(2)}) collective-permute-start(bf16[256,2048]{1,0:T(8,128)(2,1)} %get-tuple-element.112.refs_0_.cot_ref), channel_id=1, source_target_pairs={{0,1},{1,2},{2,3},{4,5},{5,6},{6,7},{8,9},{9,10},{10,11},{12,13},{... | collective-permute-start | bytes 3145736 | tf_op jit(solution)/shard_map/ppermute | solution.py:946
  245.4 48.8 %collective-permute-start.56 = (bf16[128,2048]{1,0:T(8,128)(2,1)}, bf16[128,2048]{1,0:T(8,128)(2,1)S(1)}, u32[]{:S(2)}, u32[]{:S(2)}) collective-permute-start(bf16[128,2048]{1,0:T(8,128)(2,1)} %collective-permute-done.49.refs_10_.refs_3_), channel_id=1, source_target_pairs={{0,4},{4,0},{8,12},{12,8},{16,20},{20,16},{24,28},{28,24},{1,5},{5... | collective-permute-start | bytes 1572872 | tf_op jit(solution)/shard_map/ppermute | solution.py:62
  267.2 29.4 %collective-permute-start.71 = (bf16[128,4096]{1,0:T(8,128)(2,1)S(1)}, bf16[128,4096]{1,0:T(8,128)(2,1)S(1)}, u32[]{:S(2)}, u32[]{:S(2)}) collective-permute-start(bf16[128,4096]{1,0:T(8,128)(2,1)S(1)} %collective-permute-done.64.refs_5_.refs_19_), channel_id=1, source_target_pairs={{0,4},{4,0},{8,12},{12,8},{16,20},{20,16},{24,28},{28,24},{1,5},{5... | collective-permute-start | bytes 3145736 | tf_op jit(solution)/shard_map/ppermute | solution.py:62
  267.2 30.9 %collective-permute-start.70 = (bf16[128,4096]{1,0:T(8,128)(2,1)}, bf16[128,4096]{1,0:T(8,128)(2,1)S(1)}, u32[]{:S(2)}, u32[]{:S(2)}) collective-permute-start(bf16[128,4096]{1,0:T(8,128)(2,1)} %collective-permute-done.63.refs_4_.refs_18_), channel_id=1, source_target_pairs={{0,4},{4,0},{8,12},{12,8},{16,20},{20,16},{24,28},{28,24},{1,5},{5... | collective-permute-start | bytes 3145736 | tf_op jit(solution)/shard_map/ppermute | solution.py:62
  296.4 93.4 %collective-permute-start.66 = (bf16[256,4096]{1,0:T(8,128)(2,1)S(1)}, bf16[256,4096]{1,0:T(8,128)(2,1)}, u32[]{:S(2)}, u32[]{:S(2)}) collective-permute-start(bf16[256,4096]{1,0:T(8,128)(2,1)S(1)} %constant_dynamic-update-slice_fusion.2.refs_0_.refs_14_), channel_id=1, source_target_pairs={{0,4},{4,0},{8,12},{12,8},{16,20},{20,16},{24,28},{28,24},{1,5},{5... | collective-permute-start | bytes 6291464 | tf_op jit(solution)/shard_map/ppermute | solution.py:62
  318.0 54.2 %collective-permute-start.46 = (bf16[256,2048]{1,0:T(8,128)(2,1)}, bf16[256,2048]{1,0:T(8,128)(2,1)}, u32[]{:S(2)}, u32[]{:S(2)}) collective-permute-start(bf16[256,2048]{1,0:T(8,128)(2,1)} %collective-permute-done.45.refs_5_), channel_id=1, source_target_pairs={{1,0},{5,4},{9,8},{13,12},{17,16},{21,20},{25,24},{29,28}} | collective-permute-start | bytes 3145736 | tf_op jit(solution)/shard_map/ppermute | solution.py:947
  319.3 52.9 %collective-permute-start.43 = (bf16[256,2048]{1,0:T(8,128)(2,1)}, bf16[256,2048]{1,0:T(8,128)(2,1)}, u32[]{:S(2)}, u32[]{:S(2)}) collective-permute-start(bf16[256,2048]{1,0:T(8,128)(2,1)} %collective-permute-done.42.refs_2_), channel_id=1, source_target_pairs={{2,3},{6,7},{10,11},{14,15},{18,19},{22,23},{26,27},{30,31}} | collective-permute-start | bytes 3145736 | tf_op jit(solution)/shard_map/ppermute | solution.py:946
  321.0 150.3 %reduce-scatter.10.cloned.1.call-start = ((), (), s32[]{:S(2)}) async-start(), calls=%async_computation.12 | async-start | bytes 2621440 | tf_op jit(solution)/shard_map/reduce_scatter | solution.py:907
  322.3 67.4 %collective-permute-start.67 = (bf16[128,4096]{1,0:T(8,128)(2,1)}, bf16[128,4096]{1,0:T(8,128)(2,1)S(1)}, u32[]{:S(2)}, u32[]{:S(2)}) collective-permute-start(bf16[128,4096]{1,0:T(8,128)(2,1)} %collective-permute-done.60.refs_1_.refs_15_), channel_id=1, source_target_pairs={{0,4},{4,0},{8,12},{12,8},{16,20},{20,16},{24,28},{28,24},{1,5},{5... | collective-permute-start | bytes 3145736 | tf_op jit(solution)/shard_map/ppermute | solution.py:62
  324.5 65.2 %collective-permute-start.68 = (bf16[128,4096]{1,0:T(8,128)(2,1)}, bf16[128,4096]{1,0:T(8,128)(2,1)S(1)}, u32[]{:S(2)}, u32[]{:S(2)}) collective-permute-start(bf16[128,4096]{1,0:T(8,128)(2,1)} %copy-done.2), channel_id=1, source_target_pairs={{0,4},{4,0},{8,12},{12,8},{16,20},{20,16},{24,28},{28,24},{1,5},{5... | collective-permute-start | bytes 3145736 | tf_op jit(solution)/shard_map/ppermute | solution.py:62
  421.8 94.6 %reduce-scatter.12.cloned.1.call-start = ((), (), s32[]{:S(2)}) async-start(), calls=%async_computation.13 | async-start | bytes 2621440 | tf_op jit(solution)/shard_map/reduce_scatter | solution.py:907
  452.7 258.7 %reduce-scatter.14.cloned.1.call-start = ((), (), s32[]{:S(2)}) async-start(), calls=%async_computation.14 | async-start | bytes 2621440 | tf_op jit(solution)/shard_map/reduce_scatter | solution.py:907
  561.7 309.5 %reduce-scatter.8.cloned.1.call-start = ((), (), s32[]{:S(2)}) async-start(), calls=%async_computation.11 | async-start | bytes 5242880 | tf_op jit(solution)/shard_map/reduce_scatter | solution.py:907
  580.1 296.8 %reduce-scatter.20.cloned.1.call-start = ((), (), s32[]{:S(2)}) async-start(), calls=%async_computation.17 | async-start | bytes 1310720 | tf_op jit(solution)/shard_map/reduce_scatter | solution.py:907
  590.8 79.7 %collective-permute-start.78 = (bf16[1024,2048]{1,0:T(8,128)(2,1)}, bf16[1024,2048]{1,0:T(8,128)(2,1)S(1)}, u32[]{:S(2)}, u32[]{:S(2)}) collective-permute-start(bf16[1024,2048]{1,0:T(8,128)(2,1)} %shard_map.233), channel_id=1, source_target_pairs={{0,4},{4,0},{8,12},{12,8},{16,20},{20,16},{24,28},{28,24},{1,5},{5... | collective-permute-start | bytes 12582920 | tf_op jit(solution)/shard_map/ppermute | solution.py:62
  600.3 114.3 %collective-permute-start.93 = (bf16[1024,2048]{1,0:T(8,128)(2,1)}, bf16[1024,2048]{1,0:T(8,128)(2,1)}, u32[]{:S(2)}, u32[]{:S(2)}) collective-permute-start(bf16[1024,2048]{1,0:T(8,128)(2,1)} %shard_map.245), channel_id=1, source_target_pairs={{0,4},{4,0},{8,12},{12,8},{16,20},{20,16},{24,28},{28,24},{1,5},{5... | collective-permute-start | bytes 12582920 | tf_op jit(solution)/shard_map/ppermute | solution.py:62
  609.3 115.6 %collective-permute-start.98 = (bf16[1024,2048]{1,0:T(8,128)(2,1)}, bf16[1024,2048]{1,0:T(8,128)(2,1)}, u32[]{:S(2)}, u32[]{:S(2)}) collective-permute-start(bf16[1024,2048]{1,0:T(8,128)(2,1)} %shard_map.249), channel_id=1, source_target_pairs={{0,4},{4,0},{8,12},{12,8},{16,20},{20,16},{24,28},{28,24},{1,5},{5... | collective-permute-start | bytes 12582920 | tf_op jit(solution)/shard_map/ppermute | solution.py:62
  626.5 139.6 %collective-permute-start.103 = (bf16[1024,2048]{1,0:T(8,128)(2,1)}, bf16[1024,2048]{1,0:T(8,128)(2,1)}, u32[]{:S(2)}, u32[]{:S(2)}) collective-permute-start(bf16[1024,2048]{1,0:T(8,128)(2,1)} %shard_map.253), channel_id=1, source_target_pairs={{0,4},{4,0},{8,12},{12,8},{16,20},{20,16},{24,28},{28,24},{1,5},{5... | collective-permute-start | bytes 12582920 | tf_op jit(solution)/shard_map/ppermute | solution.py:62
  688.2 190.6 %reduce-scatter.16.cloned.1.call-start = ((), (), s32[]{:S(2)}) async-start(), calls=%async_computation.15 | async-start | bytes 1310720 | tf_op jit(solution)/shard_map/reduce_scatter | solution.py:907
  714.6 73.5 %collective-permute-start.83 = (bf16[1024,1024]{1,0:T(8,128)(2,1)}, bf16[1024,1024]{1,0:T(8,128)(2,1)}, u32[]{:S(2)}, u32[]{:S(2)}) collective-permute-start(bf16[1024,1024]{1,0:T(8,128)(2,1)} %shard_map.237), channel_id=1, source_target_pairs={{0,4},{4,0},{8,12},{12,8},{16,20},{20,16},{24,28},{28,24},{1,5},{5... | collective-permute-start | bytes 6291464 | tf_op jit(solution)/shard_map/ppermute | solution.py:62
  724.3 52.5 %collective-permute-start.94 = (bf16[256,2048]{1,0:T(8,128)(2,1)}, bf16[256,2048]{1,0:T(8,128)(2,1)S(1)}, u32[]{:S(2)}, u32[]{:S(2)}) collective-permute-start(bf16[256,2048]{1,0:T(8,128)(2,1)} %get-tuple-element.154), channel_id=1, source_target_pairs={{0,16},{4,20},{8,24},{12,28},{16,0},{20,4},{24,8},{28,12},{1,17},{... | collective-permute-start | bytes 3145736 | tf_op jit(solution)/shard_map/ppermute | solution.py:62
  725.0 52.8 %collective-permute-start.95 = (bf16[256,2048]{1,0:T(8,128)(2,1)}, bf16[256,2048]{1,0:T(8,128)(2,1)S(1)}, u32[]{:S(2)}, u32[]{:S(2)}) collective-permute-start(bf16[256,2048]{1,0:T(8,128)(2,1)} %get-tuple-element.156), channel_id=1, source_target_pairs={{0,8},{4,12},{8,0},{12,4},{16,24},{20,28},{24,16},{28,20},{1,9},{5... | collective-permute-start | bytes 3145736 | tf_op jit(solution)/shard_map/ppermute | solution.py:62
  726.2 35.1 %collective-permute-start.82 = (bf16[128,2048]{1,0:T(8,128)(2,1)S(1)}, bf16[128,2048]{1,0:T(8,128)(2,1)S(1)}, u32[]{:S(2)}, u32[]{:S(2)}) collective-permute-start(bf16[128,2048]{1,0:T(8,128)(2,1)S(1)} %copy-done.71), channel_id=1, source_target_pairs={{0,16},{4,20},{8,24},{12,28},{16,0},{20,4},{24,8},{28,12},{1,17},{... | collective-permute-start | bytes 1572872 | tf_op jit(solution)/shard_map/ppermute | solution.py:62
  765.8 125.5 %reduce-scatter.18.cloned.1.call-start = ((), (), s32[]{:S(2)}) async-start(), calls=%async_computation.16 | async-start | bytes 655360 | tf_op jit(solution)/shard_map/reduce_scatter | solution.py:907
  776.9 33.1 %collective-permute-start.104 = (bf16[256,2048]{1,0:T(8,128)(2,1)}, bf16[256,2048]{1,0:T(8,128)(2,1)S(1)}, u32[]{:S(2)}, u32[]{:S(2)}) collective-permute-start(bf16[256,2048]{1,0:T(8,128)(2,1)} %get-tuple-element.168), channel_id=1, source_target_pairs={{0,16},{4,20},{8,24},{12,28},{16,0},{20,4},{24,8},{28,12},{1,17},{... | collective-permute-start | bytes 3145736 | tf_op jit(solution)/shard_map/ppermute | solution.py:62
  777.8 37.2 %collective-permute-start.105 = (bf16[256,2048]{1,0:T(8,128)(2,1)}, bf16[256,2048]{1,0:T(8,128)(2,1)}, u32[]{:S(2)}, u32[]{:S(2)}) collective-permute-start(bf16[256,2048]{1,0:T(8,128)(2,1)} %get-tuple-element.170), channel_id=1, source_target_pairs={{0,8},{4,12},{8,0},{12,4},{16,24},{20,28},{24,16},{28,20},{1,9},{5... | collective-permute-start | bytes 3145736 | tf_op jit(solution)/shard_map/ppermute | solution.py:62
  787.6 38.5 %collective-permute-start.96 = (bf16[128,2048]{1,0:T(8,128)(2,1)}, bf16[128,2048]{1,0:T(8,128)(2,1)S(1)}, u32[]{:S(2)}, u32[]{:S(2)}) collective-permute-start(bf16[128,2048]{1,0:T(8,128)(2,1)} %get-tuple-element.157), channel_id=1, source_target_pairs={{0,8},{4,12},{8,0},{12,4},{16,24},{20,28},{24,16},{28,20},{1,9},{5... | collective-permute-start | bytes 1572872 | tf_op jit(solution)/shard_map/ppermute | solution.py:62
  788.0 39.5 %collective-permute-start.97 = (bf16[128,2048]{1,0:T(8,128)(2,1)}, bf16[128,2048]{1,0:T(8,128)(2,1)S(1)}, u32[]{:S(2)}, u32[]{:S(2)}) collective-permute-start(bf16[128,2048]{1,0:T(8,128)(2,1)} %get-tuple-element.158), channel_id=1, source_target_pairs={{0,16},{4,20},{8,24},{12,28},{16,0},{20,4},{24,8},{28,12},{1,17},{... | collective-permute-start | bytes 1572872 | tf_op jit(solution)/shard_map/ppermute | solution.py:62
  792.8 40.2 %collective-permute-start.84 = (bf16[256,1024]{1,0:T(8,128)(2,1)}, bf16[256,1024]{1,0:T(8,128)(2,1)S(1)}, u32[]{:S(2)}, u32[]{:S(2)}) collective-permute-start(bf16[256,1024]{1,0:T(8,128)(2,1)} %get-tuple-element.142), channel_id=1, source_target_pairs={{0,16},{4,20},{8,24},{12,28},{16,0},{20,4},{24,8},{28,12},{1,17},{... | collective-permute-start | bytes 1572872 | tf_op jit(solution)/shard_map/ppermute | solution.py:62
  819.0 29.5 %collective-permute-start.101 = (bf16[128,2048]{1,0:T(8,128)(2,1)}, bf16[128,2048]{1,0:T(8,128)(2,1)S(1)}, u32[]{:S(2)}, u32[]{:S(2)}) collective-permute-start(bf16[128,2048]{1,0:T(8,128)(2,1)} %get-tuple-element.163), channel_id=1, source_target_pairs={{0,8},{4,12},{8,0},{12,4},{16,24},{20,28},{24,16},{28,20},{1,9},{5... | collective-permute-start | bytes 1572872 | tf_op jit(solution)/shard_map/ppermute | solution.py:62
  (144 other events, 2426.7 us)
Sparse Core Ops, SparseCore 0:
  10.2 58.0 all-gather.6
  90.7 50.9 all-gather.4
  219.0 70.0 all-gather.10
  321.1 57.1 all-gather.8
  421.9 49.4 reduce-scatter.9
  473.5 42.8 reduce-scatter.11
  561.9 42.8 reduce-scatter.13
  607.0 76.0 reduce-scatter.7
  688.4 26.2 reduce-scatter.19
  765.9 25.3 reduce-scatter.15
  871.3 19.9 reduce-scatter.17
